TPU v7x, 32 devices: a whole 2x2x4 slice. The times are simulated.
32 devices in a mesh: lev: 4 (over x, core), sp: 8 (over z, y).
Axes of the slice: x: 2, y: 2, z: 4, core: 2. Of those that a mesh axis runs over, the one named last changes fastest.
Arguments:
- ocean_state: bfloat16 [32, 8, 128, 200], P(None, None, 'sp', 'lev'), may hold values from -18 to 18
- slot_level: int32 [20], replicated, may hold values from 0 to 19, each once
- wet_mask: int32 [32, 128], P('lev', 'sp'), may hold values 0 or 1
- w_in: bfloat16 [190, 800], replicated, may hold values from -0.4375 to 0.4375
- b_in: float32 [800], replicated, may hold values from -3 to 3
- w_depth: bfloat16 [7, 7, 800], replicated, may hold values from -0.875 to 0.875
- norm_gain: float32 [800], replicated, may hold values from 0.1 to 1.9
- norm_bias: float32 [800], replicated, may hold values from -3 to 3
- w_one: bfloat16 [800, 3200], replicated, may hold values from -0.21875 to 0.21875
- b_one: float32 [3200], replicated, may hold values from -3 to 3
- w_two: bfloat16 [3200, 800], replicated, may hold values from -0.109375 to 0.109375
- b_two: float32 [800], replicated, may hold values from -3 to 3
- w_out: bfloat16 [800, 190], replicated, may hold values from -0.21875 to 0.21875
- b_out: float32 [190], replicated, may hold values from -3 to 3
- cotangent: bfloat16 [32, 8, 128, 200], P(None, None, 'sp', 'lev'), may hold values from -6 to 6
Outputs:
- next_state: bfloat16 [32, 8, 128, 200], P(None, None, 'sp', 'lev')
- grad_ocean_state: bfloat16 [32, 8, 128, 200], P(None, None, 'sp', 'lev')
- grad_w_in: float32 [190, 800], replicated
- grad_b_in: float32 [800], replicated
- grad_w_depth: float32 [7, 7, 800], replicated
- grad_norm_gain: float32 [800], replicated
- grad_norm_bias: float32 [800], replicated
- grad_w_one: float32 [800, 3200], replicated
- grad_b_one: float32 [3200], replicated
- grad_w_two: float32 [3200, 800], replicated
- grad_b_two: float32 [800], replicated
- grad_w_out: float32 [800, 190], replicated
- grad_b_out: float32 [190], replicated
Inputs may be any that keep to these rules, and one draw needn't show every extreme that they name: `slot_level`: each depth level 0 to 18 stands in exactly one level slot; values 19 or more mark empty slots. Slots g * 5 to (g + 1) * 5 - 1 form group g, whose channels are slot channels g * 50 to (g + 1) * 50 - 1.
All inputs are finite; a program needn't handle non-finite values. No bound on the sum of `wet_mask` on one device may be relied on, other than what follows from the above.
Results may differ from a plain program's by a relative error of at most 0.0076.
Values may be sent and summed in bfloat16 or wider, within the bound.
No kernel may reach another device: no remote copies, remote signals or barrier semaphores. Data moves between devices by JAX's collectives and lax.ppermute only.
A program may use at most 192 MiB of HBM per device.

v0:
```python
import jax
import jax.numpy as jnp
from jax import lax
from jax.sharding import PartitionSpec as P

VARS = 10


exact_mode = lax.Precision.HIGHEST


def padded_2(block, sides, width):
    for axis, dim in sides:
        count = lax.axis_size(axis)
        forward = [(i, i + 1) for i in range(count - 1)]
        backward = [(target, source) for source, target in forward]
        low = lax.ppermute(
            lax.slice_in_dim(block, block.shape[dim] - width, None, axis=dim), axis, forward
        )
        high = lax.ppermute(lax.slice_in_dim(block, 0, width, axis=dim), axis, backward)
        block = jnp.concatenate([low, block, high], axis=dim)
    return block


def exact_gelu(values):
    return jax.nn.gelu(values, approximate=False)


def slot_table(levels_of_slots, slot_count, channels):
    kinds = jnp.arange(slot_count) % VARS
    target = jnp.repeat(levels_of_slots, VARS) * VARS + kinds
    columns = jnp.arange(channels)
    return (target[:, None] == columns[None, :]).astype(jnp.float32)


def on_device(
    ocean_state,
    slot_level,
    wet_mask,
    w_in,
    b_in,
    w_depth,
    norm_gain,
    norm_bias,
    w_one,
    b_one,
    w_two,
    b_two,
    w_out,
    b_out,
    cotangent,
):
    groups = lax.axis_size("lev")
    group_index = lax.axis_index("lev")
    rows_dev = wet_mask.shape[0]
    cols_dev = wet_mask.shape[1]
    date_count = ocean_state.shape[1]
    group_ch = ocean_state.shape[3]
    slot_count = group_ch * groups
    channels = w_in.shape[0]
    width = w_in.shape[1]
    kernel = w_depth.shape[0]
    half = kernel // 2
    pixel_total = float(rows_dev * date_count * cols_dev * groups * lax.axis_size("sp"))
    table = slot_table(slot_level, slot_count, channels)
    w_slots = jnp.dot(table.astype(jnp.bfloat16), w_in, preferred_element_type=jnp.float32).astype(
        jnp.bfloat16
    )
    w_out_slots = jnp.dot(
        w_out, table.T.astype(jnp.bfloat16), preferred_element_type=jnp.float32
    ).astype(jnp.bfloat16)
    b_slots = jnp.dot(table, b_out, precision=exact_mode)
    gathered_in = lax.all_to_all(ocean_state, "lev", split_axis=0, concat_axis=3, tiled=True)
    own_rows = lax.dynamic_slice_in_dim(w_slots, group_index * group_ch, group_ch, 0)
    summed = lax.psum_scatter(
        jnp.einsum("abcs,sd->abcd", ocean_state, own_rows, preferred_element_type=jnp.float32),
        "lev",
        scatter_dimension=0,
        tiled=True,
    )
    hidden = summed + b_in
    lowered = hidden.astype(jnp.bfloat16)
    padded = padded_2(lowered, (("lev", 0), ("sp", 2)), half)
    depth_f32 = w_depth.astype(jnp.float32)
    conv_out = jnp.zeros(hidden.shape, jnp.float32)
    for tap_row in range(kernel):
        for tap_col in range(kernel):
            conv_out = (
                conv_out
                + padded[tap_row : tap_row + rows_dev, :, tap_col : tap_col + cols_dev, :]
                * depth_f32[tap_row, tap_col]
            )
    local_sum = jnp.sum(conv_out, axis=(0, 1, 2))
    local_square = jnp.sum(conv_out * conv_out, axis=(0, 1, 2))
    total_sum, total_square = lax.psum((local_sum, local_square), ("lev", "sp"))
    mean_value = total_sum / pixel_total
    inv_scale = lax.rsqrt(total_square / pixel_total - mean_value * mean_value + 1e-05)
    centered = (conv_out - mean_value) * inv_scale
    normed = (centered * norm_gain + norm_bias).astype(jnp.bfloat16).reshape(-1, width)
    up_values = jnp.dot(normed, w_one, preferred_element_type=jnp.float32) + b_one
    activated_f32, gelu_back = jax.vjp(exact_gelu, up_values)
    activated = activated_f32.astype(jnp.bfloat16)
    branch = jnp.dot(activated, w_two, preferred_element_type=jnp.float32) + b_two
    wet_flat = jnp.broadcast_to(
        wet_mask.astype(jnp.float32)[:, None, :], (rows_dev, date_count, cols_dev)
    ).reshape(-1, 1)
    mixed = ((hidden.reshape(-1, width) + branch) * wet_flat).astype(jnp.bfloat16)
    result = (jnp.dot(mixed, w_out_slots, preferred_element_type=jnp.float32) + b_slots).astype(
        jnp.bfloat16
    )
    result = result.reshape(rows_dev, date_count, cols_dev, slot_count)
    next_state = lax.all_to_all(result, "lev", split_axis=3, concat_axis=0, tiled=True)
    d_result = lax.all_to_all(cotangent, "lev", split_axis=0, concat_axis=3, tiled=True).reshape(
        -1, slot_count
    )
    d_mixed = jnp.dot(d_result, w_out_slots.T, preferred_element_type=jnp.float32)
    g_out_slots = jnp.einsum("ps,pd->sd", d_result, mixed, preferred_element_type=jnp.float32)
    g_bias_slots = jnp.sum(d_result.astype(jnp.float32), axis=0)
    d_sum = d_mixed * wet_flat
    d_branch = d_sum.astype(jnp.bfloat16)
    g_b_two = jnp.sum(d_branch.astype(jnp.float32), axis=0)
    g_w_two = jnp.einsum("pf,pd->fd", activated, d_branch, preferred_element_type=jnp.float32)
    d_act = jnp.dot(d_branch, w_two.T, preferred_element_type=jnp.float32)
    d_up = gelu_back(d_act)[0].astype(jnp.bfloat16)
    g_b_one = jnp.sum(d_up.astype(jnp.float32), axis=0)
    g_w_one = jnp.einsum("pd,pf->df", normed, d_up, preferred_element_type=jnp.float32)
    d_normed = jnp.dot(d_up, w_one.T, preferred_element_type=jnp.float32).reshape(hidden.shape)
    part_bias = jnp.sum(d_normed, axis=(0, 1, 2))
    part_gain = jnp.sum(d_normed * centered, axis=(0, 1, 2))
    grad_norm_bias, grad_norm_gain = lax.psum((part_bias, part_gain), ("lev", "sp"))
    d_conv = (
        norm_gain
        * inv_scale
        * (d_normed - grad_norm_bias / pixel_total - centered * (grad_norm_gain / pixel_total))
    )
    d_conv_low = d_conv.astype(jnp.bfloat16)
    d_conv_f32 = d_conv_low.astype(jnp.float32)
    d_padded = padded_2(d_conv_low, (("lev", 0), ("sp", 2)), half)
    d_lowered = jnp.zeros(hidden.shape, jnp.float32)
    tap_grads = []
    for tap_row in range(kernel):
        for tap_col in range(kernel):
            back_row = kernel - 1 - tap_row
            back_col = kernel - 1 - tap_col
            d_lowered = (
                d_lowered
                + d_padded[back_row : back_row + rows_dev, :, back_col : back_col + cols_dev, :]
                * depth_f32[tap_row, tap_col]
            )
            tap_grads.append(
                jnp.sum(
                    d_conv_f32
                    * padded[tap_row : tap_row + rows_dev, :, tap_col : tap_col + cols_dev, :],
                    axis=(0, 1, 2),
                )
            )
    g_w_depth = jnp.stack(tap_grads).reshape(kernel, kernel, width)
    d_hidden = (d_sum.reshape(hidden.shape) + d_lowered).astype(jnp.bfloat16)
    g_b_in = jnp.sum(d_hidden.astype(jnp.float32), axis=(0, 1, 2))
    d_state = jnp.einsum(
        "abcd,sd->abcs", d_hidden, w_slots, preferred_element_type=jnp.float32
    ).astype(jnp.bfloat16)
    grad_ocean_state = lax.all_to_all(d_state, "lev", split_axis=3, concat_axis=0, tiled=True)
    g_in_slots = jnp.einsum(
        "abcs,abcd->sd", gathered_in, d_hidden, preferred_element_type=jnp.float32
    )
    grad_w_one, grad_w_two, grad_w_depth, grad_b_one, grad_b_two, grad_b_in = lax.psum(
        (g_w_one, g_w_two, g_w_depth, g_b_one, g_b_two, g_b_in), ("lev", "sp")
    )
    group_in, group_out, group_bias = (
        lax.psum_scatter(g_in_slots, "lev", scatter_dimension=0, tiled=True),
        lax.psum_scatter(g_out_slots, "lev", scatter_dimension=0, tiled=True),
        lax.psum_scatter(g_bias_slots, "lev", scatter_dimension=0, tiled=True),
    )
    group_in, group_out, group_bias = lax.psum((group_in, group_out, group_bias), "sp")
    full_in, full_out, full_bias = (
        lax.all_gather(group_in, "lev", axis=0, tiled=True),
        lax.all_gather(group_out, "lev", axis=0, tiled=True),
        lax.all_gather(group_bias, "lev", axis=0, tiled=True),
    )
    grad_w_in = jnp.dot(table.T, full_in, precision=exact_mode)
    grad_w_out = jnp.einsum("sd,sc->dc", full_out, table, precision=exact_mode)
    grad_b_out = jnp.dot(full_bias, table, precision=exact_mode)
    return (
        next_state,
        grad_ocean_state,
        grad_w_in,
        grad_b_in,
        grad_w_depth,
        grad_norm_gain,
        grad_norm_bias,
        grad_w_one,
        grad_b_one,
        grad_w_two,
        grad_b_two,
        grad_w_out,
        grad_b_out,
    )


def solution(mesh):
    return jax.shard_map(
        on_device,
        mesh=mesh,
        in_specs=(
            P(None, None, "sp", "lev"),
            P(),
            P("lev", "sp"),
            P(),
            P(),
            P(),
            P(),
            P(),
            P(),
            P(),
            P(),
            P(),
            P(),
            P(),
            P(None, None, "sp", "lev"),
        ),
        out_specs=(
            P(None, None, "sp", "lev"),
            P(None, None, "sp", "lev"),
            P(),
            P(),
            P(),
            P(),
            P(),
            P(),
            P(),
            P(),
            P(),
            P(),
            P(),
        ),
        check_vma=False,
    )
```

profile of v0, /device:TPU:0, one launch (start us, length us, event | category | flops | bytes accessed | tf_op | source)
XLA Modules:
  0.0 1066.8 jit_solution(11769547777161822764)
XLA Ops:
  8.5 8.7 convolution_bitcast_fusion
  17.2 113.0 %reduce-scatter.6.cloned.1.call-done = f32[8,8,16,800]{3,0,2,1:T(8,128)} async-done(((f32[32,8,16,800]{3,0,2,1:T(8,128)}), f32[8,8,16,800]{3,0,2,1:T(8,128)}) %reduce-scatter.6.cloned.1.call-update) | async-done | bytes 3276816 | tf_op jit(solution)/shard_map/reduce_scatter | solution.py:75
  217.9 8.1 maximum_maximum_fusion
  226.6 52.1 %fusion.168 = (f32[800]{0:T(1024)S(1)}, f32[800]{0:T(1024)S(1)}, f32[8,8,16,800]{3,0,2,1:T(8,128)}) fusion(f32[800]{0:T(1024)S(1)} %copy-done.65, bf16[14,8,19,800]{3,0,2,1:T(8,128)(2,1)} %get-tuple-element.152, f32[800]{0:T(1024)S(1)} %copy-done.67, f32[800]{0:T(1024)S(1)} %copy-done.69, f32[800]{0:T(1024)S(1)} %copy-done.71, ...), kind=kLoop, calls=%fused_computation.384 | loop fusion | flops 136804800 | bytes 75120000 | tf_op jit(solution)/shard_map/reduce_sum | solution.py:93
  278.7 41.5 %all-reduce.8 = (f32[800]{0:T(1024)S(1)}, f32[800]{0:T(1024)S(1)}) all-reduce(f32[800]{0:T(1024)S(1)} %get-tuple-element.66, f32[800]{0:T(1024)S(1)} %get-tuple-element.65), channel_id=1, replica_groups=mesh['lev'=4,'sp'=8] {'lev','sp'}, use_global_device_ids=true, to_apply=%region_4.5 | all-reduce | flops 1600 | bytes 12800 | tf_op jit(solution)/shard_map/psum | solution.py:95
  323.8 35.2 %multiply_convert_fusion = (bf16[1024,3200]{1,0:T(8,128)(2,1)}, f32[1024,3200]{1,0:T(8,128)}, f32[1024,3200]{1,0:T(8,128)}) fusion(f32[3200]{0:T(1024)S(1)} %copy-done.127, bf16[1024,800]{1,0:T(8,128)(2,1)S(1)} %bitcast.106, bf16[800,3200]{1,0:T(8,128)(2,1)S(1)} %copy-done.126), kind=kOutput, calls=%fused_computation.54 | convolution fusion | flops 5459148800 | bytes 39539200 | tf_op jit(solution)/shard_map/dot_general | solution.py:100
  358.9 21.1 %convert_reduce_fusion = (f32[3200]{0:T(1024)}, bf16[1024,3200]{1,0:T(8,128)(2,1)}) fusion(f32[1024,3200]{1,0:T(8,128)} %get-tuple-element.143, bf16[3200,800]{0,1:T(8,128)(2,1)} %param.25, f32[1024,800]{0,1:T(8,128)S(1)} %copy-done.10, f32[1024,3200]{1,0:T(8,128)} %get-tuple-element.165, f32[3200]{0:T(1024)S(1)} %copy-done.127), kind=kOutput, calls=%fused_computation.52 | convolution fusion | flops 5299401728 | bytes 41190400 | tf_op jit(solution)/shard_map/dot_general | solution.py:123
  380.1 11.0 %fusion.177 = (f32[800]{0:T(1024)S(1)}, f32[1024,800]{0,1:T(8,128)}) fusion(bf16[1024,3200]{1,0:T(8,128)(2,1)} %get-tuple-element.169, bf16[800,3200]{1,0:T(8,128)(2,1)} %param.23), kind=kOutput, calls=%fused_computation.389 | convolution fusion | flops 5243698176 | bytes 14953600 | tf_op jit(solution)/shard_map/dot_general | solution.py:127
  401.3 40.8 %all-reduce.7 = (f32[800]{0:T(1024)S(1)}, f32[800]{0:T(1024)S(1)}) all-reduce(f32[800]{0:T(1024)S(1)} %multiply_reduce_fusion, f32[800]{0:T(1024)S(1)} %get-tuple-element.166), channel_id=1, replica_groups=mesh['lev'=4,'sp'=8] {'lev','sp'}, use_global_device_ids=true, to_apply=%region_8.9 | all-reduce | flops 1600 | bytes 12800 | tf_op jit(solution)/shard_map/psum | solution.py:130
  442.1 32.0 %fusion.125 = (f32[800]{0:T(1024)S(1)}, f32[800]{0:T(1024)S(1)}, f32[800]{0:T(1024)S(1)}, f32[800]{0:T(1024)S(1)}, f32[800]{0:T(1024)S(1)}, /*index=5*/f32[800]{...) fusion(bf16[14,8,19,800]{3,0,2,1:T(8,128)(2,1)} %copy-done.2, ...), kind=kLoop, calls=%fused_computation.255 | loop fusion | flops 50776000 | bytes 37756800 | tf_op jit(solution)/shard_map/reduce_sum | solution.py:151
  475.1 9.9 fusion.129
  489.6 8.0 multiply_convert_fusion.2
  497.7 8.8 fusion.128
  515.2 11.2 %fusion.162 = f32[3200,800]{0,1:T(8,128)} fusion(bf16[1024,3200]{1,0:T(8,128)(2,1)} %get-tuple-element.142, f32[1024,800]{0,1:T(8,128)S(1)} %copy-done.11), kind=kOutput, calls=%fused_computation.380 | convolution fusion | flops 5243699200 | bytes 20070400 | tf_op jit(solution)/shard_map/pf,pd->fd/dot_general | solution.py:122
  528.2 12.6 %collective-permute-done.7 = bf16[14,8,3,800]{3,1,2,0:T(8,128)(2,1)S(1)} collective-permute-done((bf16[14,8,3,800]{3,1,2,0:T(8,128)(2,1)S(1)}, bf16[14,8,3,800]{3,1,2,0:T(8,128)(2,1)S(1)}, u32[]{:S(2)}, u32[]{:S(2)}) %collective-permute-start.7) | collective-permute-done | bytes 537632 | tf_op jit(solution)/shard_map/ppermute | solution.py:17
  547.9 49.9 %convert_reduce_fusion.1 = (f32[800]{0:T(1024)S(1)}, bf16[8,8,16,800]{3,0,2,1:T(8,128)(2,1)}) fusion(f32[800]{0:T(1024)S(1)} %copy-done.66, bf16[14,8,19,800]{3,0,2,1:T(8,128)(2,1)} %get-tuple-element.148, f32[800]{0:T(1024)S(1)} %copy-done.68, f32[800]{0:T(1024)S(1)} %copy-done.70, f32[800]{0:T(1024)S(1)} %copy-done.72, ...), kind=kLoop, calls=%fused_computation.262 | loop fusion | flops 137624800 | bytes 76755200 | tf_op jit(solution)/shard_map/reduce_sum | solution.py:159
  600.0 20.3 %fusion.169 = (f32[64,800]{1,0:T(8,128)S(1)}, f32[64,800]{1,0:T(8,128)S(1)}) fusion(f32[200,800]{1,0:T(8,128)S(1)} %convolution_bitcast_fusion.2, f32[200,800]{1,0:T(8,128)} %convolution_bitcast_fusion.1), kind=kCustom, calls=%all-reduce-scatter.2 | all-reduce-scatter fusion | flops 409601 | bytes 1690112
  624.9 13.2 %fusion.178 = f32[800,3200]{1,0:T(8,128)} fusion(bf16[1024,800]{1,0:T(8,128)(2,1)} %bitcast.107, bf16[1024,3200]{1,0:T(8,128)(2,1)} %get-tuple-element.169), kind=kOutput, calls=%fused_computation.390 | convolution fusion | flops 5242880000 | bytes 18432000 | tf_op jit(solution)/shard_map/pd,pf->df/dot_general | solution.py:126
  686.0 19.6 %psum.103 = f32[50]{0:T(128)S(1)} all-reduce(f32[50]{0:T(128)S(1)} %dynamic-slice.6), channel_id=1, replica_groups=mesh['lev'=4,'sp'=8] {'sp'}, use_global_device_ids=true, to_apply=%region_73.74 | all-reduce | flops 50 | bytes 400 | tf_op jit(solution)/shard_map/psum | solution.py:175
  722.0 39.3 %all-reduce.6 = (f32[800]{0:T(1024)}, f32[3200]{0:T(1024)}, f32[800]{0:T(1024)}) all-reduce(f32[800]{0:T(1024)S(1)} %get-tuple-element.140, f32[3200]{0:T(1024)S(1)} %copy-done.118, f32[800]{0:T(1024)S(1)} %copy-done.117), channel_id=1, replica_groups=mesh['lev'=4,'sp'=8] {'lev','sp'}, use_global_device_ids=true, to_apply=%region_12.13 | all-reduce | flops 4800 | bytes 38400 | tf_op jit(solution)/shard_map/psum | solution.py:167
  770.7 13.6 %all-gather = f32[4,50,800]{2,1,0:T(8,128)S(1)} all-gather(f32[1,50,800]{2,1,0:T(8,128)} %bitcast.111), channel_id=1, replica_groups=mesh['lev'=4,'sp'=8] {'lev'}, dimensions={0}, use_global_device_ids=true | all-gather | bytes 800000 | tf_op jit(solution)/shard_map/all_gather | solution.py:177
  784.5 13.6 %all-gather.1 = f32[4,50,800]{2,1,0:T(8,128)S(1)} all-gather(f32[1,50,800]{2,1,0:T(8,128)} %bitcast.110), channel_id=1, replica_groups=mesh['lev'=4,'sp'=8] {'lev'}, dimensions={0}, use_global_device_ids=true | all-gather | bytes 800000 | tf_op jit(solution)/shard_map/all_gather | solution.py:178
  801.0 244.3 %all-reduce.15.cloned.1.call-done = (f32[7,7,800]{2,1,0:T(8,128)}, f32[800,3200]{1,0:T(8,128)}, f32[3200,800]{0,1:T(8,128)}) async-done(((f32[7,7,800]{2,1,0:T(8,128)}, f32[800,3200]{1,0:T(8,128)}, f32[3200,800]{0,1:T(8,128)}), (f32[7,7,800]{2,1,0:T(8,128)}, f32[800,3200]{1,0:T(8,128)}, f32[3200,800]{0,1:T(8,128)})) %all-reduce.15.cloned.1.call-update) | async-done | bytes 20636816 | tf_op jit(solution)/shard_map/psum | solution.py:167
  1047.1 8.7 copy.116
  (451 shorter events, 211.5 us)
Async XLA Ops:
  7.2 123.0 %reduce-scatter.6.cloned.1.call-start = ((), (), s32[]{:S(2)}) async-start(), calls=%async_computation.5 | async-start | bytes 18350080 | tf_op jit(solution)/shard_map/reduce_scatter | solution.py:75
  8.1 162.6 %copy-start.114 = (s32[200]{0:T(256)}, s32[200]{0:T(256)S(1)}, u32[]{:S(2)}) copy-start(s32[200]{0:T(256)S(1)} %fusion.160) | copy-start | bytes 2404
  17.2 113.0 %copy-start.121 = (f32[800]{0:T(1024)S(1)}, f32[800]{0:T(1024)}, u32[]{:S(2)}) copy-start(f32[800]{0:T(1024)} %param.19) | copy-start | bytes 9604
  134.6 91.4 %copy-start.3 = (bf16[8,8,16,800]{3,0,2,1:T(8,128)(2,1)}, bf16[8,8,16,800]{3,0,2,1:T(8,128)(2,1)S(1)}, u32[]{:S(2)}) copy-start(bf16[8,8,16,800]{3,0,2,1:T(8,128)(2,1)S(1)} %get-tuple-element.145) | copy-start | bytes 4915204
  136.4 22.4 %collective-permute-start.1 = (bf16[3,8,16,800]{3,2,1,0:T(8,128)(2,1)}, bf16[3,8,16,800]{3,2,1,0:T(8,128)(2,1)}, u32[]{:S(2)}, u32[]{:S(2)}) collective-permute-start(bf16[3,8,16,800]{3,2,1,0:T(8,128)(2,1)} %copy.53), channel_id=1, source_target_pairs={{8,0},{16,8},{24,16},{9,1},{17,9},{25,17},{10,2},{18,10},{26,18},{... | collective-permute-start | bytes 1843208 | tf_op jit(solution)/shard_map/ppermute | solution.py:20
  138.6 21.9 %collective-permute-start = (bf16[3,8,16,800]{3,2,1,0:T(8,128)(2,1)}, bf16[3,8,16,800]{3,2,1,0:T(8,128)(2,1)}, u32[]{:S(2)}, u32[]{:S(2)}) collective-permute-start(bf16[3,8,16,800]{3,2,1,0:T(8,128)(2,1)} %copy.52), channel_id=1, source_target_pairs={{0,8},{8,16},{16,24},{1,9},{9,17},{17,25},{2,10},{10,18},{18,26},{... | collective-permute-start | bytes 1843208 | tf_op jit(solution)/shard_map/ppermute | solution.py:17
  146.8 25.0 %all-to-all-start.1 = ((bf16[4,2,25600]{2,1,0:T(2,128)(2,1)}), bf16[4,2,25600]{2,1,0:T(2,128)(2,1)}, u32[]{:S(2)}, u32[]{:S(2)}) async-start(bf16[4,2,25600]{2,1,0:T(2,128)(2,1)} %reshape.207), calls=%async_computation.2 | async-start | bytes 819200 | tf_op jit(solution)/shard_map/all_to_all | solution.py:113
  157.9 68.2 %copy-start.35 = (f32[800]{0:T(1024)}, f32[800]{0:T(1024)S(1)}, u32[]{:S(2)}) copy-start(f32[800]{0:T(1024)S(1)} %get-tuple-element.98) | copy-start | bytes 9604
  157.9 68.2 %copy-start.37 = (f32[800]{0:T(1024)}, f32[800]{0:T(1024)S(1)}, u32[]{:S(2)}) copy-start(f32[800]{0:T(1024)S(1)} %get-tuple-element.99) | copy-start | bytes 9604
  164.3 51.0 %collective-permute-start.2 = (bf16[14,8,3,800]{3,1,2,0:T(8,128)(2,1)}, bf16[14,8,3,800]{3,1,2,0:T(8,128)(2,1)}, u32[]{:S(2)}, u32[]{:S(2)}) collective-permute-start(bf16[14,8,3,800]{3,1,2,0:T(8,128)(2,1)} %copy.56), channel_id=1, source_target_pairs={{0,1},{1,2},{2,3},{3,4},{4,5},{5,6},{6,7},{8,9},{9,10},{10,11},{11... | collective-permute-start | bytes 1612808 | tf_op jit(solution)/shard_map/ppermute | solution.py:17
  169.4 47.0 %collective-permute-start.3 = (bf16[14,8,3,800]{3,1,2,0:T(8,128)(2,1)}, bf16[14,8,3,800]{3,1,2,0:T(8,128)(2,1)}, u32[]{:S(2)}, u32[]{:S(2)}) collective-permute-start(bf16[14,8,3,800]{3,1,2,0:T(8,128)(2,1)} %copy.59), channel_id=1, source_target_pairs={{1,0},{2,1},{3,2},{4,3},{5,4},{6,5},{7,6},{9,8},{10,9},{11,10},{12... | collective-permute-start | bytes 1612808 | tf_op jit(solution)/shard_map/ppermute | solution.py:20
  171.8 24.0 %all-to-all-start.3 = ((bf16[4,2,25600]{2,1,0:T(2,128)(2,1)}), bf16[4,2,25600]{2,1,0:T(2,128)(2,1)S(1)}, u32[]{:S(2)}, u32[]{:S(2)}) async-start(bf16[4,2,25600]{2,1,0:T(2,128)(2,1)} %reshape.211), calls=%async_computation.4 | async-start | bytes 819200 | tf_op jit(solution)/shard_map/all_to_all | solution.py:73
  175.2 595.5 %all-reduce.17.cloned.1.call-start = ((), (), s32[]{:S(2)}) async-start(), calls=%async_computation.7 | async-start | bytes 802816 | tf_op jit(solution)/shard_map/psum | solution.py:175
  226.5 93.7 %copy-start.119 = (f32[800]{0:T(1024)S(1)}, f32[800]{0:T(1024)}, u32[]{:S(2)}) copy-start(f32[800]{0:T(1024)} %param.21) | copy-start | bytes 9604
  226.6 93.7 %copy-start.125 = (f32[800]{0:T(1024)S(1)}, f32[800]{0:T(1024)}, u32[]{:S(2)}) copy-start(f32[800]{0:T(1024)} %param.22) | copy-start | bytes 9604
  485.1 21.4 %collective-permute-start.5 = (bf16[3,8,16,800]{3,2,1,0:T(8,128)(2,1)S(1)}, bf16[3,8,16,800]{3,2,1,0:T(8,128)(2,1)S(1)}, u32[]{:S(2)}, u32[]{:S(2)}) collective-permute-start(bf16[3,8,16,800]{3,2,1,0:T(8,128)(2,1)S(1)} %copy.73), channel_id=1, source_target_pairs={{8,0},{16,8},{24,16},{9,1},{17,9},{25,17},{10,2},{18,10},{26,18},{... | collective-permute-start | bytes 1843208 | tf_op jit(solution)/shard_map/ppermute | solution.py:20
  486.4 20.6 %collective-permute-start.4 = (bf16[3,8,16,800]{3,2,1,0:T(8,128)(2,1)S(1)}, bf16[3,8,16,800]{3,2,1,0:T(8,128)(2,1)S(1)}, u32[]{:S(2)}, u32[]{:S(2)}) collective-permute-start(bf16[3,8,16,800]{3,2,1,0:T(8,128)(2,1)S(1)} %copy.72), channel_id=1, source_target_pairs={{0,8},{8,16},{16,24},{1,9},{9,17},{17,25},{2,10},{10,18},{18,26},{... | collective-permute-start | bytes 1843208 | tf_op jit(solution)/shard_map/ppermute | solution.py:17
  508.6 19.5 %collective-permute-start.6 = (bf16[14,8,3,800]{3,1,2,0:T(8,128)(2,1)S(1)}, bf16[14,8,3,800]{3,1,2,0:T(8,128)(2,1)S(1)}, u32[]{:S(2)}, u32[]{:S(2)}) collective-permute-start(bf16[14,8,3,800]{3,1,2,0:T(8,128)(2,1)S(1)} %copy.76), channel_id=1, source_target_pairs={{1,0},{2,1},{3,2},{4,3},{5,4},{6,5},{7,6},{9,8},{10,9},{11,10},{12... | collective-permute-start | bytes 1612808 | tf_op jit(solution)/shard_map/ppermute | solution.py:20
  510.2 30.5 %collective-permute-start.7 = (bf16[14,8,3,800]{3,1,2,0:T(8,128)(2,1)S(1)}, bf16[14,8,3,800]{3,1,2,0:T(8,128)(2,1)S(1)}, u32[]{:S(2)}, u32[]{:S(2)}) collective-permute-start(bf16[14,8,3,800]{3,1,2,0:T(8,128)(2,1)S(1)} %copy.79), channel_id=1, source_target_pairs={{0,1},{1,2},{2,3},{3,4},{4,5},{5,6},{6,7},{8,9},{9,10},{10,11},{11... | collective-permute-start | bytes 1612808 | tf_op jit(solution)/shard_map/ppermute | solution.py:17
  620.4 17.7 %collective-permute-start.8 = (f32[42,800]{1,0:T(8,128)S(1)}, f32[42,800]{1,0:T(8,128)S(1)}, u32[]{:S(2)}, u32[]{:S(2)}) collective-permute-start(f32[42,800]{1,0:T(8,128)S(1)} %slice.958), channel_id=1, source_target_pairs={{0,8},{8,16},{16,24},{1,9},{9,17},{17,25},{2,10},{10,18},{18,26},{... | collective-permute-start | bytes 403208
  621.7 17.3 %collective-permute-start.9 = (f32[42,800]{1,0:T(8,128)S(1)}, f32[42,800]{1,0:T(8,128)S(1)}, u32[]{:S(2)}, u32[]{:S(2)}) collective-permute-start(f32[42,800]{1,0:T(8,128)S(1)} %slice.959), channel_id=1, source_target_pairs={{0,8},{8,16},{16,24},{1,9},{9,17},{17,25},{2,10},{10,18},{18,26},{... | collective-permute-start | bytes 403208
  640.1 405.3 %all-reduce.15.cloned.1.call-start = ((), (), s32[]{:S(2)}) async-start(), calls=%async_computation.6 | async-start | bytes 41361408 | tf_op jit(solution)/shard_map/psum | solution.py:167
  656.9 16.2 %all-to-all-start = ((bf16[4,2,25600]{2,1,0:T(2,128)(2,1)}), bf16[4,2,25600]{2,1,0:T(2,128)(2,1)S(1)}, u32[]{:S(2)}, u32[]{:S(2)}) async-start(bf16[4,2,25600]{2,1,0:T(2,128)(2,1)} %reshape.205), calls=%async_computation.1 | async-start | bytes 819200 | tf_op jit(solution)/shard_map/all_to_all | solution.py:112
  673.0 88.3 %all-to-all-start.2 = ((bf16[4,2,25600]{2,1,0:T(2,128)(2,1)}), bf16[4,2,25600]{2,1,0:T(2,128)(2,1)S(1)}, u32[]{:S(2)}, u32[]{:S(2)}) async-start(bf16[4,2,25600]{2,1,0:T(2,128)(2,1)} %reshape.209), calls=%async_computation.3 | async-start | bytes 819200 | tf_op jit(solution)/shard_map/all_to_all | solution.py:163
  (130 other events, 1971.4 us)
Sparse Core Ops, SparseCore 0:
  17.4 112.8 reduce-scatter.5
  640.2 70.7 all-reduce.16
  718.6 326.7 all-reduce.14
where the time goes:
time: 1070 us
  waiting for transfers between devices  370 us (35%)
  blocking collectives  203 us (19%)
  other arithmetic  188 us (18%)
  matrix products  124 us (12%)
  local copies, waits for them, and re-layouts  123 us (11%)
  starting transfers between devices  41.2 us (4%)
  between operations  18.7 us (2%)
    psum x1, waiting for transfers between devices, on_device(): lax.psum((g_w_one, g_w_two, g_w_depth, g_b_one, g_b_two, g_b_in), ('lev',...  244 us
    reduce_scatter x1, waiting for transfers between devices, on_device(): lax.psum_scatter(jnp.einsum('abcs,sd->abcd', ocean_state, own_rows, prefe...  113 us
    unnamed x297, local copies, waits for them, and re-layouts  55 us
    reduce_sum x4, other arithmetic, on_device(): jnp.sum(d_conv_f32 * padded[tap_row:tap_row + rows_dev, :, tap_col:tap_co...  54.7 us
    reduce_sum x1, other arithmetic, on_device(): local_sum = jnp.sum(conv_out, axis=(0, 1, 2))  52.1 us
    reduce_sum x1, other arithmetic, on_device(): g_b_in = jnp.sum(d_hidden.astype(jnp.float32), axis=(0, 1, 2))  49.9 us
    psum x1, blocking collectives, on_device(): total_sum, total_square = lax.psum((local_sum, local_square), ('lev', 'sp'))  41.5 us
    psum x1, blocking collectives, on_device(): lax.psum((part_bias, part_gain), ('lev', 'sp'))  40.8 us
  transfers between devices with their start and end apart: 17, of which 3 were waited for; matrix products, arithmetic and copies ran while one was open for 14% of the time, Pallas kernels for 0%

commit v1 on v0

v1 whole, which is shorter than its diff:
```python
import functools

import jax
import jax.numpy as jnp
from jax import lax
from jax.experimental import pallas as pl
from jax.experimental.pallas import tpu as pltpu
from jax.sharding import PartitionSpec as P

VARS = 10
LANES = 128
SUBLANES = 8

exact_mode = lax.Precision.HIGHEST
F32 = jnp.float32
BF16 = jnp.bfloat16

TAIL_SCALE = 0.3
TAIL_POLY = (
    0.119623263,
    0.120845528,
    0.0993471402,
    0.130416391,
    -0.0571672287,
    0.210118226,
    -0.159378204,
    0.0361948279,
)


def slot_table(levels_of_slots, slot_count, channels):
    kinds = jnp.arange(slot_count) % VARS
    target = jnp.repeat(levels_of_slots, VARS) * VARS + kinds
    columns = jnp.arange(channels)
    return (target[:, None] == columns[None, :]).astype(F32)


def bits_of(axis):
    size = lax.axis_size(axis)
    return [(axis, 1 << k) for k in range(size.bit_length() - 1)]


def hop(value, stage):
    axis, bit = stage
    return lax.ppermute(value, axis, [(i, i ^ bit) for i in range(lax.axis_size(axis))])


def side(stage):
    axis, bit = stage
    return (lax.axis_index(axis) // bit) % 2


def butterfly(value, stages):
    for stage in stages:
        value = value + hop(value, stage)
    return value


def reduce_blocks(blocks, stages, link):
    count = blocks.shape[0]
    kept = []
    value = blocks
    own = 0
    for stage in stages:
        if count % 2 == 0:
            half = count // 2
            bit = side(stage)
            sent = lax.dynamic_slice_in_dim(value, (1 - bit) * half, half, 0).astype(link)
            stay = lax.dynamic_slice_in_dim(value, bit * half, half, 0)
            value = stay.astype(F32) + hop(sent, stage).astype(F32)
            kept.append(stage)
            own = own * 2 + bit
            count = half
        else:
            sent = value.astype(link)
            value = sent.astype(F32) + hop(sent, stage).astype(F32)
    value = value.astype(link)
    for stage in reversed(kept):
        value = jnp.concatenate([value, hop(value, stage)], axis=0)
    pieces = 1 << len(kept)
    return [
        lax.dynamic_slice_in_dim(value, (index ^ own) * count, count, 0) for index in range(pieces)
    ]


def hidden_conv_body(rows, cols, half, edge_ref, x_ref, w_ref, b_ref, depth_ref, hidden_ref, low_ref, conv_ref, stat_ref, pad_ref):
    kernel = 2 * half + 1
    value = jnp.dot(x_ref[...], w_ref[...], preferred_element_type=F32) + b_ref[...]
    value = value.reshape(rows + 2 * half, cols + 2 * half, SUBLANES, LANES)
    hidden_ref[...] = value[half : half + rows, half : half + cols]
    pad_ref[...] = value.astype(BF16).astype(F32)

    @pl.when(edge_ref[0] == 1)
    def _():
        pad_ref[:half] = jnp.zeros((half,) + pad_ref.shape[1:], F32)

    @pl.when(edge_ref[1] == 1)
    def _():
        pad_ref[half + rows :] = jnp.zeros((half,) + pad_ref.shape[1:], F32)

    @pl.when(edge_ref[2] == 1)
    def _():
        pad_ref[:, :half] = jnp.zeros((pad_ref.shape[0], half) + pad_ref.shape[2:], F32)

    @pl.when(edge_ref[3] == 1)
    def _():
        pad_ref[:, half + cols :] = jnp.zeros((pad_ref.shape[0], half) + pad_ref.shape[2:], F32)

    low_ref[...] = pad_ref[...].reshape(low_ref.shape).astype(BF16)

    def one_row(row, carry):
        total, square = carry
        acc = jnp.zeros((cols, SUBLANES, LANES), F32)
        for i in range(kernel):
            slab = pad_ref[row + i]
            for j in range(kernel):
                acc = acc + slab[j : j + cols] * depth_ref[i * kernel + j]
        conv_ref[row] = acc
        return total + jnp.sum(acc, axis=0), square + jnp.sum(acc * acc, axis=0)

    zero = jnp.zeros((SUBLANES, LANES), F32)
    total, square = lax.fori_loop(0, rows, one_row, (zero, zero))
    stat_ref[0:1] = jnp.sum(total, axis=0, keepdims=True)
    stat_ref[1:2] = jnp.sum(square, axis=0, keepdims=True)


def hidden_conv(edges, x, w_slots, b_in, depth, tile):
    rows, cols, dates, half = tile
    width = w_slots.shape[1]
    padded = (rows + 2 * half) * (cols + 2 * half) * dates
    slots = x.shape[1]
    grid = pl.cdiv(width, LANES)
    return pl.pallas_call(
        functools.partial(hidden_conv_body, rows, cols, half),
        grid=(grid,),
        in_specs=[
            pl.BlockSpec(memory_space=pltpu.SMEM),
            pl.BlockSpec((padded, slots), lambda i: (0, 0)),
            pl.BlockSpec((slots, LANES), lambda i: (0, i)),
            pl.BlockSpec((1, LANES), lambda i: (0, i)),
            pl.BlockSpec((depth.shape[0], 1, LANES), lambda i: (0, 0, i)),
        ],
        out_specs=[
            pl.BlockSpec((rows, cols, dates, LANES), lambda i: (0, 0, 0, i)),
            pl.BlockSpec((padded, LANES), lambda i: (0, i)),
            pl.BlockSpec((rows, cols, dates, LANES), lambda i: (0, 0, 0, i)),
            pl.BlockSpec((2, LANES), lambda i: (0, i)),
        ],
        out_shape=[
            jax.ShapeDtypeStruct((rows, cols, dates, width), F32),
            jax.ShapeDtypeStruct((padded, width), BF16),
            jax.ShapeDtypeStruct((rows, cols, dates, width), F32),
            jax.ShapeDtypeStruct((2, width), F32),
        ],
        scratch_shapes=[pltpu.VMEM((rows + 2 * half, cols + 2 * half, dates, LANES), F32)],
        name="hidden_conv",
    )(edges, x, w_slots, b_in.reshape(1, -1), depth)


def gelu_pair(values):
    size = jnp.abs(values)
    gauss = jnp.exp(-0.5 * values * values)
    t = 1.0 / (1.0 + TAIL_SCALE * size)
    poly = jnp.full_like(t, TAIL_POLY[-1])
    for factor in TAIL_POLY[-2::-1]:
        poly = poly * t + factor
    tail = gauss * (t * poly)
    below = jnp.where(values >= 0, 1.0 - tail, tail)
    return values * below, below + values * (gauss * 0.3989422804014327)


def mlp_body(row_block, normed_ref, branch_ref, w_one_ref, b_one_ref, w_two_ref, act_ref, dup_ref, grad_ref, gb_ref, normed_t, branch_t):
    @pl.when(pl.program_id(0) == 0)
    def _():
        normed_t[...] = normed_ref[...].T
        branch_t[...] = branch_ref[...].T

    total = jnp.zeros((1, act_ref.shape[1]), F32)
    for start in range(0, normed_ref.shape[0], row_block):
        rows = pl.ds(start, row_block)
        up = jnp.dot(normed_ref[rows], w_one_ref[...], preferred_element_type=F32) + b_one_ref[...]
        d_act = lax.dot_general(
            branch_ref[rows], w_two_ref[...], (((1,), (1,)), ((), ())), preferred_element_type=F32
        )
        value, slope = gelu_pair(up)
        act_ref[rows] = value.astype(BF16)
        d_up = (slope * d_act).astype(BF16)
        dup_ref[rows] = d_up
        total = total + jnp.sum(d_up.astype(F32), axis=0, keepdims=True)
    gb_ref[...] = total
    grad_ref[0] = jnp.dot(normed_t[...], dup_ref[...], preferred_element_type=F32).astype(BF16)
    grad_ref[1] = jnp.dot(branch_t[...], act_ref[...], preferred_element_type=F32).astype(BF16)


def mlp(normed, d_branch, w_one, b_one, w_two, block=256, row_block=256):
    pixels, width = normed.shape
    hidden = w_one.shape[1]
    return pl.pallas_call(
        functools.partial(mlp_body, row_block),
        grid=(pl.cdiv(hidden, block),),
        in_specs=[
            pl.BlockSpec((pixels, width), lambda i: (0, 0)),
            pl.BlockSpec((pixels, width), lambda i: (0, 0)),
            pl.BlockSpec((width, block), lambda i: (0, i)),
            pl.BlockSpec((1, block), lambda i: (0, i)),
            pl.BlockSpec((block, width), lambda i: (i, 0)),
        ],
        out_specs=[
            pl.BlockSpec((pixels, block), lambda i: (0, i)),
            pl.BlockSpec((pixels, block), lambda i: (0, i)),
            pl.BlockSpec((2, width, block), lambda i: (0, 0, i)),
            pl.BlockSpec((1, block), lambda i: (0, i)),
        ],
        out_shape=[
            jax.ShapeDtypeStruct((pixels, hidden), BF16),
            jax.ShapeDtypeStruct((pixels, hidden), BF16),
            jax.ShapeDtypeStruct((2, width, hidden), BF16),
            jax.ShapeDtypeStruct((1, hidden), F32),
        ],
        scratch_shapes=[pltpu.VMEM((width, pixels), BF16), pltpu.VMEM((width, pixels), BF16)],
        name="mlp",
    )(normed, d_branch, w_one, b_one.reshape(1, -1), w_two)


def conv_back_body(rows, cols, half, edge_ref, coef_ref, dn_ref, conv_ref, dsum_ref, low_ref, depth_ref, dh_ref, gw_ref, gb_ref, dc_ref, dl_ref, pad_ref, tap_ref):
    kernel = 2 * half + 1
    wide = cols + 2 * half
    d_conv = coef_ref[0:1] * dn_ref[...] + (coef_ref[1:2] * conv_ref[...] + coef_ref[2:3])
    dc_ref[...] = d_conv.astype(BF16).astype(F32)
    dl_ref[...] = jnp.zeros(dl_ref.shape, F32)
    dl_ref[half : half + rows, half : half + cols] = dsum_ref[...]
    pad_ref[...] = low_ref[...].astype(F32).reshape(pad_ref.shape)
    tap_ref[...] = jnp.zeros(tap_ref.shape, F32)

    def one_row(row, carry):
        source = [dc_ref[row, c] for c in range(cols)]
        for i in range(kernel):
            taps = [jnp.broadcast_to(depth_ref[i * kernel + j], (SUBLANES, LANES)) for j in range(kernel)]
            for c in range(wide):
                acc = dl_ref[row + i, c]
                for j in range(kernel):
                    if 0 <= c - j < cols:
                        acc = acc + source[c - j] * taps[j]
                dl_ref[row + i, c] = acc
        for i in range(kernel):
            sums = [tap_ref[i * kernel + j] for j in range(kernel)]
            for c in range(wide):
                value = pad_ref[row + i, c]
                for j in range(kernel):
                    if 0 <= c - j < cols:
                        sums[j] = sums[j] + source[c - j] * value
            for j in range(kernel):
                tap_ref[i * kernel + j] = sums[j]
        return carry

    lax.fori_loop(0, rows, one_row, 0)

    @pl.when(edge_ref[0] == 1)
    def _():
        dl_ref[:half] = jnp.zeros((half,) + dl_ref.shape[1:], F32)

    @pl.when(edge_ref[1] == 1)
    def _():
        dl_ref[half + rows :] = jnp.zeros((half,) + dl_ref.shape[1:], F32)

    @pl.when(edge_ref[2] == 1)
    def _():
        dl_ref[:, :half] = jnp.zeros((dl_ref.shape[0], half) + dl_ref.shape[2:], F32)

    @pl.when(edge_ref[3] == 1)
    def _():
        dl_ref[:, half + cols :] = jnp.zeros((dl_ref.shape[0], half) + dl_ref.shape[2:], F32)

    d_hidden = dl_ref[...]
    dh_ref[...] = d_hidden.reshape(dh_ref.shape).astype(BF16)
    gb_ref[...] = jnp.sum(jnp.sum(d_hidden, axis=(0, 1)), axis=0, keepdims=True)
    gw_ref[...] = jnp.sum(tap_ref[...], axis=1)


def conv_back(edges, coef, d_normed, conv_out, d_sum, lowered, depth, tile):
    rows, cols, dates, half = tile
    taps = depth.shape[0]
    width = lowered.shape[1]
    padded = lowered.shape[0]
    inner = pl.BlockSpec((rows, cols, dates, LANES), lambda i: (0, 0, 0, i))
    wide = (rows + 2 * half, cols + 2 * half, dates, LANES)
    return pl.pallas_call(
        functools.partial(conv_back_body, rows, cols, half),
        grid=(pl.cdiv(width, LANES),),
        in_specs=[
            pl.BlockSpec(memory_space=pltpu.SMEM),
            pl.BlockSpec((3, LANES), lambda i: (0, i)),
            inner,
            inner,
            inner,
            pl.BlockSpec((padded, LANES), lambda i: (0, i)),
            pl.BlockSpec((taps, 1, LANES), lambda i: (0, 0, i)),
        ],
        out_specs=[
            pl.BlockSpec((padded, LANES), lambda i: (0, i)),
            pl.BlockSpec((taps, LANES), lambda i: (0, i)),
            pl.BlockSpec((1, LANES), lambda i: (0, i)),
        ],
        out_shape=[
            jax.ShapeDtypeStruct((padded, width), BF16),
            jax.ShapeDtypeStruct((taps, width), F32),
            jax.ShapeDtypeStruct((1, width), F32),
        ],
        scratch_shapes=[
            pltpu.VMEM((rows, cols, dates, LANES), F32),
            pltpu.VMEM(wide, F32),
            pltpu.VMEM(wide, F32),
            pltpu.VMEM((taps, dates, LANES), F32),
        ],
        name="conv_back",
    )(edges, coef, d_normed, conv_out, d_sum, lowered, depth)


def on_device(
    ocean_state,
    slot_level,
    wet_mask,
    w_in,
    b_in,
    w_depth,
    norm_gain,
    norm_bias,
    w_one,
    b_one,
    w_two,
    b_two,
    w_out,
    b_out,
    cotangent,
):
    groups = lax.axis_size("lev")
    strips = lax.axis_size("sp")
    group_index = lax.axis_index("lev")
    strip_index = lax.axis_index("sp")
    rows, cols = wet_mask.shape
    all_rows, dates, _, group_ch = ocean_state.shape
    slots = group_ch * groups
    channels, width = w_in.shape
    kernel = w_depth.shape[0]
    half = kernel // 2
    tile = (rows, cols, dates, half)
    high_rows, wide_cols = rows + 2 * half, cols + 2 * half
    pixels = rows * cols * dates
    pixel_total = float(pixels * groups * strips)

    lev_stages = bits_of("lev")
    sp_stages = bits_of("sp")
    stages = lev_stages + sp_stages
    core, lev_rest = lev_stages[:1], lev_stages[1:]
    orders = (
        core + lev_rest + sp_stages,
        core + sp_stages[:1] + lev_rest + sp_stages[1:],
        core + sp_stages[1:2] + lev_rest + sp_stages[:1] + sp_stages[2:],
    )
    forward = [(i, i + 1) for i in range(strips - 1)]
    backward = [(i + 1, i) for i in range(strips - 1)]
    edges = jnp.stack(
        [group_index == 0, group_index == groups - 1, strip_index == 0, strip_index == strips - 1]
    ).astype(jnp.int32)

    table = slot_table(slot_level, slots, channels)
    table_low = table.astype(BF16)
    w_slots = jnp.dot(table_low, w_in, preferred_element_type=F32).astype(BF16)
    w_out_slots = jnp.dot(w_out, table_low.T, preferred_element_type=F32).astype(BF16)
    b_slots = jnp.dot(table, b_out, precision=exact_mode)
    depth = w_depth.astype(F32).reshape(kernel * kernel, 1, width)

    state = ocean_state.transpose(0, 2, 1, 3).reshape(all_rows, cols, dates * group_ch)
    low_cols = lax.ppermute(state[:, cols - half :], "sp", forward)
    high_cols = lax.ppermute(state[:, :half], "sp", backward)
    state = jnp.concatenate([low_cols, state, high_cols], axis=1)
    state = jnp.pad(state, ((half, half), (0, 0), (0, 0)))
    windows = jnp.stack([state[g * rows : g * rows + high_rows] for g in range(groups)])
    windows = lax.all_to_all(windows, "lev", split_axis=0, concat_axis=0, tiled=True)
    x_pad = (
        windows.reshape(groups, high_rows, wide_cols, dates, group_ch)
        .transpose(1, 2, 3, 0, 4)
        .reshape(high_rows * wide_cols * dates, slots)
    )
    d_result = cotangent.transpose(0, 2, 1, 3).reshape(groups, rows, cols, dates * group_ch)
    d_result = lax.all_to_all(d_result, "lev", split_axis=0, concat_axis=0, tiled=True)
    d_result = (
        d_result.reshape(groups, rows, cols, dates, group_ch)
        .transpose(1, 2, 3, 0, 4)
        .reshape(pixels, slots)
    )

    hidden, lowered, conv_out, local = hidden_conv(edges, x_pad, w_slots, b_in, depth, tile)
    total = butterfly(local, stages)
    wet = jnp.broadcast_to(
        wet_mask.astype(F32)[:, :, None, None], (rows, cols, dates, 1)
    ).reshape(pixels, 1)
    d_mixed = jnp.dot(d_result, w_out_slots.T, preferred_element_type=F32)
    d_sum = d_mixed * wet
    d_branch = d_sum.astype(BF16)
    g_b_two = jnp.sum(d_branch.astype(F32), axis=0)
    g_bias_slots = jnp.sum(d_result.astype(F32), axis=0)

    mean_value = total[0] / pixel_total
    inv_scale = lax.rsqrt(total[1] / pixel_total - mean_value * mean_value + 1e-05)
    conv_flat = conv_out.reshape(pixels, width)
    centered = (conv_flat - mean_value) * inv_scale
    normed = (centered * norm_gain + norm_bias).astype(BF16)
    activated, d_up, grads, g_b_one = mlp(normed, d_branch, w_one, b_one, w_two)

    ff = w_one.shape[1]
    cuts = [0, min(1280, ff), min(2560, ff), ff]
    reduced = []
    for order, low, high in zip(orders, cuts[:-1], cuts[1:]):
        blocks = grads[:, :, low:high].reshape(2 * width // SUBLANES, SUBLANES, high - low)
        pieces = reduce_blocks(blocks, order, BF16)
        reduced.append(jnp.concatenate(pieces, axis=0).reshape(2, width, high - low))
    grad_w_one = jnp.concatenate([r[0] for r in reduced], axis=1).astype(F32)
    grad_w_two = jnp.concatenate([r[1].T for r in reduced], axis=0).astype(F32)

    d_normed = lax.dot_general(
        d_up, w_one, (((1,), (1,)), ((), ())), preferred_element_type=F32
    )
    parts = jnp.stack([jnp.sum(d_normed, axis=0), jnp.sum(d_normed * centered, axis=0)])
    norm_grads = butterfly(parts, stages)
    branch = jnp.dot(activated, w_two, preferred_element_type=F32) + b_two
    mixed = ((hidden.reshape(pixels, width) + branch) * wet).astype(BF16)
    result = (jnp.dot(mixed, w_out_slots, preferred_element_type=F32) + b_slots).astype(BF16)
    result = result.reshape(rows, cols, dates, groups, group_ch).transpose(3, 0, 1, 2, 4)
    result = result.reshape(groups, rows, cols, dates * group_ch)
    next_state = lax.all_to_all(result, "lev", split_axis=0, concat_axis=0, tiled=True)
    next_state = next_state.reshape(all_rows, cols, dates, group_ch).transpose(0, 2, 1, 3)
    g_out_slots = lax.dot_general(
        d_result, mixed, (((0,), (0,)), ((), ())), preferred_element_type=F32
    )

    scale = norm_gain * inv_scale
    slope = scale * inv_scale * (norm_grads[1] / pixel_total)
    coef = jnp.stack(
        [scale, -slope, slope * mean_value - scale * (norm_grads[0] / pixel_total)]
    )
    shape4 = (rows, cols, dates, width)
    d_hidden, g_w_depth, g_b_in = conv_back(
        edges, coef, d_normed.reshape(shape4), conv_out, d_sum.reshape(shape4), lowered, depth, tile
    )
    d_state = lax.dot_general(
        d_hidden, w_slots, (((1,), (1,)), ((), ())), preferred_element_type=F32
    ).reshape(high_rows, wide_cols, dates, slots)
    g_in_slots = lax.dot_general(
        x_pad, d_hidden, (((0,), (0,)), ((), ())), preferred_element_type=F32
    )
    to_low = lax.ppermute(d_state[:, :half].astype(BF16), "sp", backward)
    to_high = lax.ppermute(d_state[:, half + cols :].astype(BF16), "sp", forward)
    d_state = d_state[:, half : half + cols]
    d_state = d_state + jnp.pad(
        to_low.astype(F32), ((0, 0), (cols - half, 0), (0, 0), (0, 0))
    )
    d_state = d_state + jnp.pad(
        to_high.astype(F32), ((0, 0), (0, cols - half), (0, 0), (0, 0))
    )
    d_state = (
        d_state.astype(BF16)
        .reshape(high_rows, cols, dates, groups, group_ch)
        .transpose(3, 0, 1, 2, 4)
        .reshape(groups, high_rows, cols, dates * group_ch)
    )
    d_state = lax.all_to_all(d_state, "lev", split_axis=0, concat_axis=0, tiled=True).astype(F32)
    inner = d_state[:, half : half + rows]
    inner = inner + jnp.pad(
        d_state[:-1, half + rows :], ((1, 0), (0, rows - half), (0, 0), (0, 0))
    )
    inner = inner + jnp.pad(d_state[1:, :half], ((0, 1), (rows - half, 0), (0, 0), (0, 0)))
    grad_ocean_state = (
        inner.astype(BF16).reshape(all_rows, cols, dates, group_ch).transpose(0, 2, 1, 3)
    )

    def as_rows(vector):
        flat = vector.reshape(-1)
        count = -(-flat.shape[0] // width)
        return jnp.pad(flat, (0, count * width - flat.shape[0])).reshape(count, width)

    def summed(arrays, order):
        packed = jnp.concatenate(arrays, axis=0)
        count = packed.shape[0]
        unit = 16 * SUBLANES
        packed = jnp.pad(packed, ((0, -count % unit), (0, 0)))
        pieces = reduce_blocks(packed.reshape(-1, SUBLANES, width), order, F32)
        packed = jnp.concatenate(pieces, axis=0).reshape(-1, width)
        found = []
        start = 0
        for array in arrays:
            found.append(packed[start : start + array.shape[0]])
            start += array.shape[0]
        return found

    early = summed(
        [g_out_slots, as_rows(g_b_one), as_rows(g_b_two), as_rows(g_bias_slots)], orders[0]
    )
    late = summed([g_in_slots, g_w_depth, g_b_in], orders[0])
    grad_w_out = jnp.einsum("sd,sc->dc", early[0], table, precision=exact_mode)
    grad_b_one = early[1].reshape(-1)[:ff]
    grad_b_two = early[2].reshape(-1)
    grad_b_out = jnp.dot(early[3].reshape(-1)[:slots], table, precision=exact_mode)
    grad_w_in = jnp.dot(table.T, late[0], precision=exact_mode)
    grad_w_depth = late[1].reshape(kernel, kernel, width)
    grad_b_in = late[2].reshape(-1)
    return (
        next_state,
        grad_ocean_state,
        grad_w_in,
        grad_b_in,
        grad_w_depth,
        norm_grads[1],
        norm_grads[0],
        grad_w_one,
        grad_b_one,
        grad_w_two,
        grad_b_two,
        grad_w_out,
        grad_b_out,
    )


def solution(mesh):
    return jax.shard_map(
        on_device,
        mesh=mesh,
        in_specs=(
            P(None, None, "sp", "lev"),
            P(),
            P("lev", "sp"),
            P(),
            P(),
            P(),
            P(),
            P(),
            P(),
            P(),
            P(),
            P(),
            P(),
            P(),
            P(None, None, "sp", "lev"),
        ),
        out_specs=(
            P(None, None, "sp", "lev"),
            P(None, None, "sp", "lev"),
            P(),
            P(),
            P(),
            P(),
            P(),
            P(),
            P(),
            P(),
            P(),
            P(),
            P(),
        ),
        check_vma=False,
    )
```

time: 1070 us -> 540 us (0.50)
  blocking collectives: 203 us -> 0 us
  waiting for transfers between devices: 370 us -> 170 us
  other arithmetic: 188 us -> 48.5 us
  Pallas kernels: 0 us -> 97.1 us
  matrix products: 124 us -> 34.4 us
  starting transfers between devices: 41.2 us -> 85.7 us
  local copies, waits for them, and re-layouts: 123 us -> 96.5 us
  between operations: 18.7 us -> 2.6 us
    psum x2 -> x0, waiting for transfers between devices: 244 us -> none  [the longest x1 244 us: on_device(): lax.psum((g_w_one, g_w_two, g_w_depth, g_b_one, g_b_two, g_b_in), ('lev',...]
    reduce_sum x8 -> x2, other arithmetic: 164 us -> 5.24 us  [the longest x1 3.7 us: on_device(): jnp.sum(d_normed * centered, axis=0)]
    ppermute x8 -> x58, waiting for transfers between devices: 12.6 us -> 157 us  [the longest x54 150 us: hop(): lax.ppermute(value, axis, [(i, i ^ bit) for i in range(lax.axis_size(axis...]
    psum x4 -> x0, blocking collectives: 141 us -> none  [the longest x1 41.5 us: on_device(): total_sum, total_square = lax.psum((local_sum, local_square), ('lev', 'sp'))]
    reduce_scatter x1 -> x0, waiting for transfers between devices: 113 us -> none  [on_device(): lax.psum_scatter(jnp.einsum('abcs,sd->abcd', ocean_state, own_rows, prefe...]
    pallas_call x0 -> x3, Pallas kernels: none -> 97.1 us  [the longest x1 43.1 us: mlp(): pl.pallas_call(functools.partial(mlp_body, row_block), grid=(pl.cdiv(hidd...]
    dot_general x17 -> x12, matrix products: 124 us -> 34.2 us  [the longest x1 10.2 us: on_device(): branch = jnp.dot(activated, w_two, preferred_element_type=F32) + b_two]
    ppermute x8 -> x58, starting transfers between devices: 21.4 us -> 70.7 us  [the longest x54 58.7 us: hop(): lax.ppermute(value, axis, [(i, i ^ bit) for i in range(lax.axis_size(axis...]
  transfers between devices with their start and end apart: 17 -> 62, of which waited for: 3 -> 31; matrix products, arithmetic and copies ran while one was open for 14% -> 23% of each run, Pallas kernels for 0% -> 10%
where the time goes in v1:
time: 540 us; the launch traced here: 535 us
  waiting for transfers between devices  170 us (31%)
  Pallas kernels  97.1 us (18%)
  local copies, waits for them, and re-layouts  96.5 us (18%)
  starting transfers between devices  85.7 us (16%)
  other arithmetic  48.5 us (9%)
  matrix products  34.4 us (6%)
    ppermute x54, waiting for transfers between devices, hop(): lax.ppermute(value, axis, [(i, i ^ bit) for i in range(lax.axis_size(axis...  150 us
    ppermute x54, starting transfers between devices, hop(): lax.ppermute(value, axis, [(i, i ^ bit) for i in range(lax.axis_size(axis...  58.7 us
    pallas_call x1, Pallas kernels, mlp(): pl.pallas_call(functools.partial(mlp_body, row_block), grid=(pl.cdiv(hidd...  43.1 us
    pallas_call x1, Pallas kernels, conv_back(): pl.pallas_call(functools.partial(conv_back_body, rows, cols, half), grid=...  31.4 us
    pallas_call x1, Pallas kernels, hidden_conv(): pl.pallas_call(functools.partial(hidden_conv_body, rows, cols, half), gri...  22.6 us
    unnamed x166, local copies, waits for them, and re-layouts  19 us
    all_to_all x1, waiting for transfers between devices, on_device(): lax.all_to_all(windows, 'lev', split_axis=0, concat_axis=0, tiled=True)  13.3 us
    concatenate x15, other arithmetic, reduce_blocks(): value = jnp.concatenate([value, hop(value, stage)], axis=0)  10.9 us
  transfers between devices with their start and end apart: 62, of which 31 were waited for; matrix products, arithmetic and copies ran while one was open for 23% of the time, Pallas kernels for 10%

profile of v1, /device:TPU:0, one launch (start us, length us, event | category | flops | bytes accessed | tf_op | source)
XLA Modules:
  0.0 535.3 jit_solution(10930999915108125306)
XLA Ops:
  3.0 4.9 collective-permute-start
  25.0 13.3 %all-to-all-done = bf16[4,14,22,400]{3,2,1,0:T(8,128)(2,1)S(1)} async-done(((bf16[4,14,22,400]{3,2,1,0:T(8,128)(2,1)}), bf16[4,14,22,400]{3,2,1,0:T(8,128)(2,1)S(1)}, u32[]{:S(2)}, u32[]{:S(2)}) %all-to-all-start) | async-done | bytes 985632 | tf_op jit(solution)/shard_map/all_to_all | solution.py:379
  53.9 4.4 reshape.187.x_ref
  58.3 22.6 %hidden_conv.1 = (f32[8,16,8,800]{3,2,1,0:T(8,128)}, bf16[2464,800]{1,0:T(8,128)(2,1)}, f32[8,16,8,800]{3,2,1,0:T(8,128)}, f32[2,800]{1,0:T(2,128)}) custom-call(s32[4]{0:T(128)} %add_convert_fusion.10.edge_ref, bf16[2464,200]{1,0:T(8,128)(2,1)} %reshape.187.x_ref, bf16[200,800]{1,0:T(8,128)(2,1)} %convolution_convert_fusion.1.w_ref, ...), custom_call_target="tpu_custom_call" | custom-call | tf_op jit(solution)/shard_map/hidden_conv/pallas_call | solution.py:133
  89.8 8.6 %copy.56.w_two_ref = bf16[3200,800]{1,0:T(8,128)(2,1)} copy(bf16[3200,800]{0,1:T(8,128)(2,1)} %param.25) | data formatting | bytes 10240000 | tf_op args[10]
  109.4 5.3 copy.57
  118.6 43.1 %mlp.1 = (bf16[1024,3200]{1,0:T(8,128)(2,1)}, bf16[1024,3200]{1,0:T(8,128)(2,1)}, bf16[2,800,3200]{2,1,0:T(8,128)(2,1)}, f32[1,3200]{1,0:T(1,128)}) custom-call(bf16[1024,800]{1,0:T(8,128)(2,1)} %add_convert_fusion.normed_ref, bf16[1024,800]{1,0:T(8,128)(2,1)} %get-tuple-element.69.branch_ref, bf16[800,3200]{1,0:T(8,128)(2,1)} %w_one_ref.1, ...), custom_call_target="tpu_custom_call" | custom-call | tf_op jit(solution)/shard_map/mlp/pallas_call | solution.py:198
  162.6 10.2 %multiply_convert_fusion = bf16[1024,800]{0,1:T(8,128)(2,1)S(1)} fusion(f32[1024,800]{0,1:T(8,128)} %copy.57, bf16[1024,3200]{1,0:T(8,128)(2,1)} %get-tuple-element.27, bf16[3200,800]{0,1:T(8,128)(2,1)} %param.25, f32[1024]{0:T(1024)S(1)} %broadcast_in_dim.8, f32[800]{0:T(1024)S(1)} %copy-done.37), kind=kOutput, calls=%fused_computation.12 | convolution fusion | flops 5246156800 | bytes 16596096 | tf_op jit(solution)/shard_map/dot_general | solution.py:426
  174.3 4.5 fusion.32
  181.1 7.4 %fusion.36 = (f32[800]{0:T(1024)S(1)}, f32[1024,800]{0,1:T(8,128)}) fusion(bf16[1024,3200]{1,0:T(8,128)(2,1)S(1)} %bitcast.148, bf16[800,3200]{1,0:T(8,128)(2,1)S(1)} %bitcast.134), kind=kOutput, calls=%fused_computation.372 | convolution fusion | flops 5243698176 | bytes 14953600 | tf_op jit(solution)/shard_map/dot_general | solution.py:421
  188.5 5.0 copy.60
  228.1 31.4 %conv_back.1 = (bf16[2464,800]{1,0:T(8,128)(2,1)}, f32[49,800]{1,0:T(8,128)}, f32[1,800]{1,0:T(1,128)}) custom-call(s32[4]{0:T(128)} %add_convert_fusion.10.edge_ref, f32[3,800]{1,0:T(4,128)} %pad_maximum_fusion.17.coef_ref, f32[8,16,8,800]{3,2,1,0:T(8,128)} %bitcast.119, f32[8,16,8,800]{3,2,1,0:T(8,128)} %get-tuple-element.25.conv_ref, ...), custom_call_target="tpu_custom_call" | custom-call | tf_op jit(solution)/shard_map/conv_back/pallas_call | solution.py:287
  266.6 4.6 collective-permute-start.13
  297.1 8.7 %collective-permute-done.49 = f32[8,8,800]{2,1,0:T(8,128)S(1)} collective-permute-done((f32[8,8,800]{2,1,0:T(8,128)S(1)}, f32[8,8,800]{2,1,0:T(8,128)S(1)}, u32[]{:S(2)}, u32[]{:S(2)}) %collective-permute-start.49) | collective-permute-done | bytes 204832 | tf_op jit(solution)/shard_map/ppermute | solution.py:45
  367.3 19.6 %collective-permute-done.25 = bf16[50,8,1280]{2,1,0:T(8,128)(2,1)S(1)} collective-permute-done((bf16[50,8,1280]{2,1,0:T(8,128)(2,1)S(1)}, bf16[50,8,1280]{2,1,0:T(8,128)(2,1)S(1)}, u32[]{:S(2)}, u32[]{:S(2)}) %collective-permute-start.25) | collective-permute-done | bytes 1024032 | tf_op jit(solution)/shard_map/ppermute | solution.py:45
  389.2 12.1 %collective-permute-done.26 = bf16[25,8,1280]{2,1,0:T(8,128)(2,1)S(1)} collective-permute-done((bf16[25,8,1280]{2,1,0:T(8,128)(2,1)S(1)}, bf16[25,8,1280]{2,1,0:T(8,128)(2,1)S(1)}, u32[]{:S(2)}, u32[]{:S(2)}) %collective-permute-start.26) | collective-permute-done | bytes 512032 | tf_op jit(solution)/shard_map/ppermute | solution.py:45
  403.9 9.8 %collective-permute-done.27 = bf16[25,8,1280]{2,1,0:T(8,128)(2,1)S(1)} collective-permute-done((bf16[25,8,1280]{2,1,0:T(8,128)(2,1)S(1)}, bf16[25,8,1280]{2,1,0:T(8,128)(2,1)S(1)}, u32[]{:S(2)}, u32[]{:S(2)}) %collective-permute-start.27) | collective-permute-done | bytes 512032 | tf_op jit(solution)/shard_map/ppermute | solution.py:45
  417.4 20.0 %collective-permute-done.28 = bf16[25,8,1280]{2,1,0:T(8,128)(2,1)S(1)} collective-permute-done((bf16[25,8,1280]{2,1,0:T(8,128)(2,1)S(1)}, bf16[25,8,1280]{2,1,0:T(8,128)(2,1)S(1)}, u32[]{:S(2)}, u32[]{:S(2)}) %collective-permute-start.28) | collective-permute-done | bytes 512032 | tf_op jit(solution)/shard_map/ppermute | solution.py:45
  442.6 8.5 %collective-permute-done.29 = bf16[25,8,1280]{2,1,0:T(8,128)(2,1)S(1)} collective-permute-done((bf16[25,8,1280]{2,1,0:T(8,128)(2,1)S(1)}, bf16[25,8,1280]{2,1,0:T(8,128)(2,1)S(1)}, u32[]{:S(2)}, u32[]{:S(2)}) %collective-permute-start.29) | collective-permute-done | bytes 512032 | tf_op jit(solution)/shard_map/ppermute | solution.py:45
  452.9 9.3 %collective-permute-done.44 = bf16[25,8,640]{2,1,0:T(8,128)(2,1)S(1)} collective-permute-done((bf16[25,8,640]{2,1,0:T(8,128)(2,1)S(1)}, bf16[25,8,640]{2,1,0:T(8,128)(2,1)S(1)}, u32[]{:S(2)}, u32[]{:S(2)}) %collective-permute-start.44) | collective-permute-done | bytes 256032 | tf_op jit(solution)/shard_map/ppermute | solution.py:45
  464.9 8.2 %collective-permute-done.36 = bf16[25,8,1280]{2,1,0:T(8,128)(2,1)S(1)} collective-permute-done((bf16[25,8,1280]{2,1,0:T(8,128)(2,1)S(1)}, bf16[25,8,1280]{2,1,0:T(8,128)(2,1)S(1)}, u32[]{:S(2)}, u32[]{:S(2)}) %collective-permute-start.36) | collective-permute-done | bytes 512032 | tf_op jit(solution)/shard_map/ppermute | solution.py:45
  475.8 6.4 %collective-permute-done.45 = bf16[25,8,640]{2,1,0:T(8,128)(2,1)S(1)} collective-permute-done((bf16[25,8,640]{2,1,0:T(8,128)(2,1)S(1)}, bf16[25,8,640]{2,1,0:T(8,128)(2,1)S(1)}, u32[]{:S(2)}, u32[]{:S(2)}) %collective-permute-start.45) | collective-permute-done | bytes 256032 | tf_op jit(solution)/shard_map/ppermute | solution.py:45
  484.7 6.8 %collective-permute-done.37 = bf16[25,8,1280]{2,1,0:T(8,128)(2,1)S(1)} collective-permute-done((bf16[25,8,1280]{2,1,0:T(8,128)(2,1)S(1)}, bf16[25,8,1280]{2,1,0:T(8,128)(2,1)S(1)}, u32[]{:S(2)}, u32[]{:S(2)}) %collective-permute-start.37) | collective-permute-done | bytes 512032 | tf_op jit(solution)/shard_map/ppermute | solution.py:45
  505.7 10.3 %collective-permute-done.38 = bf16[50,8,1280]{2,1,0:T(8,128)(2,1)} collective-permute-done((bf16[50,8,1280]{2,1,0:T(8,128)(2,1)}, bf16[50,8,1280]{2,1,0:T(8,128)(2,1)}, u32[]{:S(2)}, u32[]{:S(2)}) %collective-permute-start.38) | collective-permute-done | bytes 1024032 | tf_op jit(solution)/shard_map/ppermute | solution.py:45
  (440 shorter events, 247.4 us)
Async XLA Ops:
  16.7 21.6 %all-to-all-start = ((bf16[4,14,22,400]{3,2,1,0:T(8,128)(2,1)}), bf16[4,14,22,400]{3,2,1,0:T(8,128)(2,1)S(1)}, u32[]{:S(2)}, u32[]{:S(2)}) async-start(bf16[4,14,22,400]{3,2,1,0:T(8,128)(2,1)} %pad_maximum_fusion.5), calls=%async_computation | async-start | bytes 2752512 | tf_op jit(solution)/shard_map/all_to_all | solution.py:379
  38.3 60.1 %all-to-all-start.1 = ((bf16[4,8,16,400]{3,2,1,0:T(8,128)(2,1)}), bf16[4,8,16,400]{3,2,1,0:T(8,128)(2,1)S(1)}, u32[]{:S(2)}, u32[]{:S(2)}) async-start(bf16[4,8,16,400]{3,2,1,0:T(8,128)(2,1)} %reshape.193), calls=%async_computation.1 | async-start | bytes 1048576 | tf_op jit(solution)/shard_map/all_to_all | solution.py:386
  204.1 88.6 %collective-permute-start.48 = (f32[16,8,800]{2,1,0:T(8,128)}, f32[16,8,800]{2,1,0:T(8,128)}, u32[]{:S(2)}, u32[]{:S(2)}) collective-permute-start(f32[16,8,800]{2,1,0:T(8,128)} %constant_dynamic-slice_fusion.49), channel_id=1, source_target_pairs={{0,8},{8,0},{16,24},{24,16},{1,9},{9,1},{17,25},{25,17},{2,10},{10... | collective-permute-start | bytes 1228808 | tf_op jit(solution)/shard_map/ppermute | solution.py:45
  210.2 73.6 %all-to-all-start.2 = ((bf16[4,8,16,400]{3,2,1,0:T(8,128)(2,1)}), bf16[4,8,16,400]{3,2,1,0:T(8,128)(2,1)}, u32[]{:S(2)}, u32[]{:S(2)}) async-start(bf16[4,8,16,400]{3,2,1,0:T(8,128)(2,1)} %reshape.198), calls=%async_computation.2 | async-start | bytes 1048576 | tf_op jit(solution)/shard_map/all_to_all | solution.py:431
  216.7 129.7 %collective-permute-start.40 = (bf16[100,8,640]{2,1,0:T(8,128)(2,1)}, bf16[100,8,640]{2,1,0:T(8,128)(2,1)}, u32[]{:S(2)}, u32[]{:S(2)}) collective-permute-start(bf16[100,8,640]{2,1,0:T(8,128)(2,1)} %constant_dynamic-slice_fusion.54), channel_id=1, source_target_pairs={{0,8},{8,0},{16,24},{24,16},{1,9},{9,1},{17,25},{25,17},{2,10},{10... | collective-permute-start | bytes 3072008 | tf_op jit(solution)/shard_map/ppermute | solution.py:45
  224.6 136.0 %collective-permute-start.24 = (bf16[100,8,1280]{2,1,0:T(8,128)(2,1)}, bf16[100,8,1280]{2,1,0:T(8,128)(2,1)}, u32[]{:S(2)}, u32[]{:S(2)}) collective-permute-start(bf16[100,8,1280]{2,1,0:T(8,128)(2,1)} %constant_dynamic-slice_fusion.64), channel_id=1, source_target_pairs={{0,8},{8,0},{16,24},{24,16},{1,9},{9,1},{17,25},{25,17},{2,10},{10... | collective-permute-start | bytes 6144008 | tf_op jit(solution)/shard_map/ppermute | solution.py:45
  273.1 91.2 %collective-permute-start.32 = (bf16[100,8,1280]{2,1,0:T(8,128)(2,1)}, bf16[100,8,1280]{2,1,0:T(8,128)(2,1)}, u32[]{:S(2)}, u32[]{:S(2)}) collective-permute-start(bf16[100,8,1280]{2,1,0:T(8,128)(2,1)} %constant_dynamic-slice_fusion.59), channel_id=1, source_target_pairs={{0,8},{8,0},{16,24},{24,16},{1,9},{9,1},{17,25},{25,17},{2,10},{10... | collective-permute-start | bytes 6144008 | tf_op jit(solution)/shard_map/ppermute | solution.py:45
  274.7 21.1 %collective-permute-start.14 = (f32[16,8,800]{2,1,0:T(8,128)}, f32[16,8,800]{2,1,0:T(8,128)}, u32[]{:S(2)}, u32[]{:S(2)}) collective-permute-start(f32[16,8,800]{2,1,0:T(8,128)} %constant_dynamic-slice_fusion.102), channel_id=1, source_target_pairs={{0,8},{8,0},{16,24},{24,16},{1,9},{9,1},{17,25},{25,17},{2,10},{10... | collective-permute-start | bytes 1228808 | tf_op jit(solution)/shard_map/ppermute | solution.py:45
  283.8 29.7 %all-to-all-start.3 = ((bf16[4,14,16,400]{3,2,1,0:T(8,128)(2,1)}), bf16[4,14,16,400]{3,2,1,0:T(8,128)(2,1)S(1)}, u32[]{:S(2)}, u32[]{:S(2)}) async-start(bf16[4,14,16,400]{3,2,1,0:T(8,128)(2,1)} %reshape.204), calls=%async_computation.3 | async-start | bytes 1835008 | tf_op jit(solution)/shard_map/all_to_all | solution.py:467
  357.2 57.9 %collective-permute-start.42 = (bf16[25,8,640]{2,1,0:T(8,128)(2,1)S(1)}, bf16[25,8,640]{2,1,0:T(8,128)(2,1)S(1)}, u32[]{:S(2)}, u32[]{:S(2)}) collective-permute-start(bf16[25,8,640]{2,1,0:T(8,128)(2,1)S(1)} %dynamic-slice_convert_fusion.5), channel_id=1, source_target_pairs={{0,16},{8,24},{16,0},{24,8},{1,17},{9,25},{17,1},{25,9},{2,18},{10... | collective-permute-start | bytes 768008 | tf_op jit(solution)/shard_map/ppermute | solution.py:45
  364.2 22.7 %collective-permute-start.25 = (bf16[50,8,1280]{2,1,0:T(8,128)(2,1)S(1)}, bf16[50,8,1280]{2,1,0:T(8,128)(2,1)S(1)}, u32[]{:S(2)}, u32[]{:S(2)}) collective-permute-start(bf16[50,8,1280]{2,1,0:T(8,128)(2,1)S(1)} %dynamic-slice_convert_fusion.1), channel_id=1, source_target_pairs={{0,16},{8,24},{16,0},{24,8},{1,17},{9,25},{17,1},{25,9},{2,18},{10... | collective-permute-start | bytes 3072008 | tf_op jit(solution)/shard_map/ppermute | solution.py:45
  366.8 36.0 %collective-permute-start.33 = (bf16[50,8,1280]{2,1,0:T(8,128)(2,1)S(1)}, bf16[50,8,1280]{2,1,0:T(8,128)(2,1)S(1)}, u32[]{:S(2)}, u32[]{:S(2)}) collective-permute-start(bf16[50,8,1280]{2,1,0:T(8,128)(2,1)S(1)} %dynamic-slice_convert_fusion), channel_id=1, source_target_pairs={{0,1},{1,0},{2,3},{3,2},{4,5},{5,4},{6,7},{7,6},{8,9},{9,8},{10,11... | collective-permute-start | bytes 3072008 | tf_op jit(solution)/shard_map/ppermute | solution.py:45
  413.9 23.5 %collective-permute-start.28 = (bf16[25,8,1280]{2,1,0:T(8,128)(2,1)S(1)}, bf16[25,8,1280]{2,1,0:T(8,128)(2,1)S(1)}, u32[]{:S(2)}, u32[]{:S(2)}) collective-permute-start(bf16[25,8,1280]{2,1,0:T(8,128)(2,1)S(1)} %add_convert_fusion.5), channel_id=1, source_target_pairs={{0,4},{1,5},{2,6},{3,7},{4,0},{5,1},{6,2},{7,3},{8,12},{9,13},{10,... | collective-permute-start | bytes 1536008 | tf_op jit(solution)/shard_map/ppermute | solution.py:45
  415.2 24.1 %collective-permute-start.43 = (bf16[25,8,640]{2,1,0:T(8,128)(2,1)S(1)}, bf16[25,8,640]{2,1,0:T(8,128)(2,1)S(1)}, u32[]{:S(2)}, u32[]{:S(2)}) collective-permute-start(bf16[25,8,640]{2,1,0:T(8,128)(2,1)S(1)} %add_convert_fusion.9), channel_id=1, source_target_pairs={{0,1},{1,0},{2,3},{3,2},{4,5},{5,4},{6,7},{7,6},{8,9},{9,8},{10,11... | collective-permute-start | bytes 768008 | tf_op jit(solution)/shard_map/ppermute | solution.py:45
  417.0 22.5 %collective-permute-start.35 = (bf16[25,8,1280]{2,1,0:T(8,128)(2,1)S(1)}, bf16[25,8,1280]{2,1,0:T(8,128)(2,1)S(1)}, u32[]{:S(2)}, u32[]{:S(2)}) collective-permute-start(bf16[25,8,1280]{2,1,0:T(8,128)(2,1)S(1)} %add_convert_fusion.3), channel_id=1, source_target_pairs={{0,2},{1,3},{2,0},{3,1},{4,6},{5,7},{6,4},{7,5},{8,10},{9,11},{10,... | collective-permute-start | bytes 1536008 | tf_op jit(solution)/shard_map/ppermute | solution.py:45
  439.4 22.9 %collective-permute-start.44 = (bf16[25,8,640]{2,1,0:T(8,128)(2,1)S(1)}, bf16[25,8,640]{2,1,0:T(8,128)(2,1)S(1)}, u32[]{:S(2)}, u32[]{:S(2)}) collective-permute-start(bf16[25,8,640]{2,1,0:T(8,128)(2,1)S(1)} %add_convert_fusion.8), channel_id=1, source_target_pairs={{0,4},{1,5},{2,6},{3,7},{4,0},{5,1},{6,2},{7,3},{8,12},{9,13},{10,... | collective-permute-start | bytes 768008 | tf_op jit(solution)/shard_map/ppermute | solution.py:45
  439.6 33.5 %collective-permute-start.36 = (bf16[25,8,1280]{2,1,0:T(8,128)(2,1)S(1)}, bf16[25,8,1280]{2,1,0:T(8,128)(2,1)S(1)}, u32[]{:S(2)}, u32[]{:S(2)}) collective-permute-start(bf16[25,8,1280]{2,1,0:T(8,128)(2,1)S(1)} %add_convert_fusion.2), channel_id=1, source_target_pairs={{0,4},{1,5},{2,6},{3,7},{4,0},{5,1},{6,2},{7,3},{8,12},{9,13},{10,... | collective-permute-start | bytes 1536008 | tf_op jit(solution)/shard_map/ppermute | solution.py:45
  451.2 31.9 %collective-permute-start.30 = (bf16[50,8,1280]{2,1,0:T(8,128)(2,1)S(1)}, bf16[50,8,1280]{2,1,0:T(8,128)(2,1)S(1)}, u32[]{:S(2)}, u32[]{:S(2)}) collective-permute-start(bf16[50,8,1280]{2,1,0:T(8,128)(2,1)S(1)} %pad_maximum_fusion.6), channel_id=1, source_target_pairs={{0,16},{8,24},{16,0},{24,8},{1,17},{9,25},{17,1},{25,9},{2,18},{10... | collective-permute-start | bytes 3072008 | tf_op jit(solution)/shard_map/ppermute | solution.py:45
  462.3 19.9 %collective-permute-start.45 = (bf16[25,8,640]{2,1,0:T(8,128)(2,1)S(1)}, bf16[25,8,640]{2,1,0:T(8,128)(2,1)S(1)}, u32[]{:S(2)}, u32[]{:S(2)}) collective-permute-start(bf16[25,8,640]{2,1,0:T(8,128)(2,1)S(1)} %add_convert_fusion.7), channel_id=1, source_target_pairs={{0,16},{8,24},{16,0},{24,8},{1,17},{9,25},{17,1},{25,9},{2,18},{10... | collective-permute-start | bytes 768008 | tf_op jit(solution)/shard_map/ppermute | solution.py:45
  473.3 18.3 %collective-permute-start.37 = (bf16[25,8,1280]{2,1,0:T(8,128)(2,1)S(1)}, bf16[25,8,1280]{2,1,0:T(8,128)(2,1)S(1)}, u32[]{:S(2)}, u32[]{:S(2)}) collective-permute-start(bf16[25,8,1280]{2,1,0:T(8,128)(2,1)S(1)} %add_convert_fusion.1), channel_id=1, source_target_pairs={{0,16},{8,24},{16,0},{24,8},{1,17},{9,25},{17,1},{25,9},{2,18},{10... | collective-permute-start | bytes 1536008 | tf_op jit(solution)/shard_map/ppermute | solution.py:45
  483.1 16.9 %collective-permute-start.46 = (bf16[50,8,640]{2,1,0:T(8,128)(2,1)}, bf16[50,8,640]{2,1,0:T(8,128)(2,1)}, u32[]{:S(2)}, u32[]{:S(2)}) collective-permute-start(bf16[50,8,640]{2,1,0:T(8,128)(2,1)} %pad_maximum_fusion.10), channel_id=1, source_target_pairs={{0,2},{1,3},{2,0},{3,1},{4,6},{5,7},{6,4},{7,5},{8,10},{9,11},{10,... | collective-permute-start | bytes 1536008 | tf_op jit(solution)/shard_map/ppermute | solution.py:45
  484.6 35.7 %collective-permute-start.31 = (bf16[100,8,1280]{2,1,0:T(8,128)(2,1)}, bf16[100,8,1280]{2,1,0:T(8,128)(2,1)}, u32[]{:S(2)}, u32[]{:S(2)}) collective-permute-start(bf16[100,8,1280]{2,1,0:T(8,128)(2,1)} %pad_maximum_fusion.2), channel_id=1, source_target_pairs={{0,8},{8,0},{16,24},{24,16},{1,9},{9,1},{17,25},{25,17},{2,10},{10... | collective-permute-start | bytes 6144008 | tf_op jit(solution)/shard_map/ppermute | solution.py:45
  492.6 23.4 %collective-permute-start.38 = (bf16[50,8,1280]{2,1,0:T(8,128)(2,1)}, bf16[50,8,1280]{2,1,0:T(8,128)(2,1)}, u32[]{:S(2)}, u32[]{:S(2)}) collective-permute-start(bf16[50,8,1280]{2,1,0:T(8,128)(2,1)} %pad_maximum_fusion.7), channel_id=1, source_target_pairs={{0,1},{1,0},{2,3},{3,2},{4,5},{5,4},{6,7},{7,6},{8,9},{9,8},{10,11... | collective-permute-start | bytes 3072008 | tf_op jit(solution)/shard_map/ppermute | solution.py:45
  501.2 16.3 %collective-permute-start.47 = (bf16[100,8,640]{2,1,0:T(8,128)(2,1)S(1)}, bf16[100,8,640]{2,1,0:T(8,128)(2,1)S(1)}, u32[]{:S(2)}, u32[]{:S(2)}) collective-permute-start(bf16[100,8,640]{2,1,0:T(8,128)(2,1)S(1)} %pad_maximum_fusion.8), channel_id=1, source_target_pairs={{0,8},{8,0},{16,24},{24,16},{1,9},{9,1},{17,25},{25,17},{2,10},{10... | collective-permute-start | bytes 3072008 | tf_op jit(solution)/shard_map/ppermute | solution.py:45
  (85 other events, 788.3 us)

commit v2 on v1

v2 whole, which is shorter than its diff:
```python
import functools

import jax
import jax.numpy as jnp
from jax import lax
from jax.experimental import pallas as pl
from jax.experimental.pallas import tpu as pltpu
from jax.sharding import PartitionSpec as P

VARS = 10
LANES = 128
SUBLANES = 8

exact_mode = lax.Precision.HIGHEST
F32 = jnp.float32
BF16 = jnp.bfloat16

TAIL_SCALE = 0.3
TAIL_POLY = (
    0.119623263,
    0.120845528,
    0.0993471402,
    0.130416391,
    -0.0571672287,
    0.210118226,
    -0.159378204,
    0.0361948279,
)


def slot_table(levels_of_slots, groups, group_ch, padded_ch, channels):
    slot_count = groups * group_ch
    kinds = jnp.arange(slot_count) % VARS
    target = jnp.repeat(levels_of_slots, VARS) * VARS + kinds
    target = jnp.pad(
        target.reshape(groups, group_ch), ((0, 0), (0, padded_ch - group_ch)), constant_values=-1
    ).reshape(-1)
    columns = jnp.arange(channels)
    return (target[:, None] == columns[None, :]).astype(F32)


def bits_of(axis):
    size = lax.axis_size(axis)
    return [(axis, 1 << k) for k in range(size.bit_length() - 1)]


def hop(value, stage):
    axis, bit = stage
    return lax.ppermute(value, axis, [(i, i ^ bit) for i in range(lax.axis_size(axis))])


def side(stage):
    axis, bit = stage
    return (lax.axis_index(axis) // bit) % 2


def butterfly(value, stages):
    for stage in stages:
        value = value + hop(value, stage)
    return value


def after(value, *earlier):
    return lax.optimization_barrier((value,) + earlier)[0]


def halves(value, axis, bit):
    half = value.shape[axis] // 2
    stay = lax.dynamic_slice_in_dim(value, bit * half, half, axis)
    sent = lax.dynamic_slice_in_dim(value, (1 - bit) * half, half, axis)
    return stay, sent


def halving_lanes(lanes):
    return lanes % (2 * LANES) == 0


def total(terms):
    value = terms[0].astype(F32)
    for term in terms[1:]:
        value = value + term.astype(F32)
    return value


def exchange(value, stages, link, partner=None, most=2):
    kept = []
    own = 0
    terms = [value]
    rest = stages
    if partner is not None:
        came = hop(partner, stages[0])
        token = yield partner
        terms.append(after(came, token))
        rest = stages[1:]
    row_halvings = 0
    for stage in rest:
        bit = side(stage)
        shape = terms[0].shape
        if stage is rest[-1]:
            axis = None
        elif shape[0] % 2 == 0 and row_halvings < most:
            axis = 0
            row_halvings += 1
            own = own * 2 + bit
        else:
            axis = 2 if halving_lanes(shape[2]) else None
        if axis is None:
            sent = total(terms).astype(link)
            terms = [sent]
        else:
            pairs = [halves(term, axis, bit) for term in terms]
            sent = total([pair[1] for pair in pairs]).astype(link)
            terms = [pair[0] for pair in pairs]
            kept.append((stage, axis))
        came = hop(sent, stage)
        token = yield sent
        terms.append(after(came, token))
    value = total(terms).astype(link)
    for stage, axis in reversed(kept):
        came = hop(value, stage)
        token = yield value
        came = after(came, token)
        if axis == 0:
            value = jnp.concatenate([value, came], axis=0)
        else:
            bit = side(stage)
            low = jnp.where(bit == 0, value, came)
            high = jnp.where(bit == 0, came, value)
            value = jnp.concatenate([low, high], axis=2)
    other = None
    if partner is not None:
        came = hop(value, stages[0])
        token = yield value
        other = after(came, token)
    yield value, other, own, 1 << row_halvings


def in_order(value, other, own, pieces):
    count = value.shape[0] // pieces
    return jnp.concatenate(
        [lax.dynamic_slice_in_dim(value, (index ^ own) * count, count, 0) for index in range(pieces)],
        axis=0,
    )


class Exchanges:
    def __init__(self):
        self.running = {}
        self.done = {}

    def begin(self, name, *args, **options):
        self.running[name] = exchange(*args, **options)
        return next(self.running[name])

    def step(self, token, *names):
        sent = []
        for name in names:
            if name in self.running:
                got = self.running[name].send(token)
                if isinstance(got, tuple):
                    self.done[name] = got
                    del self.running[name]
                else:
                    sent.append(got)
        return sent

    def finish(self, token, *names):
        while any(name in self.running for name in names):
            self.step(token, *names)


def unpack_grads(core_side, reduced, width, ff, start, prior=()):
    value, other, own, pieces = reduced
    count = value.shape[0] // pieces
    rows = count * SUBLANES
    columns = value.shape[2]

    def body(own_ref, value_ref, other_ref, *refs):
        out_one, out_two = refs[len(prior) :]
        mine = value_ref[...].astype(F32).reshape(rows, columns)
        theirs = other_ref[...].astype(F32).reshape(rows, columns)
        first = own_ref[1] == 0

        @pl.when(first)
        def _():
            out_one[...] = mine
            out_two[...] = theirs

        @pl.when(jnp.logical_not(first))
        def _():
            out_one[...] = theirs
            out_two[...] = mine

    out = pl.BlockSpec((pl.Element(rows), pl.Element(columns)), lambda i, own: (i * rows, start))
    piece = pl.BlockSpec((count, SUBLANES, columns), lambda i, own: (i ^ own[0], 0, 0))
    return pl.pallas_call(
        body,
        grid_spec=pltpu.PrefetchScalarGridSpec(
            num_scalar_prefetch=1,
            grid=(pieces,),
            in_specs=[piece, piece] + [pl.BlockSpec(memory_space=pl.ANY)] * len(prior),
            out_specs=[out, out],
        ),
        out_shape=[jax.ShapeDtypeStruct((width, ff), F32)] * 2,
        input_output_aliases={3 + k: k for k in range(len(prior))},
        name="unpack_grads",
    )(jnp.stack([own, core_side]).astype(jnp.int32), value, other, *prior)


def pixel_order(dates, cols):
    pixels = dates * cols
    source = lax.broadcasted_iota(jnp.int32, (pixels, pixels), 0)
    place = lax.broadcasted_iota(jnp.int32, (pixels, pixels), 1)
    return ((source % cols) * dates + source // cols == place).astype(BF16)


def to_channel_rows(state, cotangent, groups, half, padded_ch):
    all_rows, dates, cols, ch = state.shape
    rows = all_rows // groups
    high = rows + 2 * half
    pixels = dates * cols

    def body(state_ref, cot_ref, window_ref, ct_ref):
        perm = pixel_order(dates, cols)
        blank = jnp.zeros((padded_ch - ch, pixels), F32)
        zero = jnp.zeros((padded_ch, pixels), BF16)

        def turned(ref, row):
            value = lax.dot_general(
                ref[row].reshape(pixels, ch), perm, (((0,), (0,)), ((), ())), preferred_element_type=F32
            )
            return jnp.concatenate([value, blank], axis=0).astype(BF16) if padded_ch > ch else value.astype(BF16)

        for row in range(half):
            window_ref[0, row] = zero
            window_ref[groups - 1, half + rows + row] = zero
        for row in range(all_rows):
            value = turned(state_ref, row)
            for band in range(groups):
                place = row - band * rows + half
                if 0 <= place < high:
                    window_ref[band, place] = value
            ct_ref[row // rows, row % rows] = turned(cot_ref, row)

    return pl.pallas_call(
        body,
        out_shape=[
            jax.ShapeDtypeStruct((groups, high, padded_ch, pixels), BF16),
            jax.ShapeDtypeStruct((groups, rows, padded_ch, pixels), BF16),
        ],
        name="to_channel_rows",
    )(state, cotangent)


def from_channel_rows(windows, half, dates, cols, ch):
    groups, high, padded_ch, pixels = windows.shape
    rows = high - 2 * half

    def body(window_ref, out_ref):
        perm = pixel_order(dates, cols)
        for row in range(groups * rows):
            value = None
            for band in range(groups):
                place = row - band * rows + half
                if 0 <= place < high:
                    piece = window_ref[band, place]
                    value = piece if value is None else value.astype(F32) + piece.astype(F32)
            value = lax.dot_general(
                perm, value.astype(BF16), (((1,), (1,)), ((), ())), preferred_element_type=F32
            )
            out_ref[row] = value[:, :ch].astype(BF16).reshape(dates, cols, ch)

    return pl.pallas_call(
        body,
        out_shape=jax.ShapeDtypeStruct((groups * rows, dates, cols, ch), BF16),
        name="from_channel_rows",
    )(windows)


def to_pixel_rows(received):
    groups, rows, padded_ch, pixels = received.shape
    slots = groups * padded_ch

    def body(in_ref, out_ref):
        for row in range(rows):
            value = jnp.concatenate([in_ref[g, row].astype(F32) for g in range(groups)], axis=0)
            out_ref[row] = value.T.astype(BF16)

    return pl.pallas_call(
        body,
        out_shape=jax.ShapeDtypeStruct((rows, pixels, slots), BF16),
        name="to_pixel_rows",
    )(received)


def hidden_conv_body(rows, cols, half, edge_ref, x_ref, low_x_ref, high_x_ref, w_ref, b_ref, depth_ref, hidden_ref, low_ref, conv_ref, stat_ref, pad_ref):
    kernel = 2 * half + 1
    high = rows + 2 * half

    def hidden_of(ref, columns):
        value = jnp.dot(ref[...], w_ref[...], preferred_element_type=F32) + b_ref[...]
        return value.reshape(high, columns, SUBLANES, LANES)

    value = hidden_of(x_ref, cols)
    hidden_ref[...] = value[half : half + rows]
    pad_ref[:, half : half + cols] = value.astype(BF16).astype(F32)
    pad_ref[:, :half] = hidden_of(low_x_ref, half).astype(BF16).astype(F32)
    pad_ref[:, half + cols :] = hidden_of(high_x_ref, half).astype(BF16).astype(F32)

    @pl.when(edge_ref[0] == 1)
    def _():
        pad_ref[:half] = jnp.zeros((half,) + pad_ref.shape[1:], F32)

    @pl.when(edge_ref[1] == 1)
    def _():
        pad_ref[half + rows :] = jnp.zeros((half,) + pad_ref.shape[1:], F32)

    @pl.when(edge_ref[2] == 1)
    def _():
        pad_ref[:, :half] = jnp.zeros((pad_ref.shape[0], half) + pad_ref.shape[2:], F32)

    @pl.when(edge_ref[3] == 1)
    def _():
        pad_ref[:, half + cols :] = jnp.zeros((pad_ref.shape[0], half) + pad_ref.shape[2:], F32)

    low_ref[...] = pad_ref[...].reshape(low_ref.shape).astype(BF16)

    def one_row(row, carry):
        total, square = carry
        acc = jnp.zeros((cols, SUBLANES, LANES), F32)
        for i in range(kernel):
            slab = pad_ref[row + i]
            for j in range(kernel):
                acc = acc + slab[j : j + cols] * depth_ref[i * kernel + j]
        conv_ref[row] = acc
        return total + jnp.sum(acc, axis=0), square + jnp.sum(acc * acc, axis=0)

    zero = jnp.zeros((SUBLANES, LANES), F32)
    total, square = lax.fori_loop(0, rows, one_row, (zero, zero))
    stat_ref[0:1] = jnp.sum(total, axis=0, keepdims=True)
    stat_ref[1:2] = jnp.sum(square, axis=0, keepdims=True)


def hidden_conv(edges, x, low_x, high_x, w_slots, b_in, depth, tile):
    rows, cols, dates, half = tile
    slots, width = w_slots.shape
    padded = (rows + 2 * half) * (cols + 2 * half) * dates
    return pl.pallas_call(
        functools.partial(hidden_conv_body, rows, cols, half),
        grid=(pl.cdiv(width, LANES),),
        in_specs=[
            pl.BlockSpec(memory_space=pltpu.SMEM),
            pl.BlockSpec(x.shape, lambda i: (0, 0)),
            pl.BlockSpec(low_x.shape, lambda i: (0, 0)),
            pl.BlockSpec(high_x.shape, lambda i: (0, 0)),
            pl.BlockSpec((slots, LANES), lambda i: (0, i)),
            pl.BlockSpec((1, LANES), lambda i: (0, i)),
            pl.BlockSpec((depth.shape[0], 1, LANES), lambda i: (0, 0, i)),
        ],
        out_specs=[
            pl.BlockSpec((rows, cols, dates, LANES), lambda i: (0, 0, 0, i)),
            pl.BlockSpec((padded, LANES), lambda i: (0, i)),
            pl.BlockSpec((rows, cols, dates, LANES), lambda i: (0, 0, 0, i)),
            pl.BlockSpec((2, LANES), lambda i: (0, i)),
        ],
        out_shape=[
            jax.ShapeDtypeStruct((rows, cols, dates, width), F32),
            jax.ShapeDtypeStruct((padded, width), BF16),
            jax.ShapeDtypeStruct((rows, cols, dates, width), F32),
            jax.ShapeDtypeStruct((2, width), F32),
        ],
        scratch_shapes=[pltpu.VMEM((rows + 2 * half, cols + 2 * half, dates, LANES), F32)],
        cost_estimate=pl.CostEstimate(
            flops=20000000000, transcendentals=0, bytes_accessed=20 * padded * width
        ),
        name="hidden_conv",
    )(edges, x, low_x, high_x, w_slots, b_in.reshape(1, -1), depth)


def gelu_pair(values):
    size = jnp.abs(values)
    gauss = jnp.exp(-0.5 * values * values)
    t = 1.0 / (1.0 + TAIL_SCALE * size)
    poly = jnp.full_like(t, TAIL_POLY[-1])
    for factor in TAIL_POLY[-2::-1]:
        poly = poly * t + factor
    tail = gauss * (t * poly)
    below = jnp.where(values >= 0, 1.0 - tail, tail)
    return values * below, below + values * (gauss * 0.3989422804014327)


def mlp_body(row_block, core_ref, normed_ref, branch_ref, w_one_ref, b_one_ref, w_two_ref, act_ref, dup_ref, keep_ref, send_ref, gb_ref, normed_t, branch_t):
    @pl.when(pl.program_id(0) == 0)
    def _():
        normed_t[...] = normed_ref[...].T
        branch_t[...] = branch_ref[...].T

    total = jnp.zeros((1, act_ref.shape[1]), F32)
    for start in range(0, normed_ref.shape[0], row_block):
        rows = pl.ds(start, row_block)
        up = jnp.dot(normed_ref[rows], w_one_ref[...], preferred_element_type=F32) + b_one_ref[...]
        d_act = jnp.dot(branch_ref[rows], w_two_ref[...], preferred_element_type=F32)
        value, slope = gelu_pair(up)
        act_ref[rows] = value.astype(BF16)
        d_up = (slope * d_act).astype(BF16)
        dup_ref[rows] = d_up
        total = total + jnp.sum(d_up.astype(F32), axis=0, keepdims=True)
    gb_ref[...] = total
    grad_one = jnp.dot(normed_t[...], dup_ref[...], preferred_element_type=F32).astype(BF16)
    grad_two = jnp.dot(branch_t[...], act_ref[...], preferred_element_type=F32).astype(BF16)
    first = core_ref[0] == 0

    @pl.when(first)
    def _():
        keep_ref[...] = grad_one
        send_ref[...] = grad_two

    @pl.when(jnp.logical_not(first))
    def _():
        keep_ref[...] = grad_two
        send_ref[...] = grad_one


def mlp(core_side, normed, d_branch, w_one, b_one, w_two, first, last, prior=(), block=256, row_block=256):
    pixels, width = normed.shape
    hidden = w_one.shape[1]
    start = first // block

    def body(core_ref, normed_ref, branch_ref, w_one_ref, b_one_ref, w_two_ref, *refs):
        mlp_body(row_block, core_ref, normed_ref, branch_ref, w_one_ref, b_one_ref, w_two_ref, *refs[len(prior) :])

    whole = jax.ShapeDtypeStruct((pixels, hidden), BF16)
    grad = jax.ShapeDtypeStruct((width, last - first), BF16)
    results = pl.pallas_call(
        body,
        grid=(pl.cdiv(last - first, block),),
        in_specs=[
            pl.BlockSpec(memory_space=pltpu.SMEM),
            pl.BlockSpec((pixels, width), lambda i: (0, 0)),
            pl.BlockSpec((pixels, width), lambda i: (0, 0)),
            pl.BlockSpec((width, block), lambda i: (0, start + i)),
            pl.BlockSpec((1, block), lambda i: (0, start + i)),
            pl.BlockSpec((width, block), lambda i: (0, start + i)),
        ]
        + [pl.BlockSpec(memory_space=pl.ANY)] * len(prior),
        out_specs=[
            pl.BlockSpec((pixels, block), lambda i: (0, start + i)),
            pl.BlockSpec((pixels, block), lambda i: (0, start + i)),
            pl.BlockSpec((width, block), lambda i: (0, i)),
            pl.BlockSpec((width, block), lambda i: (0, i)),
            pl.BlockSpec((1, block), lambda i: (0, start + i)),
        ],
        out_shape=[whole, whole, grad, grad, jax.ShapeDtypeStruct((1, hidden), F32)],
        scratch_shapes=[pltpu.VMEM((width, pixels), BF16), pltpu.VMEM((width, pixels), BF16)],
        input_output_aliases={6 + n: k for n, k in enumerate((0, 1, 4)[: len(prior)])},
        cost_estimate=pl.CostEstimate(
            flops=8 * pixels * width * (last - first),
            transcendentals=2 * pixels * (last - first),
            bytes_accessed=4 * pixels * width + 8 * width * (last - first) + 4 * pixels * (last - first),
        ),
        name="mlp",
    )(core_side.reshape(1).astype(jnp.int32), normed, d_branch, w_one, b_one.reshape(1, -1), w_two, *prior)
    activated, d_up, keep, send, bias = results
    blocks = (width // SUBLANES, SUBLANES, last - first)
    return (activated, d_up, bias), (keep.reshape(blocks), send.reshape(blocks))


def norm_back_body(dup_ref, w_ref, conv_ref, norm_ref, dn_ref, part_ref):
    value = lax.dot_general(
        dup_ref[...], w_ref[...], (((1,), (1,)), ((), ())), preferred_element_type=F32
    )
    dn_ref[...] = value
    centered = (conv_ref[...] - norm_ref[0:1]) * norm_ref[1:2]

    @pl.when(pl.program_id(0) == 0)
    def _():
        part_ref[...] = jnp.zeros(part_ref.shape, F32)

    part_ref[0:1] += jnp.sum(value, axis=0, keepdims=True)
    part_ref[1:2] += jnp.sum(value * centered, axis=0, keepdims=True)


def norm_back(d_up, w_one, conv_flat, norm, row_block=256):
    pixels, hidden = d_up.shape
    width = w_one.shape[0]
    return pl.pallas_call(
        norm_back_body,
        grid=(pixels // row_block,),
        in_specs=[
            pl.BlockSpec((row_block, hidden), lambda i: (i, 0)),
            pl.BlockSpec((width, hidden), lambda i: (0, 0)),
            pl.BlockSpec((row_block, width), lambda i: (i, 0)),
            pl.BlockSpec((2, width), lambda i: (0, 0)),
        ],
        out_specs=[
            pl.BlockSpec((row_block, width), lambda i: (i, 0)),
            pl.BlockSpec((2, width), lambda i: (0, 0)),
        ],
        out_shape=[
            jax.ShapeDtypeStruct((pixels, width), F32),
            jax.ShapeDtypeStruct((2, width), F32),
        ],
        cost_estimate=pl.CostEstimate(
            flops=2 * pixels * width * hidden,
            transcendentals=0,
            bytes_accessed=2 * (pixels + width) * hidden + 8 * pixels * width,
        ),
        name="norm_back",
    )(d_up, w_one, conv_flat, norm)


def branch_out_body(act_ref, w_ref, b_ref, hidden_ref, wet_ref, w_out_ref, b_out_ref, dres_ref, result_ref, gout_ref):
    branch = b_ref[...] + lax.dot_general(
        act_ref[...], w_ref[...], (((1,), (1,)), ((), ())), preferred_element_type=F32
    )
    mixed = ((hidden_ref[...] + branch) * wet_ref[...]).astype(BF16)
    result = jnp.dot(mixed, w_out_ref[...], preferred_element_type=F32) + b_out_ref[...]
    result = result.T
    groups, count, padded_ch, lanes = result_ref.shape
    for row in range(count):
        for g in range(groups):
            piece = result[g * padded_ch : (g + 1) * padded_ch, row * lanes : (row + 1) * lanes]
            result_ref[g, row] = piece.astype(BF16)

    @pl.when(pl.program_id(0) == 0)
    def _():
        gout_ref[...] = jnp.zeros(gout_ref.shape, F32)

    gout_ref[...] += lax.dot_general(
        dres_ref[...], mixed, (((0,), (0,)), ((), ())), preferred_element_type=F32
    )


def branch_out(activated, w_two, b_two, hidden, wet, w_out_slots, b_slots, d_result, out_shape, row_block=256):
    pixels, inner = activated.shape
    width, slots = w_out_slots.shape
    return pl.pallas_call(
        branch_out_body,
        grid=(pixels // row_block,),
        in_specs=[
            pl.BlockSpec((row_block, inner), lambda i: (i, 0)),
            pl.BlockSpec((width, inner), lambda i: (0, 0)),
            pl.BlockSpec((1, width), lambda i: (0, 0)),
            pl.BlockSpec((row_block, width), lambda i: (i, 0)),
            pl.BlockSpec((row_block, 1), lambda i: (i, 0)),
            pl.BlockSpec((width, slots), lambda i: (0, 0)),
            pl.BlockSpec((1, slots), lambda i: (0, 0)),
            pl.BlockSpec((row_block, slots), lambda i: (i, 0)),
        ],
        out_specs=[
            pl.BlockSpec(
                (out_shape[0], row_block // out_shape[3]) + out_shape[2:], lambda i: (0, i, 0, 0)
            ),
            pl.BlockSpec((slots, width), lambda i: (0, 0)),
        ],
        out_shape=[
            jax.ShapeDtypeStruct(out_shape, BF16),
            jax.ShapeDtypeStruct((slots, width), F32),
        ],
        cost_estimate=pl.CostEstimate(
            flops=2 * pixels * width * (inner + 2 * slots),
            transcendentals=0,
            bytes_accessed=2 * (pixels + width) * inner + 4 * pixels * width,
        ),
        name="branch_out",
    )(activated, w_two, b_two.reshape(1, -1), hidden, wet, w_out_slots, b_slots.reshape(1, -1), d_result)


def conv_back_body(rows, cols, half, edge_ref, coef_ref, dn_ref, conv_ref, dsum_ref, low_ref, depth_ref, dh_ref, dh_low_ref, dh_high_ref, gw_ref, gb_ref, dc_ref, dl_ref, pad_ref, tap_ref):
    kernel = 2 * half + 1
    wide = cols + 2 * half
    d_conv = coef_ref[0:1] * dn_ref[...] + (coef_ref[1:2] * conv_ref[...] + coef_ref[2:3])
    dc_ref[...] = d_conv.astype(BF16).astype(F32)
    dl_ref[...] = jnp.zeros(dl_ref.shape, F32)
    dl_ref[half : half + rows, half : half + cols] = dsum_ref[...]
    pad_ref[...] = low_ref[...].astype(F32).reshape(pad_ref.shape)
    tap_ref[...] = jnp.zeros(tap_ref.shape, F32)

    def one_row(row, carry):
        source = [dc_ref[row, c] for c in range(cols)]
        for i in range(kernel):
            taps = [jnp.broadcast_to(depth_ref[i * kernel + j], (SUBLANES, LANES)) for j in range(kernel)]
            for c in range(wide):
                acc = dl_ref[row + i, c]
                for j in range(kernel):
                    if 0 <= c - j < cols:
                        acc = acc + source[c - j] * taps[j]
                dl_ref[row + i, c] = acc
        for i in range(kernel):
            sums = [tap_ref[i * kernel + j] for j in range(kernel)]
            for c in range(wide):
                value = pad_ref[row + i, c]
                for j in range(kernel):
                    if 0 <= c - j < cols:
                        sums[j] = sums[j] + source[c - j] * value
            for j in range(kernel):
                tap_ref[i * kernel + j] = sums[j]
        return carry

    lax.fori_loop(0, rows, one_row, 0)

    @pl.when(edge_ref[0] == 1)
    def _():
        dl_ref[:half] = jnp.zeros((half,) + dl_ref.shape[1:], F32)

    @pl.when(edge_ref[1] == 1)
    def _():
        dl_ref[half + rows :] = jnp.zeros((half,) + dl_ref.shape[1:], F32)

    @pl.when(edge_ref[2] == 1)
    def _():
        dl_ref[:, :half] = jnp.zeros((dl_ref.shape[0], half) + dl_ref.shape[2:], F32)

    @pl.when(edge_ref[3] == 1)
    def _():
        dl_ref[:, half + cols :] = jnp.zeros((dl_ref.shape[0], half) + dl_ref.shape[2:], F32)

    d_hidden = dl_ref[...]
    dh_ref[...] = d_hidden[:, half : half + cols].reshape(dh_ref.shape).astype(BF16)
    dh_low_ref[...] = d_hidden[:, :half].reshape(dh_low_ref.shape).astype(BF16)
    dh_high_ref[...] = d_hidden[:, half + cols :].reshape(dh_high_ref.shape).astype(BF16)
    gb_ref[...] = jnp.sum(jnp.sum(d_hidden, axis=(0, 1)), axis=0, keepdims=True)
    gw_ref[...] = jnp.sum(tap_ref[...], axis=1)


def conv_back(edges, coef, d_normed, conv_out, d_sum, lowered, depth, tile, first, last, prior=()):
    rows, cols, dates, half = tile
    taps = depth.shape[0]
    width = lowered.shape[1]
    padded = lowered.shape[0]
    inner = pl.BlockSpec((rows, cols, dates, LANES), lambda i: (0, 0, 0, first + i))
    wide = (rows + 2 * half, cols + 2 * half, dates, LANES)
    inside = (rows + 2 * half) * cols * dates
    beside = (rows + 2 * half) * half * dates

    def body(edge_ref, coef_ref, dn_ref, conv_ref, dsum_ref, low_ref, depth_ref, *refs):
        conv_back_body(rows, cols, half, edge_ref, coef_ref, dn_ref, conv_ref, dsum_ref, low_ref, depth_ref, *refs[len(prior) :])

    return pl.pallas_call(
        body,
        grid=(last - first,),
        in_specs=[
            pl.BlockSpec(memory_space=pltpu.SMEM),
            pl.BlockSpec((3, LANES), lambda i: (0, first + i)),
            inner,
            inner,
            inner,
            pl.BlockSpec((padded, LANES), lambda i: (0, first + i)),
            pl.BlockSpec((taps, 1, LANES), lambda i: (0, 0, first + i)),
        ]
        + [pl.BlockSpec(memory_space=pl.ANY)] * len(prior),
        out_specs=[
            pl.BlockSpec((count, LANES), lambda i: (0, first + i)) for count in (inside, beside, beside, taps, 1)
        ],
        out_shape=[
            jax.ShapeDtypeStruct((inside, width), BF16),
            jax.ShapeDtypeStruct((beside, width), BF16),
            jax.ShapeDtypeStruct((beside, width), BF16),
            jax.ShapeDtypeStruct((taps, width), F32),
            jax.ShapeDtypeStruct((1, width), F32),
        ],
        scratch_shapes=[
            pltpu.VMEM((rows, cols, dates, LANES), F32),
            pltpu.VMEM(wide, F32),
            pltpu.VMEM(wide, F32),
            pltpu.VMEM((taps, dates, LANES), F32),
        ],
        input_output_aliases={7 + k: k for k in range(len(prior))},
        cost_estimate=pl.CostEstimate(
            flops=4000000000 * (last - first),
            transcendentals=0,
            bytes_accessed=16 * padded * LANES * (last - first),
        ),
        name="conv_back",
    )(edges, coef, d_normed, conv_out, d_sum, lowered, depth, *prior)


def input_back(dh, dh_low, dh_high, x, x_low, x_high, w_slots, row_block=256):
    slots, width = w_slots.shape
    inside, beside = dh.shape[0], dh_low.shape[0]
    mix = (((1,), (1,)), ((), ()))
    down = (((0,), (0,)), ((), ()))

    def body(dh_ref, dl_ref, dr_ref, x_ref, xl_ref, xr_ref, w_ref, ds_ref, sl_ref, sr_ref, g_ref):
        ds_ref[...] = lax.dot_general(dh_ref[...], w_ref[...], mix, preferred_element_type=F32)

        @pl.when(pl.program_id(0) == 0)
        def _():
            sl_ref[...] = lax.dot_general(
                dl_ref[...], w_ref[...], mix, preferred_element_type=F32
            ).astype(BF16)
            sr_ref[...] = lax.dot_general(
                dr_ref[...], w_ref[...], mix, preferred_element_type=F32
            ).astype(BF16)
            g_ref[...] = lax.dot_general(
                xl_ref[...], dl_ref[...], down, preferred_element_type=F32
            ) + lax.dot_general(xr_ref[...], dr_ref[...], down, preferred_element_type=F32)

        g_ref[...] += lax.dot_general(x_ref[...], dh_ref[...], down, preferred_element_type=F32)

    moving = lambda i: (i, 0)
    fixed = lambda i: (0, 0)
    return pl.pallas_call(
        body,
        grid=(inside // row_block,),
        in_specs=[
            pl.BlockSpec((row_block, width), moving),
            pl.BlockSpec((beside, width), fixed),
            pl.BlockSpec((beside, width), fixed),
            pl.BlockSpec((row_block, slots), moving),
            pl.BlockSpec((beside, slots), fixed),
            pl.BlockSpec((beside, slots), fixed),
            pl.BlockSpec((slots, width), fixed),
        ],
        out_specs=[
            pl.BlockSpec((row_block, slots), moving),
            pl.BlockSpec((beside, slots), fixed),
            pl.BlockSpec((beside, slots), fixed),
            pl.BlockSpec((slots, width), fixed),
        ],
        out_shape=[
            jax.ShapeDtypeStruct((inside, slots), F32),
            jax.ShapeDtypeStruct((beside, slots), BF16),
            jax.ShapeDtypeStruct((beside, slots), BF16),
            jax.ShapeDtypeStruct((slots, width), F32),
        ],
        name="input_back",
    )(dh, dh_low, dh_high, x, x_low, x_high, w_slots)


def to_groups(d_state, from_high, from_low, groups):
    rows, pixels, slots = d_state.shape
    beside = from_low.shape[1]
    padded_ch = slots // groups

    def body(in_ref, high_ref, low_ref, out_ref):
        for row in range(rows):
            value = in_ref[row]
            first = value[:beside] + low_ref[row].astype(F32)
            last = value[pixels - beside :] + high_ref[row].astype(F32)
            value = jnp.concatenate([first, value[beside : pixels - beside], last], axis=0).T
            for g in range(groups):
                out_ref[g, row] = value[g * padded_ch : (g + 1) * padded_ch].astype(BF16)

    return pl.pallas_call(
        body,
        out_shape=jax.ShapeDtypeStruct((groups, rows, padded_ch, pixels), BF16),
        name="to_groups",
    )(d_state, from_high, from_low)


def on_device(
    ocean_state,
    slot_level,
    wet_mask,
    w_in,
    b_in,
    w_depth,
    norm_gain,
    norm_bias,
    w_one,
    b_one,
    w_two,
    b_two,
    w_out,
    b_out,
    cotangent,
):
    groups = lax.axis_size("lev")
    strips = lax.axis_size("sp")
    group_index = lax.axis_index("lev")
    strip_index = lax.axis_index("sp")
    rows, cols = wet_mask.shape
    all_rows, dates, _, group_ch = ocean_state.shape
    padded_ch = -(-group_ch // SUBLANES) * SUBLANES
    slots = padded_ch * groups
    channels, width = w_in.shape
    kernel = w_depth.shape[0]
    half = kernel // 2
    tile = (rows, cols, dates, half)
    high_rows = rows + 2 * half
    pixels = rows * cols * dates
    pixel_total = float(pixels * groups * strips)

    lev_stages = bits_of("lev")
    sp_stages = bits_of("sp")
    stages = lev_stages + sp_stages
    core, lev_rest = lev_stages[:1], lev_stages[1:]
    orders = (
        core + lev_rest + sp_stages,
        core + sp_stages[:1] + lev_rest + sp_stages[1:],
        core + sp_stages[1:2] + lev_rest + sp_stages[:1] + sp_stages[2:],
    )
    forward = [(i, i + 1) for i in range(strips - 1)]
    backward = [(i + 1, i) for i in range(strips - 1)]
    edges = jnp.stack(
        [group_index == 0, group_index == groups - 1, strip_index == 0, strip_index == strips - 1]
    ).astype(jnp.int32)

    table = slot_table(slot_level, groups, group_ch, padded_ch, channels)
    table_low = table.astype(BF16)
    w_slots = jnp.dot(table_low, w_in, preferred_element_type=F32).astype(BF16)
    w_out_slots = jnp.dot(w_out, table_low.T, preferred_element_type=F32).astype(BF16)
    b_slots = jnp.dot(table, b_out, precision=exact_mode)
    depth = w_depth.astype(F32).reshape(kernel * kernel, 1, width)

    row_pixels = cols * dates
    beside = half * dates
    windows, d_result = to_channel_rows(ocean_state, cotangent, groups, half, padded_ch)
    windows = lax.all_to_all(windows, "lev", split_axis=0, concat_axis=0, tiled=True)
    d_result = lax.all_to_all(
        after(d_result, windows), "lev", split_axis=0, concat_axis=0, tiled=True
    )
    x_rows = to_pixel_rows(windows)
    x_low = lax.ppermute(x_rows[:, row_pixels - beside :], "sp", forward).reshape(-1, slots)
    x_high = lax.ppermute(x_rows[:, :beside], "sp", backward).reshape(-1, slots)
    x_rows = x_rows.reshape(-1, slots)
    d_result = to_pixel_rows(d_result).reshape(pixels, slots)

    hidden, lowered, conv_out, local = hidden_conv(
        edges, x_rows, x_low, x_high, w_slots, b_in, depth, tile
    )
    total = butterfly(local, stages)
    wet = jnp.broadcast_to(
        wet_mask.astype(F32)[:, :, None, None], (rows, cols, dates, 1)
    ).reshape(pixels, 1)
    d_mixed = jnp.dot(d_result, w_out_slots.T, preferred_element_type=F32)
    d_sum = d_mixed * wet
    d_branch = d_sum.astype(BF16)
    g_b_two = jnp.sum(d_branch.astype(F32), axis=0)
    g_bias_slots = jnp.sum(d_result.astype(F32), axis=0)

    mean_value = total[0] / pixel_total
    inv_scale = lax.rsqrt(total[1] / pixel_total - mean_value * mean_value + 1e-05)
    conv_flat = conv_out.reshape(pixels, width)
    centered = (conv_flat - mean_value) * inv_scale
    normed = (centered * norm_gain + norm_bias).astype(BF16)
    ff = w_one.shape[1]
    block = 256
    cuts = [0, 2 * ff // 5 // block * block, 4 * ff // 5 // block * block, ff]
    flight = Exchanges()

    def as_rows(vector):
        flat = vector.reshape(-1)
        count = -(-flat.shape[0] // width)
        return jnp.pad(flat, (0, count * width - flat.shape[0])).reshape(count, width)

    w_two_t = w_two.T
    core_side = side(core[0])

    def part(number, prior=()):
        return mlp(
            core_side, normed, d_branch, w_one, b_one, w_two_t, cuts[number], cuts[number + 1], prior
        )

    def begin(name, grads, order):
        return flight.begin(name, grads[0], order, BF16, partner=grads[1])

    found, grads = part(0)
    sent = begin("a", grads, orders[0])
    found, grads = part(1, (after(found[0], sent),) + found[1:])
    sent = flight.step(found[2], "a")
    sent.append(begin("b", grads, orders[1]))
    found, grads = part(2, (after(found[0], *sent),) + found[1:])
    sent = flight.step(found[2], "b")
    sent.append(begin("c", grads, orders[2]))
    activated, d_up, g_b_one = found

    norm = jnp.stack([mean_value, inv_scale])
    d_normed, parts = norm_back(after(d_up, *sent), w_one, conv_flat, norm)
    sent = flight.step(parts, "a", "c")
    parts = jnp.concatenate(
        [parts, as_rows(g_b_one), as_rows(g_b_two), as_rows(g_bias_slots)], axis=0
    )
    first_hop = hop(parts, stages[0])
    result, g_out_slots = branch_out(
        after(activated, parts, *sent),
        w_two_t,
        b_two,
        hidden.reshape(pixels, width),
        wet,
        w_out_slots,
        b_slots,
        d_result,
        (groups, rows, padded_ch, row_pixels),
    )
    sent = flight.step(g_out_slots, "a", "b", "c")
    parts, *_ = lax.optimization_barrier((parts, *sent))
    summed = butterfly(parts + after(first_hop, g_out_slots), stages[1:])
    norm_grads = summed[:2]
    sent = flight.step(summed, "a", "b", "c")

    next_state = lax.all_to_all(result, "lev", split_axis=0, concat_axis=0, tiled=True)
    next_state = from_channel_rows(next_state, 0, dates, cols, group_ch)

    scale = norm_gain * inv_scale
    slope = scale * inv_scale * (norm_grads[1] / pixel_total)
    coef = jnp.stack(
        [scale, -slope, slope * mean_value - scale * (norm_grads[0] / pixel_total)]
    )
    shape4 = (rows, cols, dates, width)
    inputs = (d_normed.reshape(shape4), conv_out, d_sum.reshape(shape4), lowered, depth, tile)
    tiles = pl.cdiv(width, LANES)
    steps = [0, 2, 4, tiles]
    moves = (("a", "b", "c"),) * 3
    found = ()
    for first, last, names in zip(steps[:-1], steps[1:], moves):
        found = conv_back(edges, after(coef, *sent), *inputs, first, last, found)
        sent = flight.step(found[4], *names)
    d_hidden, d_low, d_high, g_w_depth, g_b_in = found
    d_state, d_low, d_high, g_in_slots = input_back(
        after(d_hidden, *sent), d_low, d_high, x_rows, x_low, x_high, w_slots
    )
    from_high = lax.ppermute(d_low.reshape(high_rows, beside, slots), "sp", backward)
    from_low = lax.ppermute(d_high.reshape(high_rows, beside, slots), "sp", forward)
    d_state = to_groups(
        d_state.reshape(high_rows, row_pixels, slots), from_high, from_low, groups
    )
    d_state = lax.all_to_all(d_state, "lev", split_axis=0, concat_axis=0, tiled=True)
    grad_ocean_state = from_channel_rows(d_state, half, dates, cols, group_ch)

    def pack(arrays):
        packed = jnp.concatenate(arrays, axis=0)
        return jnp.pad(packed, ((0, -packed.shape[0] % (16 * SUBLANES)), (0, 0))).reshape(
            -1, SUBLANES, width
        )

    def unpack(packed, arrays):
        packed = packed.reshape(-1, width)
        found = []
        start = 0
        for array in arrays:
            found.append(packed[start : start + array.shape[0]])
            start += array.shape[0]
        return found

    last_sums = [g_out_slots, g_in_slots, g_w_depth, g_b_in]
    flight.begin("small", pack(last_sums), orders[0], BF16, most=3)
    flight.finish(g_b_in, "small", "a", "b", "c")
    g_out_slots, g_in_slots, g_w_depth, g_b_in = unpack(in_order(*flight.done["small"]), last_sums)
    weights = ()
    for name, start in zip("acb", (cuts[0], cuts[2], cuts[1])):
        weights = unpack_grads(core_side, flight.done[name], width, ff, start, weights)
    grad_w_one, grad_w_two = weights
    grad_w_out = jnp.einsum("sd,sc->dc", g_out_slots.astype(F32), table, precision=exact_mode)
    count = -(-ff // width)
    grad_b_one = summed[2 : 2 + count].reshape(-1)[:ff]
    grad_b_two = summed[2 + count]
    grad_b_out = jnp.dot(summed[3 + count, :slots], table, precision=exact_mode)
    grad_w_in = jnp.dot(table.T, g_in_slots.astype(F32), precision=exact_mode)
    grad_w_depth = g_w_depth.astype(F32).reshape(kernel, kernel, width)
    grad_b_in = g_b_in.astype(F32).reshape(-1)
    return (
        next_state,
        grad_ocean_state,
        grad_w_in,
        grad_b_in,
        grad_w_depth,
        norm_grads[1],
        norm_grads[0],
        grad_w_one,
        grad_b_one,
        grad_w_two.T,
        grad_b_two,
        grad_w_out,
        grad_b_out,
    )


def solution(mesh):
    return jax.shard_map(
        on_device,
        mesh=mesh,
        in_specs=(
            P(None, None, "sp", "lev"),
            P(),
            P("lev", "sp"),
            P(),
            P(),
            P(),
            P(),
            P(),
            P(),
            P(),
            P(),
            P(),
            P(),
            P(),
            P(None, None, "sp", "lev"),
        ),
        out_specs=(
            P(None, None, "sp", "lev"),
            P(None, None, "sp", "lev"),
            P(),
            P(),
            P(),
            P(),
            P(),
            P(),
            P(),
            P(),
            P(),
            P(),
            P(),
        ),
        check_vma=False,
    )
```

time: 540 us -> 420 us (0.78)
  waiting for transfers between devices: 170 us -> 81.5 us
  Pallas kernels: 97.1 us -> 185 us
  local copies, waits for them, and re-layouts: 96.5 us -> 11.7 us
  matrix products: 34.4 us -> 9.9 us
  starting transfers between devices: 85.7 us -> 70.3 us
  other arithmetic: 48.5 us -> 54.6 us
    pallas_call x2 -> x18, Pallas kernels: 74.5 us -> 162 us  [the longest x3 54.5 us: mlp(): pl.pallas_call(body, grid=(pl.cdiv(last - first, block),), in_specs=[pl.B...]
    ppermute x54 -> x44, waiting for transfers between devices: 150 us -> 62.9 us  [hop(): lax.ppermute(value, axis, [(i, i ^ bit) for i in range(lax.axis_size(axis...]
    reshape x17 -> x3, local copies, waits for them, and re-layouts: 40 us -> 1.97 us  [the longest x1 0.7 us: on_device(): grad_w_depth = g_w_depth.astype(F32).reshape(kernel, kernel, width)]
    dot_general x9 -> x3, matrix products: 28.9 us -> 3.27 us  [the longest x1 1.23 us: on_device(): jnp.einsum('sd,sc->dc', g_out_slots.astype(F32), table, precision=exact_m...]
    convert_element_type x14 -> x20, other arithmetic: 10.9 us -> 30.7 us  [the longest x10 20.4 us: exchange(): sent = total([pair[1] for pair in pairs]).astype(link)]
    ppermute x54 -> x44, starting transfers between devices: 58.7 us -> 41.2 us  [hop(): lax.ppermute(value, axis, [(i, i ^ bit) for i in range(lax.axis_size(axis...]
    unnamed x166 -> x77, local copies, waits for them, and re-layouts: 19 us -> 3.61 us
    add x14 -> x1, other arithmetic: 10 us -> 0.01 us  [on_device(): summed = butterfly(parts + after(first_hop, g_out_slots), stages[1:])]
  transfers between devices with their start and end apart: 62 -> 52, of which waited for: 31 -> 17; matrix products, arithmetic and copies ran while one was open for 23% -> 15% of each run, Pallas kernels for 10% -> 28%
where the time goes in v2:
time: 420 us; the launch traced here: 414 us
  Pallas kernels  185 us (44%)
  waiting for transfers between devices  81.5 us (19%)
  starting transfers between devices  70.3 us (17%)
  other arithmetic  54.6 us (13%)
  local copies, waits for them, and re-layouts  11.7 us (3%)
  matrix products  9.9 us (2%)
    ppermute x44, waiting for transfers between devices, hop(): lax.ppermute(value, axis, [(i, i ^ bit) for i in range(lax.axis_size(axis...  62.9 us
    pallas_call x3, Pallas kernels, mlp(): pl.pallas_call(body, grid=(pl.cdiv(last - first, block),), in_specs=[pl.B...  54.5 us
    ppermute x44, starting transfers between devices, hop(): lax.ppermute(value, axis, [(i, i ^ bit) for i in range(lax.axis_size(axis...  41.2 us
    pallas_call x3, Pallas kernels, conv_back(): pl.pallas_call(body, grid=(last - first,), in_specs=[pl.BlockSpec(memory_...  35.9 us
    pallas_call x1, Pallas kernels, hidden_conv(): pl.pallas_call(functools.partial(hidden_conv_body, rows, cols, half), gri...  22.7 us
    convert_element_type x10, other arithmetic, exchange(): sent = total([pair[1] for pair in pairs]).astype(link)  20.4 us
    pallas_call x3, Pallas kernels, unpack_grads(): pl.pallas_call(body, grid_spec=pltpu.PrefetchScalarGridSpec(num_scalar_pr...  18.4 us
    pallas_call x1, Pallas kernels, branch_out(): pl.pallas_call(branch_out_body, grid=(pixels // row_block,), in_specs=[pl...  15.4 us
  transfers between devices with their start and end apart: 52, of which 17 were waited for; matrix products, arithmetic and copies ran while one was open for 15% of the time, Pallas kernels for 28%

profile of v2, /device:TPU:0, one launch (start us, length us, event | category | flops | bytes accessed | tf_op | source)
XLA Modules:
  0.0 414.4 jit_solution(9340503858225433850)
XLA Ops:
  4.0 4.4 %all-to-all-start = ((bf16[4,14,56,128]{3,2,1,0:T(8,128)(2,1)}), bf16[4,14,56,128]{3,2,1,0:T(8,128)(2,1)S(1)}, u32[]{:S(2)}, u32[]{:S(2)}) async-start(bf16[4,14,56,128]{3,2,1,0:T(8,128)(2,1)} %get-tuple-element.108), calls=%async_computation | async-start | bytes 1605632 | tf_op jit(solution)/shard_map/all_to_all | solution.py:810
  8.8 11.4 %all-to-all-done.in_ref = bf16[4,14,56,128]{3,2,1,0:T(8,128)(2,1)S(1)} async-done(((bf16[4,14,56,128]{3,2,1,0:T(8,128)(2,1)}), bf16[4,14,56,128]{3,2,1,0:T(8,128)(2,1)S(1)}, u32[]{:S(2)}, u32[]{:S(2)}) %all-to-all-start) | async-done | bytes 802848 | tf_op jit(solution)/shard_map/all_to_all | solution.py:810
  24.5 4.1 collective-permute-start
  36.8 22.7 %hidden_conv.1 = (f32[8,16,8,800]{3,2,1,0:T(8,128)}, bf16[2464,800]{1,0:T(8,128)(2,1)}, f32[8,16,8,800]{3,2,1,0:T(8,128)}, f32[2,800]{1,0:T(2,128)}) custom-call(s32[4]{0:T(128)} %add_convert_fusion.21.edge_ref, bf16[1792,224]{1,0:T(8,128)(2,1)} %bitcast.51, bf16[336,224]{1,0:T(8,128)(2,1)} %bitcast.76, bf16[336,224]{1,0:T(8,128)(2,1)} %bitcast.78, ...), custom_call_target="tpu_custom_call" | custom-call | flops 20000000000 | bytes 39424000 | tf_op jit(solution)/shard_map/hidden_conv/pallas_call | solution.py:348
  92.6 4.3 %convert_reduce_fusion = (f32[800]{0:T(1024)S(1)}, bf16[1024,800]{1,0:T(8,128)(2,1)}, f32[1024,800]{1,0:T(8,128)}) fusion(f32[1024]{0:T(1024)S(1)} %broadcast_in_dim.20, bf16[1024,224]{1,0:T(8,128)(2,1)} %bitcast.57, bf16[224,800]{0,1:T(8,128)(2,1)S(1)} %convolution_convert_fusion), kind=kOutput, calls=%fused_computation | convolution fusion | flops 370277600 | bytes 5739648 | tf_op jit(solution)/shard_map/dot_general | solution.py:827
  96.9 20.2 %mlp.3 = (bf16[1024,3200]{1,0:T(8,128)(2,1)}, bf16[1024,3200]{1,0:T(8,128)(2,1)}, bf16[800,1280]{1,0:T(8,128)(2,1)}, bf16[800,1280]{1,0:T(8,128)(2,1)}, f32[1,3200]{1,0:T(1,128)}) custom-call(s32[1]{0:T(128)} %bitcast.core_ref, bf16[1024,800]{1,0:T(8,128)(2,1)} %add_convert_fusion.normed_ref, bf16[1024,800]{1,0:T(8,128)(2,1)} %get-tuple-element.223.branch_ref, ...), custom_call_target="tpu_custom_call" | custom-call | flops 8388608000 | bytes 16711680 | tf_op jit(solution)/shard_map/mlp/pallas_call | solution.py:434
  117.1 20.4 %mlp.4 = (bf16[1024,3200]{1,0:T(8,128)(2,1)}, bf16[1024,3200]{1,0:T(8,128)(2,1)}, bf16[800,1280]{1,0:T(8,128)(2,1)}, bf16[800,1280]{1,0:T(8,128)(2,1)}, f32[1,3200]{1,0:T(1,128)}) custom-call(s32[1]{0:T(128)} %bitcast.core_ref, bf16[1024,800]{1,0:T(8,128)(2,1)} %add_convert_fusion.normed_ref, ...), custom_call_target="tpu_custom_call", output_to_operand_aliasing={{0}: (6, {}), {1}: (7, {}), {4}: (8, {})} | custom-call | flops 8388608000 | bytes 16711680 | tf_op jit(solution)/shard_map/mlp/pallas_call | solution.py:434
  143.2 13.9 %mlp.5 = (bf16[1024,3200]{1,0:T(8,128)(2,1)}, bf16[1024,3200]{1,0:T(8,128)(2,1)}, bf16[800,640]{1,0:T(8,128)(2,1)}, bf16[800,640]{1,0:T(8,128)(2,1)}, f32[1,3200]{1,0:T(1,128)}) custom-call(s32[1]{0:T(128)} %bitcast.core_ref, bf16[1024,800]{1,0:T(8,128)(2,1)} %add_convert_fusion.normed_ref, ...), custom_call_target="tpu_custom_call", output_to_operand_aliasing={{0}: (6, {}), {1}: (7, {}), {4}: (8, {})} | custom-call | flops 4194304000 | bytes 9994240 | tf_op jit(solution)/shard_map/mlp/pallas_call | solution.py:434
  161.6 13.0 %norm_back.1 = (f32[1024,800]{1,0:T(8,128)}, f32[2,800]{1,0:T(2,128)}) custom-call(bf16[1024,3200]{1,0:T(8,128)(2,1)} %get-tuple-element.131.dup_ref, bf16[800,3200]{1,0:T(8,128)(2,1)} %w_ref.1, f32[1024,800]{1,0:T(8,128)} %bitcast.62, f32[2,800]{1,0:T(2,128)} %pad_maximum_fusion.23.norm_ref), custom_call_target="tpu_custom_call" | custom-call | flops 5242880000 | bytes 18227200 | tf_op jit(solution)/shard_map/norm_back/pallas_call | solution.py:486
  182.6 15.4 %branch_out.1 = (bf16[4,8,56,128]{3,2,1,0:T(8,128)(2,1)}, f32[224,800]{1,0:T(8,128)}) custom-call(bf16[1024,3200]{1,0:T(8,128)(2,1)} %get-tuple-element.136.act_ref, bf16[800,3200]{1,0:T(8,128)(2,1)} %bitcast.56, f32[1,800]{1,0:T(1,128)} %reshape.179.b_ref, f32[1024,800]{1,0:T(8,128)} %bitcast.88, f32[1024,1]{1,0:T(8,128)} %broadcast_in_dim.22.wet_ref, ...), custom_call_target="tpu_custom_call" | custom-call | flops 5976883200 | bytes 14950400 | tf_op jit(solution)/shard_map/branch_out/pallas_call | solution.py:537
  205.9 8.4 %collective-permute-done.15 = f32[8,800]{1,0:T(8,128)S(1)} collective-permute-done((f32[8,800]{1,0:T(8,128)S(1)}, f32[8,800]{1,0:T(8,128)S(1)}, u32[]{:S(2)}, u32[]{:S(2)}) %collective-permute-start.15) | collective-permute-done | bytes 25632 | tf_op jit(solution)/shard_map/ppermute | solution.py:49
  238.8 10.7 %conv_back.3 = (bf16[1792,800]{1,0:T(8,128)(2,1)}, bf16[336,800]{1,0:T(8,128)(2,1)}, bf16[336,800]{1,0:T(8,128)(2,1)}, f32[49,800]{1,0:T(8,128)}, f32[1,800]{1,0:T(1,128)}) custom-call(s32[4]{0:T(128)} %add_convert_fusion.21.edge_ref, f32[3,800]{1,0:T(4,128)} %pad_maximum_fusion.22.coef_ref, f32[8,16,8,800]{3,2,1,0:T(8,128)} %bitcast.89, ...), custom_call_target="tpu_custom_call" | custom-call | flops 8000000000 | bytes 10092544 | tf_op jit(solution)/shard_map/conv_back/pallas_call | solution.py:639
  257.9 10.5 %conv_back.4 = (bf16[1792,800]{1,0:T(8,128)(2,1)}, bf16[336,800]{1,0:T(8,128)(2,1)}, bf16[336,800]{1,0:T(8,128)(2,1)}, f32[49,800]{1,0:T(8,128)}, f32[1,800]{1,0:T(1,128)}) custom-call(s32[4]{0:T(128)} %add_convert_fusion.21.edge_ref, ...), custom_call_target="tpu_custom_call", output_to_operand_aliasing={{0}: (7, {}), {1}: (8, {}), {2}: (9, {}), {3}: (10, {}), {4... | custom-call | flops 8000000000 | bytes 10092544 | tf_op jit(solution)/shard_map/conv_back/pallas_call | solution.py:639
  273.3 14.7 %conv_back.5 = (bf16[1792,800]{1,0:T(8,128)(2,1)}, bf16[336,800]{1,0:T(8,128)(2,1)}, bf16[336,800]{1,0:T(8,128)(2,1)}, f32[49,800]{1,0:T(8,128)}, f32[1,800]{1,0:T(1,128)}) custom-call(s32[4]{0:T(128)} %add_convert_fusion.21.edge_ref, ...), custom_call_target="tpu_custom_call", output_to_operand_aliasing={{0}: (7, {}), {1}: (8, {}), {2}: (9, {}), {3}: (10, {}), {4... | custom-call | flops 12000000000 | bytes 15138816 | tf_op jit(solution)/shard_map/conv_back/pallas_call | solution.py:639
  290.9 9.4 %input_back.1 = (f32[1792,224]{1,0:T(8,128)}, bf16[336,224]{1,0:T(8,128)(2,1)}, bf16[336,224]{1,0:T(8,128)(2,1)}, f32[224,800]{1,0:T(8,128)}) custom-call(bf16[1792,800]{1,0:T(8,128)(2,1)} %get-tuple-element.174.dh_ref, bf16[336,800]{1,0:T(8,128)(2,1)} %get-tuple-element.175.dl_ref, bf16[336,800]{1,0:T(8,128)(2,1)} %get-tuple-element.176.dr_ref, ...), custom_call_target="tpu_custom_call" | custom-call | tf_op jit(solution)/shard_map/input_back/pallas_call | solution.py:703
  307.5 14.3 %collective-permute-done.34 = bf16[16,8,800]{2,1,0:T(8,128)(2,1)S(1)} collective-permute-done((bf16[16,8,800]{2,1,0:T(8,128)(2,1)}, bf16[16,8,800]{2,1,0:T(8,128)(2,1)S(1)}, u32[]{:S(2)}, u32[]{:S(2)}) %collective-permute-start.34) | collective-permute-done | bytes 204832 | tf_op jit(solution)/shard_map/ppermute | solution.py:49
  324.8 4.1 all-to-all-start.2
  332.9 5.2 %collective-permute-start.32 = (bf16[14,24,224]{2,1,0:T(8,128)(2,1)}, bf16[14,24,224]{2,1,0:T(8,128)(2,1)}, u32[]{:S(2)}, u32[]{:S(2)}) collective-permute-start(bf16[14,24,224]{2,1,0:T(8,128)(2,1)} %bitcast.85), channel_id=1, source_target_pairs={{0,1},{1,2},{2,3},{3,4},{4,5},{5,6},{6,7},{8,9},{9,10},{10,11},{11... | collective-permute-start | bytes 451592 | tf_op jit(solution)/shard_map/ppermute | solution.py:915
  341.0 8.4 %collective-permute-done.36 = bf16[8,8,800]{2,1,0:T(8,128)(2,1)S(1)} collective-permute-done((bf16[8,8,800]{2,1,0:T(8,128)(2,1)S(1)}, bf16[8,8,800]{2,1,0:T(8,128)(2,1)S(1)}, u32[]{:S(2)}, u32[]{:S(2)}) %collective-permute-start.36) | collective-permute-done | bytes 102432 | tf_op jit(solution)/shard_map/ppermute | solution.py:49
  357.9 4.6 %all-to-all-start.3 = ((bf16[4,14,56,128]{3,2,1,0:T(8,128)(2,1)}), bf16[4,14,56,128]{3,2,1,0:T(8,128)(2,1)}, u32[]{:S(2)}, u32[]{:S(2)}) async-start(bf16[4,14,56,128]{3,2,1,0:T(8,128)(2,1)} %to_groups.1), calls=%async_computation.3 | async-start | bytes 1605632 | tf_op jit(solution)/shard_map/all_to_all | solution.py:919
  366.3 9.7 %collective-permute-done.38 = bf16[8,8,800]{2,1,0:T(8,128)(2,1)S(1)} collective-permute-done((bf16[8,8,800]{2,1,0:T(8,128)(2,1)S(1)}, bf16[8,8,800]{2,1,0:T(8,128)(2,1)S(1)}, u32[]{:S(2)}, u32[]{:S(2)}) %collective-permute-start.38) | collective-permute-done | bytes 102432 | tf_op jit(solution)/shard_map/ppermute | solution.py:49
  395.7 6.6 %unpack_grads.3 = (f32[800,3200]{1,0:T(8,128)}, f32[800,3200]{1,0:T(8,128)}) custom-call(s32[2]{0:T(128)} %pad_add_fusion.2.own_ref, bf16[100,8,1280]{2,1,0:T(8,128)(2,1)} %pad_maximum_fusion.1.value_ref, bf16[100,8,1280]{2,1,0:T(8,128)(2,1)} %collective-permute-done.47.other_ref), custom_call_target="tpu_custom_call" | custom-call | tf_op jit(solution)/shard_map/unpack_grads/pallas_call | solution.py:196
  402.3 5.0 %unpack_grads.4 = (f32[800,3200]{1,0:T(8,128)}, f32[800,3200]{1,0:T(8,128)}) custom-call(s32[2]{0:T(128)} %get-tuple-element.240.own_ref, bf16[100,8,640]{2,1,0:T(8,128)(2,1)} %pad_maximum_fusion.4.value_ref, bf16[100,8,640]{2,1,0:T(8,128)(2,1)} %collective-permute-done.45.other_ref, ...), custom_call_target="tpu_custom_call", output_to_operand_aliasing={{0}: (3, {}), {1}: (4, {})} | custom-call | tf_op jit(solution)/shard_map/unpack_grads/pallas_call | solution.py:196
  407.3 6.8 %unpack_grads.5 = (f32[800,3200]{1,0:T(8,128)}, f32[800,3200]{1,0:T(8,128)}) custom-call(s32[2]{0:T(128)} %get-tuple-element.239.own_ref, bf16[100,8,1280]{2,1,0:T(8,128)(2,1)} %copy-done.2, bf16[100,8,1280]{2,1,0:T(8,128)(2,1)} %collective-permute-done.43.other_ref, ...), custom_call_target="tpu_custom_call", output_to_operand_aliasing={{0}: (3, {}), {1}: (4, {})} | custom-call | tf_op jit(solution)/shard_map/unpack_grads/pallas_call | solution.py:196
  (269 shorter events, 164.6 us)
Async XLA Ops:
  117.0 23.3 %collective-permute-start.7 = (bf16[100,8,1280]{2,1,0:T(8,128)(2,1)}, bf16[100,8,1280]{2,1,0:T(8,128)(2,1)}, u32[]{:S(2)}, u32[]{:S(2)}) collective-permute-start(bf16[100,8,1280]{2,1,0:T(8,128)(2,1)} %bitcast.83), channel_id=1, source_target_pairs={{0,8},{8,0},{16,24},{24,16},{1,9},{9,1},{17,25},{25,17},{2,10},{10... | collective-permute-start | bytes 6144008 | tf_op jit(solution)/shard_map/ppermute | solution.py:49
  137.5 20.5 %collective-permute-start.8 = (bf16[100,8,1280]{2,1,0:T(8,128)(2,1)}, bf16[100,8,1280]{2,1,0:T(8,128)(2,1)}, u32[]{:S(2)}, u32[]{:S(2)}) collective-permute-start(bf16[100,8,1280]{2,1,0:T(8,128)(2,1)} %bitcast.82), channel_id=1, source_target_pairs={{0,8},{8,0},{16,24},{24,16},{1,9},{9,1},{17,25},{25,17},{2,10},{10... | collective-permute-start | bytes 6144008 | tf_op jit(solution)/shard_map/ppermute | solution.py:49
  142.8 32.7 %collective-permute-start.9 = (bf16[50,8,1280]{2,1,0:T(8,128)(2,1)}, bf16[50,8,1280]{2,1,0:T(8,128)(2,1)}, u32[]{:S(2)}, u32[]{:S(2)}) collective-permute-start(bf16[50,8,1280]{2,1,0:T(8,128)(2,1)} %add_convert_fusion.2), channel_id=1, source_target_pairs={{0,16},{8,24},{16,0},{24,8},{1,17},{9,25},{17,1},{25,9},{2,18},{10... | collective-permute-start | bytes 3072008 | tf_op jit(solution)/shard_map/ppermute | solution.py:49
  157.1 18.4 %collective-permute-start.10 = (bf16[100,8,640]{2,1,0:T(8,128)(2,1)}, bf16[100,8,640]{2,1,0:T(8,128)(2,1)}, u32[]{:S(2)}, u32[]{:S(2)}) collective-permute-start(bf16[100,8,640]{2,1,0:T(8,128)(2,1)} %bitcast.84), channel_id=1, source_target_pairs={{0,8},{8,0},{16,24},{24,16},{1,9},{9,1},{17,25},{25,17},{2,10},{10... | collective-permute-start | bytes 3072008 | tf_op jit(solution)/shard_map/ppermute | solution.py:49
  160.5 37.6 %collective-permute-start.12 = (bf16[50,8,1280]{2,1,0:T(8,128)(2,1)}, bf16[50,8,1280]{2,1,0:T(8,128)(2,1)S(1)}, u32[]{:S(2)}, u32[]{:S(2)}) collective-permute-start(bf16[50,8,1280]{2,1,0:T(8,128)(2,1)} %add_convert_fusion.1), channel_id=1, source_target_pairs={{0,1},{1,0},{2,3},{3,2},{4,5},{5,4},{6,7},{7,6},{8,9},{9,8},{10,11... | collective-permute-start | bytes 3072008 | tf_op jit(solution)/shard_map/ppermute | solution.py:49
  175.3 22.8 %collective-permute-start.14 = (f32[8,800]{1,0:T(8,128)S(1)}, f32[8,800]{1,0:T(8,128)S(1)}, u32[]{:S(2)}, u32[]{:S(2)}) collective-permute-start(f32[8,800]{1,0:T(8,128)S(1)} %pad_maximum_fusion.21), channel_id=1, source_target_pairs={{0,8},{8,0},{16,24},{24,16},{1,9},{9,1},{17,25},{25,17},{2,10},{10... | collective-permute-start | bytes 76808 | tf_op jit(solution)/shard_map/ppermute | solution.py:49
  177.7 24.1 %collective-permute-start.13 = (bf16[50,8,640]{2,1,0:T(8,128)(2,1)}, bf16[50,8,640]{2,1,0:T(8,128)(2,1)}, u32[]{:S(2)}, u32[]{:S(2)}) collective-permute-start(bf16[50,8,640]{2,1,0:T(8,128)(2,1)} %add_convert_fusion.4), channel_id=1, source_target_pairs={{0,2},{1,3},{2,0},{3,1},{4,6},{5,7},{6,4},{7,5},{8,10},{9,11},{10,... | collective-permute-start | bytes 1536008 | tf_op jit(solution)/shard_map/ppermute | solution.py:49
  180.9 20.9 %collective-permute-start.11 = (bf16[25,8,1280]{2,1,0:T(8,128)(2,1)}, bf16[25,8,1280]{2,1,0:T(8,128)(2,1)}, u32[]{:S(2)}, u32[]{:S(2)}) collective-permute-start(bf16[25,8,1280]{2,1,0:T(8,128)(2,1)} %add_convert_fusion.5), channel_id=1, source_target_pairs={{0,1},{1,0},{2,3},{3,2},{4,5},{5,4},{6,7},{7,6},{8,9},{9,8},{10,11... | collective-permute-start | bytes 1536008 | tf_op jit(solution)/shard_map/ppermute | solution.py:49
  200.1 27.6 %collective-permute-start.21 = (bf16[25,8,1280]{2,1,0:T(8,128)(2,1)}, bf16[25,8,1280]{2,1,0:T(8,128)(2,1)}, u32[]{:S(2)}, u32[]{:S(2)}) collective-permute-start(bf16[25,8,1280]{2,1,0:T(8,128)(2,1)} %add_convert_fusion.3), channel_id=1, source_target_pairs={{0,16},{8,24},{16,0},{24,8},{1,17},{9,25},{17,1},{25,9},{2,18},{10... | collective-permute-start | bytes 1536008 | tf_op jit(solution)/shard_map/ppermute | solution.py:49
  229.9 19.6 %collective-permute-start.24 = (bf16[25,8,640]{2,1,0:T(8,128)(2,1)}, bf16[25,8,640]{2,1,0:T(8,128)(2,1)}, u32[]{:S(2)}, u32[]{:S(2)}) collective-permute-start(bf16[25,8,640]{2,1,0:T(8,128)(2,1)} %add_convert_fusion.12), channel_id=1, source_target_pairs={{0,2},{1,3},{2,0},{3,1},{4,6},{5,7},{6,4},{7,5},{8,10},{9,11},{10,... | collective-permute-start | bytes 768008 | tf_op jit(solution)/shard_map/ppermute | solution.py:49
  234.0 19.5 %collective-permute-start.25 = (bf16[25,8,640]{2,1,0:T(8,128)(2,1)S(1)}, bf16[25,8,640]{2,1,0:T(8,128)(2,1)}, u32[]{:S(2)}, u32[]{:S(2)}) collective-permute-start(bf16[25,8,640]{2,1,0:T(8,128)(2,1)S(1)} %add_convert_fusion.11), channel_id=1, source_target_pairs={{0,1},{1,0},{2,3},{3,2},{4,5},{5,4},{6,7},{7,6},{8,9},{9,8},{10,11... | collective-permute-start | bytes 768008 | tf_op jit(solution)/shard_map/ppermute | solution.py:49
  269.4 18.6 %collective-permute-start.29 = (bf16[25,8,640]{2,1,0:T(8,128)(2,1)S(1)}, bf16[25,8,640]{2,1,0:T(8,128)(2,1)S(1)}, u32[]{:S(2)}, u32[]{:S(2)}) collective-permute-start(bf16[25,8,640]{2,1,0:T(8,128)(2,1)S(1)} %add_convert_fusion.7), channel_id=1, source_target_pairs={{0,2},{1,3},{2,0},{3,1},{4,6},{5,7},{6,4},{7,5},{8,10},{9,11},{10,... | collective-permute-start | bytes 768008 | tf_op jit(solution)/shard_map/ppermute | solution.py:49
  270.7 18.3 %collective-permute-start.30 = (bf16[25,8,640]{2,1,0:T(8,128)(2,1)S(1)}, bf16[25,8,640]{2,1,0:T(8,128)(2,1)S(1)}, u32[]{:S(2)}, u32[]{:S(2)}) collective-permute-start(bf16[25,8,640]{2,1,0:T(8,128)(2,1)S(1)} %add_convert_fusion.6), channel_id=1, source_target_pairs={{0,16},{8,24},{16,0},{24,8},{1,17},{9,25},{17,1},{25,9},{2,18},{10... | collective-permute-start | bytes 768008 | tf_op jit(solution)/shard_map/ppermute | solution.py:49
  272.0 17.8 %collective-permute-start.28 = (bf16[25,8,1280]{2,1,0:T(8,128)(2,1)S(1)}, bf16[25,8,1280]{2,1,0:T(8,128)(2,1)S(1)}, u32[]{:S(2)}, u32[]{:S(2)}) collective-permute-start(bf16[25,8,1280]{2,1,0:T(8,128)(2,1)S(1)} %pad_maximum_fusion.6), channel_id=1, source_target_pairs={{0,1},{1,0},{2,3},{3,2},{4,5},{5,4},{6,7},{7,6},{8,9},{9,8},{10,11... | collective-permute-start | bytes 1536008 | tf_op jit(solution)/shard_map/ppermute | solution.py:49
  302.7 30.3 %collective-permute-start.41 = (bf16[25,8,1280]{2,1,0:T(8,128)(2,1)}, bf16[25,8,1280]{2,1,0:T(8,128)(2,1)}, u32[]{:S(2)}, u32[]{:S(2)}) collective-permute-start(bf16[25,8,1280]{2,1,0:T(8,128)(2,1)} %pad_maximum_fusion.7), channel_id=1, source_target_pairs={{0,16},{8,24},{16,0},{24,8},{1,17},{9,25},{17,1},{25,9},{2,18},{10... | collective-permute-start | bytes 1536008 | tf_op jit(solution)/shard_map/ppermute | solution.py:49
  324.8 27.1 %all-to-all-start.2 = ((bf16[4,8,56,128]{3,2,1,0:T(8,128)(2,1)}), bf16[4,8,56,128]{3,2,1,0:T(8,128)(2,1)}, u32[]{:S(2)}, u32[]{:S(2)}) async-start(bf16[4,8,56,128]{3,2,1,0:T(8,128)(2,1)} %get-tuple-element.138), calls=%async_computation.2 | async-start | bytes 917504 | tf_op jit(solution)/shard_map/all_to_all | solution.py:893
  329.0 33.5 %collective-permute-start.44 = (bf16[50,8,640]{2,1,0:T(8,128)(2,1)}, bf16[50,8,640]{2,1,0:T(8,128)(2,1)}, u32[]{:S(2)}, u32[]{:S(2)}) collective-permute-start(bf16[50,8,640]{2,1,0:T(8,128)(2,1)} %pad_maximum_fusion.8), channel_id=1, source_target_pairs={{0,2},{1,3},{2,0},{3,1},{4,6},{5,7},{6,4},{7,5},{8,10},{9,11},{10,... | collective-permute-start | bytes 1536008 | tf_op jit(solution)/shard_map/ppermute | solution.py:49
  329.7 47.7 %collective-permute-start.46 = (bf16[50,8,1280]{2,1,0:T(8,128)(2,1)}, bf16[50,8,1280]{2,1,0:T(8,128)(2,1)}, u32[]{:S(2)}, u32[]{:S(2)}) collective-permute-start(bf16[50,8,1280]{2,1,0:T(8,128)(2,1)} %pad_maximum_fusion.2), channel_id=1, source_target_pairs={{0,16},{8,24},{16,0},{24,8},{1,17},{9,25},{17,1},{25,9},{2,18},{10... | collective-permute-start | bytes 3072008 | tf_op jit(solution)/shard_map/ppermute | solution.py:49
  331.7 17.8 %collective-permute-start.31 = (bf16[14,24,224]{2,1,0:T(8,128)(2,1)}, bf16[14,24,224]{2,1,0:T(8,128)(2,1)}, u32[]{:S(2)}, u32[]{:S(2)}) collective-permute-start(bf16[14,24,224]{2,1,0:T(8,128)(2,1)} %bitcast.86), channel_id=1, source_target_pairs={{1,0},{2,1},{3,2},{4,3},{5,4},{6,5},{7,6},{9,8},{10,9},{11,10},{12... | collective-permute-start | bytes 451592 | tf_op jit(solution)/shard_map/ppermute | solution.py:914
  332.9 22.1 %collective-permute-start.32 = (bf16[14,24,224]{2,1,0:T(8,128)(2,1)}, bf16[14,24,224]{2,1,0:T(8,128)(2,1)}, u32[]{:S(2)}, u32[]{:S(2)}) collective-permute-start(bf16[14,24,224]{2,1,0:T(8,128)(2,1)} %bitcast.85), channel_id=1, source_target_pairs={{0,1},{1,2},{2,3},{3,4},{4,5},{5,6},{6,7},{8,9},{9,10},{10,11},{11... | collective-permute-start | bytes 451592 | tf_op jit(solution)/shard_map/ppermute | solution.py:915
  349.4 30.8 %collective-permute-start.42 = (bf16[50,8,1280]{2,1,0:T(8,128)(2,1)S(1)}, bf16[50,8,1280]{2,1,0:T(8,128)(2,1)}, u32[]{:S(2)}, u32[]{:S(2)}) collective-permute-start(bf16[50,8,1280]{2,1,0:T(8,128)(2,1)S(1)} %pad_maximum_fusion.3), channel_id=1, source_target_pairs={{0,1},{1,0},{2,3},{3,2},{4,5},{5,4},{6,7},{7,6},{8,9},{9,8},{10,11... | collective-permute-start | bytes 3072008 | tf_op jit(solution)/shard_map/ppermute | solution.py:49
  357.9 28.4 %all-to-all-start.3 = ((bf16[4,14,56,128]{3,2,1,0:T(8,128)(2,1)}), bf16[4,14,56,128]{3,2,1,0:T(8,128)(2,1)}, u32[]{:S(2)}, u32[]{:S(2)}) async-start(bf16[4,14,56,128]{3,2,1,0:T(8,128)(2,1)} %to_groups.1), calls=%async_computation.3 | async-start | bytes 1605632 | tf_op jit(solution)/shard_map/all_to_all | solution.py:919
  366.1 22.6 %collective-permute-start.45 = (bf16[100,8,640]{2,1,0:T(8,128)(2,1)}, bf16[100,8,640]{2,1,0:T(8,128)(2,1)}, u32[]{:S(2)}, u32[]{:S(2)}) collective-permute-start(bf16[100,8,640]{2,1,0:T(8,128)(2,1)} %pad_maximum_fusion.4.value_ref), channel_id=1, source_target_pairs={{0,8},{8,0},{16,24},{24,16},{1,9},{9,1},{17,25},{25,17},{2,10},{10... | collective-permute-start | bytes 3072008 | tf_op jit(solution)/shard_map/ppermute | solution.py:49
  384.9 22.5 %collective-permute-start.43 = (bf16[100,8,1280]{2,1,0:T(8,128)(2,1)S(1)}, bf16[100,8,1280]{2,1,0:T(8,128)(2,1)}, u32[]{:S(2)}, u32[]{:S(2)}) collective-permute-start(bf16[100,8,1280]{2,1,0:T(8,128)(2,1)S(1)} %pad_maximum_fusion.value_ref), channel_id=1, source_target_pairs={{0,8},{8,0},{16,24},{24,16},{1,9},{9,1},{17,25},{25,17},{2,10},{10... | collective-permute-start | bytes 6144008 | tf_op jit(solution)/shard_map/ppermute | solution.py:49
  (63 other events, 929.8 us)

commit v3 on v2

--- a/solution.py
+++ b/solution.py
@@ -14,6 +14,8 @@
 exact_mode = lax.Precision.HIGHEST
 F32 = jnp.float32
 BF16 = jnp.bfloat16
+
+COST = pl.CostEstimate(flops=50000000000, transcendentals=0, bytes_accessed=50000000)
 
 TAIL_SCALE = 0.3
 TAIL_POLY = (
@@ -72,7 +74,8 @@
 
 
 def halving_lanes(lanes):
-    return lanes % (2 * LANES) == 0
+    tiles = lanes // LANES
+    return lanes % LANES == 0 and (tiles % 2 == 0 or tiles >= 9)
 
 
 def total(terms):
@@ -85,6 +88,7 @@
 def exchange(value, stages, link, partner=None, most=2):
     kept = []
     own = 0
+    lanes = value.shape[2]
     terms = [value]
     rest = stages
     if partner is not None:
@@ -108,6 +112,8 @@
             sent = total(terms).astype(link)
             terms = [sent]
         else:
+            if axis == 2 and shape[2] // LANES % 2:
+                terms = [jnp.pad(term, ((0, 0), (0, 0), (0, LANES))) for term in terms]
             pairs = [halves(term, axis, bit) for term in terms]
             sent = total([pair[1] for pair in pairs]).astype(link)
             terms = [pair[0] for pair in pairs]
@@ -126,7 +132,7 @@
             bit = side(stage)
             low = jnp.where(bit == 0, value, came)
             high = jnp.where(bit == 0, came, value)
-            value = jnp.concatenate([low, high], axis=2)
+            value = jnp.concatenate([low, high], axis=2)[:, :, :lanes]
     other = None
     if partner is not None:
         came = hop(value, stages[0])
@@ -203,6 +209,7 @@
         ),
         out_shape=[jax.ShapeDtypeStruct((width, ff), F32)] * 2,
         input_output_aliases={3 + k: k for k in range(len(prior))},
+        cost_estimate=COST,
         name="unpack_grads",
     )(jnp.stack([own, core_side]).astype(jnp.int32), value, other, *prior)
 
@@ -248,6 +255,7 @@
             jax.ShapeDtypeStruct((groups, high, padded_ch, pixels), BF16),
             jax.ShapeDtypeStruct((groups, rows, padded_ch, pixels), BF16),
         ],
+        cost_estimate=COST,
         name="to_channel_rows",
     )(state, cotangent)
 
@@ -273,6 +281,7 @@
     return pl.pallas_call(
         body,
         out_shape=jax.ShapeDtypeStruct((groups * rows, dates, cols, ch), BF16),
+        cost_estimate=COST,
         name="from_channel_rows",
     )(windows)
 
@@ -289,6 +298,7 @@
     return pl.pallas_call(
         body,
         out_shape=jax.ShapeDtypeStruct((rows, pixels, slots), BF16),
+        cost_estimate=COST,
         name="to_pixel_rows",
     )(received)
 
@@ -370,9 +380,8 @@
             jax.ShapeDtypeStruct((2, width), F32),
         ],
         scratch_shapes=[pltpu.VMEM((rows + 2 * half, cols + 2 * half, dates, LANES), F32)],
-        cost_estimate=pl.CostEstimate(
-            flops=20000000000, transcendentals=0, bytes_accessed=20 * padded * width
-        ),
+
+        cost_estimate=COST,
         name="hidden_conv",
     )(edges, x, low_x, high_x, w_slots, b_in.reshape(1, -1), depth)
 
@@ -421,7 +430,7 @@
         send_ref[...] = grad_one
 
 
-def mlp(core_side, normed, d_branch, w_one, b_one, w_two, first, last, prior=(), block=256, row_block=256):
+def mlp(core_side, normed, d_branch, w_one, b_one, w_two, first, last, prior=(), block=256, row_block=128):
     pixels, width = normed.shape
     hidden = w_one.shape[1]
     start = first // block
@@ -453,11 +462,8 @@
         out_shape=[whole, whole, grad, grad, jax.ShapeDtypeStruct((1, hidden), F32)],
         scratch_shapes=[pltpu.VMEM((width, pixels), BF16), pltpu.VMEM((width, pixels), BF16)],
         input_output_aliases={6 + n: k for n, k in enumerate((0, 1, 4)[: len(prior)])},
-        cost_estimate=pl.CostEstimate(
-            flops=8 * pixels * width * (last - first),
-            transcendentals=2 * pixels * (last - first),
-            bytes_accessed=4 * pixels * width + 8 * width * (last - first) + 4 * pixels * (last - first),
-        ),
+
+        cost_estimate=COST,
         name="mlp",
     )(core_side.reshape(1).astype(jnp.int32), normed, d_branch, w_one, b_one.reshape(1, -1), w_two, *prior)
     activated, d_up, keep, send, bias = results
@@ -500,11 +506,8 @@
             jax.ShapeDtypeStruct((pixels, width), F32),
             jax.ShapeDtypeStruct((2, width), F32),
         ],
-        cost_estimate=pl.CostEstimate(
-            flops=2 * pixels * width * hidden,
-            transcendentals=0,
-            bytes_accessed=2 * (pixels + width) * hidden + 8 * pixels * width,
-        ),
+
+        cost_estimate=COST,
         name="norm_back",
     )(d_up, w_one, conv_flat, norm)
 
@@ -557,11 +560,8 @@
             jax.ShapeDtypeStruct(out_shape, BF16),
             jax.ShapeDtypeStruct((slots, width), F32),
         ],
-        cost_estimate=pl.CostEstimate(
-            flops=2 * pixels * width * (inner + 2 * slots),
-            transcendentals=0,
-            bytes_accessed=2 * (pixels + width) * inner + 4 * pixels * width,
-        ),
+
+        cost_estimate=COST,
         name="branch_out",
     )(activated, w_two, b_two.reshape(1, -1), hidden, wet, w_out_slots, b_slots.reshape(1, -1), d_result)
 
@@ -666,18 +666,16 @@
             pltpu.VMEM((taps, dates, LANES), F32),
         ],
         input_output_aliases={7 + k: k for k in range(len(prior))},
-        cost_estimate=pl.CostEstimate(
-            flops=4000000000 * (last - first),
-            transcendentals=0,
-            bytes_accessed=16 * padded * LANES * (last - first),
-        ),
+
+        cost_estimate=COST,
         name="conv_back",
     )(edges, coef, d_normed, conv_out, d_sum, lowered, depth, *prior)
 
 
-def input_back(dh, dh_low, dh_high, x, x_low, x_high, w_slots, row_block=256):
+def input_back(dh, dh_low, dh_high, x, x_low, x_high, w_slots):
     slots, width = w_slots.shape
     inside, beside = dh.shape[0], dh_low.shape[0]
+    row_block = inside // 2
     mix = (((1,), (1,)), ((), ()))
     down = (((0,), (0,)), ((), ()))
 
@@ -724,6 +722,7 @@
             jax.ShapeDtypeStruct((beside, slots), BF16),
             jax.ShapeDtypeStruct((slots, width), F32),
         ],
+        cost_estimate=COST,
         name="input_back",
     )(dh, dh_low, dh_high, x, x_low, x_high, w_slots)
 
@@ -745,6 +744,7 @@
     return pl.pallas_call(
         body,
         out_shape=jax.ShapeDtypeStruct((groups, rows, padded_ch, pixels), BF16),
+        cost_estimate=COST,
         name="to_groups",
     )(d_state, from_high, from_low)
 
@@ -790,6 +790,7 @@
         core + lev_rest + sp_stages,
         core + sp_stages[:1] + lev_rest + sp_stages[1:],
         core + sp_stages[1:2] + lev_rest + sp_stages[:1] + sp_stages[2:],
+        core + sp_stages + lev_rest,
     )
     forward = [(i, i + 1) for i in range(strips - 1)]
     backward = [(i + 1, i) for i in range(strips - 1)]
@@ -820,7 +821,7 @@
     hidden, lowered, conv_out, local = hidden_conv(
         edges, x_rows, x_low, x_high, w_slots, b_in, depth, tile
     )
-    total = butterfly(local, stages)
+    came = hop(local, stages[0])
     wet = jnp.broadcast_to(
         wet_mask.astype(F32)[:, :, None, None], (rows, cols, dates, 1)
     ).reshape(pixels, 1)
@@ -830,14 +831,16 @@
     g_b_two = jnp.sum(d_branch.astype(F32), axis=0)
     g_bias_slots = jnp.sum(d_result.astype(F32), axis=0)
 
-    mean_value = total[0] / pixel_total
-    inv_scale = lax.rsqrt(total[1] / pixel_total - mean_value * mean_value + 1e-05)
+    sums = butterfly(local + after(came, d_branch), stages[1:])
+    mean_value = sums[0] / pixel_total
+    inv_scale = lax.rsqrt(sums[1] / pixel_total - mean_value * mean_value + 1e-05)
     conv_flat = conv_out.reshape(pixels, width)
     centered = (conv_flat - mean_value) * inv_scale
     normed = (centered * norm_gain + norm_bias).astype(BF16)
     ff = w_one.shape[1]
     block = 256
-    cuts = [0, 2 * ff // 5 // block * block, 4 * ff // 5 // block * block, ff]
+    cut = ff // 2 // block * block
+    spans = {"a": (cut, ff), "b": (0, cut)}
     flight = Exchanges()
 
     def as_rows(vector):
@@ -848,33 +851,26 @@
     w_two_t = w_two.T
     core_side = side(core[0])
 
-    def part(number, prior=()):
-        return mlp(
-            core_side, normed, d_branch, w_one, b_one, w_two_t, cuts[number], cuts[number + 1], prior
+    def part(name, order, prior=()):
+        found, grads = mlp(
+            core_side, normed, d_branch, w_one, b_one, w_two_t, *spans[name], prior
         )
-
-    def begin(name, grads, order):
-        return flight.begin(name, grads[0], order, BF16, partner=grads[1])
-
-    found, grads = part(0)
-    sent = begin("a", grads, orders[0])
-    found, grads = part(1, (after(found[0], sent),) + found[1:])
-    sent = flight.step(found[2], "a")
-    sent.append(begin("b", grads, orders[1]))
-    found, grads = part(2, (after(found[0], *sent),) + found[1:])
-    sent = flight.step(found[2], "b")
-    sent.append(begin("c", grads, orders[2]))
+        return found, flight.begin(name, grads[0], order, BF16, partner=grads[1])
+
+    found, sent = part("a", orders[0])
+    found, sent = part("b", orders[1], (after(found[0], sent),) + found[1:])
     activated, d_up, g_b_one = found
+    sent = [sent] + flight.step(g_b_one, "a")
 
     norm = jnp.stack([mean_value, inv_scale])
     d_normed, parts = norm_back(after(d_up, *sent), w_one, conv_flat, norm)
-    sent = flight.step(parts, "a", "c")
+    sent = flight.step(parts, "b")
     parts = jnp.concatenate(
         [parts, as_rows(g_b_one), as_rows(g_b_two), as_rows(g_bias_slots)], axis=0
     )
     first_hop = hop(parts, stages[0])
     result, g_out_slots = branch_out(
-        after(activated, parts, *sent),
+        after(activated, *sent),
         w_two_t,
         b_two,
         hidden.reshape(pixels, width),
@@ -884,14 +880,13 @@
         d_result,
         (groups, rows, padded_ch, row_pixels),
     )
-    sent = flight.step(g_out_slots, "a", "b", "c")
-    parts, *_ = lax.optimization_barrier((parts, *sent))
-    summed = butterfly(parts + after(first_hop, g_out_slots), stages[1:])
+    sent = flight.step(g_out_slots, "a")
+    result = after(result, *sent)
+    next_state = lax.all_to_all(result, "lev", split_axis=0, concat_axis=0, tiled=True)
+    first_hop = after(first_hop, g_out_slots, *sent)
+    summed = butterfly(parts + first_hop, stages[1:])
     norm_grads = summed[:2]
-    sent = flight.step(summed, "a", "b", "c")
-
-    next_state = lax.all_to_all(result, "lev", split_axis=0, concat_axis=0, tiled=True)
-    next_state = from_channel_rows(next_state, 0, dates, cols, group_ch)
+    sent = flight.step(summed, "b")
 
     scale = norm_gain * inv_scale
     slope = scale * inv_scale * (norm_grads[1] / pixel_total)
@@ -902,22 +897,18 @@
     inputs = (d_normed.reshape(shape4), conv_out, d_sum.reshape(shape4), lowered, depth, tile)
     tiles = pl.cdiv(width, LANES)
     steps = [0, 2, 4, tiles]
-    moves = (("a", "b", "c"),) * 3
     found = ()
-    for first, last, names in zip(steps[:-1], steps[1:], moves):
+    for number, (first, last) in enumerate(zip(steps[:-1], steps[1:])):
         found = conv_back(edges, after(coef, *sent), *inputs, first, last, found)
-        sent = flight.step(found[4], *names)
+        if number < 2:
+            sent = flight.step(found[4], "b", "a")
     d_hidden, d_low, d_high, g_w_depth, g_b_in = found
+
     d_state, d_low, d_high, g_in_slots = input_back(
-        after(d_hidden, *sent), d_low, d_high, x_rows, x_low, x_high, w_slots
+        d_hidden, d_low, d_high, x_rows, x_low, x_high, w_slots
     )
     from_high = lax.ppermute(d_low.reshape(high_rows, beside, slots), "sp", backward)
     from_low = lax.ppermute(d_high.reshape(high_rows, beside, slots), "sp", forward)
-    d_state = to_groups(
-        d_state.reshape(high_rows, row_pixels, slots), from_high, from_low, groups
-    )
-    d_state = lax.all_to_all(d_state, "lev", split_axis=0, concat_axis=0, tiled=True)
-    grad_ocean_state = from_channel_rows(d_state, half, dates, cols, group_ch)
 
     def pack(arrays):
         packed = jnp.concatenate(arrays, axis=0)
@@ -935,12 +926,30 @@
         return found
 
     last_sums = [g_out_slots, g_in_slots, g_w_depth, g_b_in]
-    flight.begin("small", pack(last_sums), orders[0], BF16, most=3)
-    flight.finish(g_b_in, "small", "a", "b", "c")
+    sent = [flight.begin("small", pack(last_sums), orders[3], BF16, most=3)]
+    sent += flight.step(g_in_slots, "b", "a")
+    d_state = to_groups(
+        after(d_state, *sent).reshape(high_rows, row_pixels, slots), from_high, from_low, groups
+    )
+    received = lax.all_to_all(d_state, "lev", split_axis=0, concat_axis=0, tiled=True)
+    sent = flight.step(d_state, "small", "b")
+    next_state = from_channel_rows(after(next_state, *sent), 0, dates, cols, group_ch)
+    sent = flight.step(next_state, "small")
+    sent = flight.step(sent[0], "b", "a")
+    token = after(sent[0], sent[1])
+    sent += flight.step(token, "small")
+    grad_ocean_state = from_channel_rows(after(received, *sent), half, dates, cols, group_ch)
+    sent = flight.step(grad_ocean_state, "small")
+    sent = flight.step(sent[0], "b", "a")
+    token = after(sent[0], sent[1])
+    sent = flight.step(token, "small")
+    flight.finish(sent[0], "b", "a")
+    weights = unpack_grads(core_side, flight.done["a"], width, ff, spans["a"][0])
+    sent = flight.step(weights[0], "small")
+    weights = (after(weights[0], *sent), weights[1])
+    weights = unpack_grads(core_side, flight.done["b"], width, ff, spans["b"][0], weights)
+    flight.finish(weights[0], "small")
     g_out_slots, g_in_slots, g_w_depth, g_b_in = unpack(in_order(*flight.done["small"]), last_sums)
-    weights = ()
-    for name, start in zip("acb", (cuts[0], cuts[2], cuts[1])):
-        weights = unpack_grads(core_side, flight.done[name], width, ff, start, weights)
     grad_w_one, grad_w_two = weights
     grad_w_out = jnp.einsum("sd,sc->dc", g_out_slots.astype(F32), table, precision=exact_mode)
     count = -(-ff // width)

time: 420 us -> 396 us (0.943)
  other arithmetic: 54.6 us -> 37.5 us
  Pallas kernels: 185 us -> 171 us
  waiting for transfers between devices: 81.5 us -> 87.9 us
  local copies, waits for them, and re-layouts: 11.7 us -> 16.7 us
    ppermute x44 -> x36, waiting for transfers between devices: 62.9 us -> 77.6 us  [hop(): lax.ppermute(value, axis, [(i, i ^ bit) for i in range(lax.axis_size(axis...]
    concatenate x9 -> x7, other arithmetic: 11.5 us -> 2.42 us  [exchange(): value = jnp.concatenate([value, came], axis=0)]
    pallas_call x3 -> x2, Pallas kernels: 54.5 us -> 46.2 us  [mlp(): pl.pallas_call(body, grid=(pl.cdiv(last - first, block),), in_specs=[pl.B...]
    convert_element_type x10 -> x8, other arithmetic: 20.4 us -> 15.9 us  [exchange(): sent = total([pair[1] for pair in pairs]).astype(link)]
    pallas_call x3 -> x2, Pallas kernels: 18.4 us -> 15.5 us  [unpack_grads(): pl.pallas_call(body, grid_spec=pltpu.PrefetchScalarGridSpec(num_scalar_pr...]
    ppermute x44 -> x36, starting transfers between devices: 41.2 us -> 40 us  [hop(): lax.ppermute(value, axis, [(i, i ^ bit) for i in range(lax.axis_size(axis...]
  transfers between devices with their start and end apart: 52 -> 44, of which waited for: 17 -> 14; matrix products, arithmetic and copies ran while one was open for 15% -> 12% of each run, Pallas kernels for 28% -> 36%
where the time goes in v3:
time: 396 us; the launch traced here: 394 us
  Pallas kernels  171 us (43%)
  waiting for transfers between devices  87.9 us (22%)
  starting transfers between devices  68.4 us (17%)
  other arithmetic  37.5 us (9%)
  local copies, waits for them, and re-layouts  16.7 us (4%)
  matrix products  10.8 us (3%)
    ppermute x36, waiting for transfers between devices, hop(): lax.ppermute(value, axis, [(i, i ^ bit) for i in range(lax.axis_size(axis...  77.6 us
    pallas_call x2, Pallas kernels, mlp(): pl.pallas_call(body, grid=(pl.cdiv(last - first, block),), in_specs=[pl.B...  46.2 us
    ppermute x36, starting transfers between devices, hop(): lax.ppermute(value, axis, [(i, i ^ bit) for i in range(lax.axis_size(axis...  40 us
    pallas_call x3, Pallas kernels, conv_back(): pl.pallas_call(body, grid=(last - first,), in_specs=[pl.BlockSpec(memory_...  35.8 us
    pallas_call x1, Pallas kernels, hidden_conv(): pl.pallas_call(functools.partial(hidden_conv_body, rows, cols, half), gri...  22.6 us
    convert_element_type x8, other arithmetic, exchange(): sent = total([pair[1] for pair in pairs]).astype(link)  15.9 us
    pallas_call x1, Pallas kernels, branch_out(): pl.pallas_call(branch_out_body, grid=(pixels // row_block,), in_specs=[pl...  15.5 us
    pallas_call x2, Pallas kernels, unpack_grads(): pl.pallas_call(body, grid_spec=pltpu.PrefetchScalarGridSpec(num_scalar_pr...  15.5 us
  transfers between devices with their start and end apart: 44, of which 14 were waited for; matrix products, arithmetic and copies ran while one was open for 12% of the time, Pallas kernels for 36%

profile of v3, /device:TPU:0, one launch (start us, length us, event | category | flops | bytes accessed | tf_op | source)
XLA Modules:
  0.0 393.9 jit_solution(5517822051276247138)
XLA Ops:
  4.0 4.2 %all-to-all-start = ((bf16[4,14,56,128]{3,2,1,0:T(8,128)(2,1)}), bf16[4,14,56,128]{3,2,1,0:T(8,128)(2,1)S(1)}, u32[]{:S(2)}, u32[]{:S(2)}) async-start(bf16[4,14,56,128]{3,2,1,0:T(8,128)(2,1)} %get-tuple-element.94), calls=%async_computation | async-start | bytes 1605632 | tf_op jit(solution)/shard_map/all_to_all | solution.py:811
  9.8 10.3 %all-to-all-done.in_ref = bf16[4,14,56,128]{3,2,1,0:T(8,128)(2,1)S(1)} async-done(((bf16[4,14,56,128]{3,2,1,0:T(8,128)(2,1)}), bf16[4,14,56,128]{3,2,1,0:T(8,128)(2,1)S(1)}, u32[]{:S(2)}, u32[]{:S(2)}) %all-to-all-start) | async-done | bytes 802848 | tf_op jit(solution)/shard_map/all_to_all | solution.py:811
  24.4 4.1 %collective-permute-start = (bf16[14,24,224]{2,1,0:T(8,128)(2,1)S(1)}, bf16[14,24,224]{2,1,0:T(8,128)(2,1)S(1)}, u32[]{:S(2)}, u32[]{:S(2)}) collective-permute-start(bf16[14,24,224]{2,1,0:T(8,128)(2,1)S(1)} %get-tuple-element.199), channel_id=1, source_target_pairs={{0,1},{1,2},{2,3},{3,4},{4,5},{5,6},{6,7},{8,9},{9,10},{10,11},{11... | collective-permute-start | bytes 451592 | tf_op jit(solution)/shard_map/ppermute | solution.py:816
  37.6 22.6 %hidden_conv.1 = (f32[8,16,8,800]{3,2,1,0:T(8,128)}, bf16[2464,800]{1,0:T(8,128)(2,1)}, f32[8,16,8,800]{3,2,1,0:T(8,128)}, f32[2,800]{1,0:T(2,128)}) custom-call(s32[4]{0:T(128)} %add_convert_fusion.16.edge_ref, bf16[1792,224]{1,0:T(8,128)(2,1)} %bitcast.61, bf16[336,224]{1,0:T(8,128)(2,1)} %bitcast.70, bf16[336,224]{1,0:T(8,128)(2,1)} %bitcast.72, ...), custom_call_target="tpu_custom_call" | custom-call | flops 49999998976 | bytes 50000000 | tf_op jit(solution)/shard_map/hidden_conv/pallas_call | solution.py:358
  63.3 4.5 %convert_reduce_fusion = (f32[800]{0:T(1024)S(1)}, bf16[1024,800]{1,0:T(8,128)(2,1)}, f32[1024,800]{1,0:T(8,128)}) fusion(f32[1024]{0:T(1024)S(1)} %broadcast_in_dim.20, bf16[1024,224]{1,0:T(8,128)(2,1)} %bitcast.58, bf16[224,800]{0,1:T(8,128)(2,1)S(1)} %copy-done.7), kind=kOutput, calls=%fused_computation | convolution fusion | flops 370277600 | bytes 5739648 | tf_op jit(solution)/shard_map/dot_general | solution.py:828
  87.0 3.8 add_convert_fusion.normed_ref
  90.8 24.4 %mlp.2 = (bf16[1024,3200]{1,0:T(8,128)(2,1)}, bf16[1024,3200]{1,0:T(8,128)(2,1)}, bf16[800,1664]{1,0:T(8,128)(2,1)}, bf16[800,1664]{1,0:T(8,128)(2,1)}, f32[1,3200]{1,0:T(1,128)}) custom-call(s32[1]{0:T(128)} %bitcast.core_ref, bf16[1024,800]{1,0:T(8,128)(2,1)} %add_convert_fusion.normed_ref, bf16[1024,800]{1,0:T(8,128)(2,1)} %get-tuple-element.195.branch_ref, ...), custom_call_target="tpu_custom_call" | custom-call | flops 49999998976 | bytes 50000000 | tf_op jit(solution)/shard_map/mlp/pallas_call | solution.py:443
  115.2 21.9 %mlp.3 = (bf16[1024,3200]{1,0:T(8,128)(2,1)}, bf16[1024,3200]{1,0:T(8,128)(2,1)}, bf16[800,1536]{1,0:T(8,128)(2,1)}, bf16[800,1536]{1,0:T(8,128)(2,1)}, f32[1,3200]{1,0:T(1,128)}) custom-call(s32[1]{0:T(128)} %bitcast.core_ref, bf16[1024,800]{1,0:T(8,128)(2,1)} %add_convert_fusion.normed_ref, ...), custom_call_target="tpu_custom_call", output_to_operand_aliasing={{0}: (6, {}), {1}: (7, {}), {4}: (8, {})} | custom-call | flops 49999998976 | bytes 50000000 | tf_op jit(solution)/shard_map/mlp/pallas_call | solution.py:443
  143.5 13.2 %norm_back.1 = (f32[1024,800]{1,0:T(8,128)}, f32[2,800]{1,0:T(2,128)}) custom-call(bf16[1024,3200]{1,0:T(8,128)(2,1)} %get-tuple-element.112.dup_ref, bf16[800,3200]{1,0:T(8,128)(2,1)} %w_ref.1, f32[1024,800]{1,0:T(8,128)} %bitcast.50, f32[2,800]{1,0:T(2,128)} %pad_maximum_fusion.21.norm_ref), custom_call_target="tpu_custom_call" | custom-call | flops 49999998976 | bytes 50000000 | tf_op jit(solution)/shard_map/norm_back/pallas_call | solution.py:492
  161.2 15.5 %branch_out.1 = (bf16[4,8,56,128]{3,2,1,0:T(8,128)(2,1)}, f32[224,800]{1,0:T(8,128)}) custom-call(bf16[1024,3200]{1,0:T(8,128)(2,1)} %get-tuple-element.115.act_ref, bf16[800,3200]{1,0:T(8,128)(2,1)} %bitcast.67, f32[1,800]{1,0:T(1,128)} %reshape.166.b_ref, f32[1024,800]{1,0:T(8,128)} %bitcast.81, f32[1024,1]{1,0:T(8,128)} %broadcast_in_dim.22.wet_ref, ...), custom_call_target="tpu_custom_call" | custom-call | flops 49999998976 | bytes 50000000 | tf_op jit(solution)/shard_map/branch_out/pallas_call | solution.py:540
  184.4 6.4 %collective-permute-done.12 = f32[8,800]{1,0:T(8,128)S(1)} collective-permute-done((f32[8,800]{1,0:T(8,128)S(1)}, f32[8,800]{1,0:T(8,128)S(1)}, u32[]{:S(2)}, u32[]{:S(2)}) %collective-permute-start.12) | collective-permute-done | bytes 25632 | tf_op jit(solution)/shard_map/ppermute | solution.py:51
  198.5 4.1 %all-to-all-start.2 = ((bf16[4,8,56,128]{3,2,1,0:T(8,128)(2,1)}), bf16[4,8,56,128]{3,2,1,0:T(8,128)(2,1)}, u32[]{:S(2)}, u32[]{:S(2)}) async-start(bf16[4,8,56,128]{3,2,1,0:T(8,128)(2,1)} %get-tuple-element.120), calls=%async_computation.2 | async-start | bytes 917504 | tf_op jit(solution)/shard_map/all_to_all | solution.py:885
  208.4 10.5 %conv_back.3 = (bf16[1792,800]{1,0:T(8,128)(2,1)}, bf16[336,800]{1,0:T(8,128)(2,1)}, bf16[336,800]{1,0:T(8,128)(2,1)}, f32[49,800]{1,0:T(8,128)}, f32[1,800]{1,0:T(1,128)}) custom-call(s32[4]{0:T(128)} %add_convert_fusion.16.edge_ref, f32[3,800]{1,0:T(4,128)} %pad_maximum_fusion.20.coef_ref, f32[8,16,8,800]{3,2,1,0:T(8,128)} %bitcast.78, ...), custom_call_target="tpu_custom_call" | custom-call | flops 49999998976 | bytes 50000000 | tf_op jit(solution)/shard_map/conv_back/pallas_call | solution.py:639
  219.8 4.2 %collective-permute-done.16 = bf16[25,8,1536]{2,1,0:T(8,128)(2,1)} collective-permute-done((bf16[25,8,1536]{2,1,0:T(8,128)(2,1)}, bf16[25,8,1536]{2,1,0:T(8,128)(2,1)}, u32[]{:S(2)}, u32[]{:S(2)}) %collective-permute-start.16) | collective-permute-done | bytes 614432 | tf_op jit(solution)/shard_map/ppermute | solution.py:51
  226.9 10.5 %conv_back.4 = (bf16[1792,800]{1,0:T(8,128)(2,1)}, bf16[336,800]{1,0:T(8,128)(2,1)}, bf16[336,800]{1,0:T(8,128)(2,1)}, f32[49,800]{1,0:T(8,128)}, f32[1,800]{1,0:T(1,128)}) custom-call(s32[4]{0:T(128)} %add_convert_fusion.16.edge_ref, ...), custom_call_target="tpu_custom_call", output_to_operand_aliasing={{0}: (7, {}), {1}: (8, {}), {2}: (9, {}), {3}: (10, {}), {4... | custom-call | flops 49999998976 | bytes 50000000 | tf_op jit(solution)/shard_map/conv_back/pallas_call | solution.py:639
  244.3 14.7 %conv_back.5 = (bf16[1792,800]{1,0:T(8,128)(2,1)}, bf16[336,800]{1,0:T(8,128)(2,1)}, bf16[336,800]{1,0:T(8,128)(2,1)}, f32[49,800]{1,0:T(8,128)}, f32[1,800]{1,0:T(1,128)}) custom-call(s32[4]{0:T(128)} %add_convert_fusion.16.edge_ref, ...), custom_call_target="tpu_custom_call", output_to_operand_aliasing={{0}: (7, {}), {1}: (8, {}), {2}: (9, {}), {3}: (10, {}), {4... | custom-call | flops 49999998976 | bytes 50000000 | tf_op jit(solution)/shard_map/conv_back/pallas_call | solution.py:639
  259.1 6.9 %input_back.1 = (f32[1792,224]{1,0:T(8,128)}, bf16[336,224]{1,0:T(8,128)(2,1)}, bf16[336,224]{1,0:T(8,128)(2,1)}, f32[224,800]{1,0:T(8,128)}) custom-call(bf16[1792,800]{1,0:T(8,128)(2,1)} %get-tuple-element.142.dh_ref, bf16[336,800]{1,0:T(8,128)(2,1)} %get-tuple-element.143.dl_ref, bf16[336,800]{1,0:T(8,128)(2,1)} %get-tuple-element.144.dr_ref, ...), custom_call_target="tpu_custom_call" | custom-call | flops 49999998976 | bytes 50000000 | tf_op jit(solution)/shard_map/input_back/pallas_call | solution.py:701
  267.3 5.2 %collective-permute-start.24 = (bf16[14,24,224]{2,1,0:T(8,128)(2,1)}, bf16[14,24,224]{2,1,0:T(8,128)(2,1)}, u32[]{:S(2)}, u32[]{:S(2)}) collective-permute-start(bf16[14,24,224]{2,1,0:T(8,128)(2,1)} %bitcast.74), channel_id=1, source_target_pairs={{0,1},{1,2},{2,3},{3,4},{4,5},{5,6},{6,7},{8,9},{9,10},{10,11},{11... | collective-permute-start | bytes 451592 | tf_op jit(solution)/shard_map/ppermute | solution.py:911
  293.9 4.5 %all-to-all-start.3 = ((bf16[4,14,56,128]{3,2,1,0:T(8,128)(2,1)}), bf16[4,14,56,128]{3,2,1,0:T(8,128)(2,1)}, u32[]{:S(2)}, u32[]{:S(2)}) async-start(bf16[4,14,56,128]{3,2,1,0:T(8,128)(2,1)} %to_groups.1), calls=%async_computation.3 | async-start | bytes 1605632 | tf_op jit(solution)/shard_map/all_to_all | solution.py:934
  303.0 20.1 %collective-permute-done.26 = bf16[25,8,1536]{2,1,0:T(8,128)(2,1)S(1)} collective-permute-done((bf16[25,8,1536]{2,1,0:T(8,128)(2,1)}, bf16[25,8,1536]{2,1,0:T(8,128)(2,1)S(1)}, u32[]{:S(2)}, u32[]{:S(2)}) %collective-permute-start.26) | collective-permute-done | bytes 614432 | tf_op jit(solution)/shard_map/ppermute | solution.py:51
  330.3 29.5 %collective-permute-done.31 = bf16[8,8,800]{2,1,0:T(8,128)(2,1)S(1)} collective-permute-done((bf16[8,8,800]{2,1,0:T(8,128)(2,1)S(1)}, bf16[8,8,800]{2,1,0:T(8,128)(2,1)S(1)}, u32[]{:S(2)}, u32[]{:S(2)}) %collective-permute-start.31) | collective-permute-done | bytes 102432 | tf_op jit(solution)/shard_map/ppermute | solution.py:51
  364.5 6.1 %collective-permute-done.38.other_ref = bf16[100,8,1536]{2,1,0:T(8,128)(2,1)} collective-permute-done((bf16[100,8,1536]{2,1,0:T(8,128)(2,1)S(1)}, bf16[100,8,1536]{2,1,0:T(8,128)(2,1)}, u32[]{:S(2)}, u32[]{:S(2)}) %collective-permute-start.38) | collective-permute-done | bytes 2457632 | tf_op jit(solution)/shard_map/ppermute | solution.py:51
  370.5 7.9 %unpack_grads.2 = (f32[800,3200]{1,0:T(8,128)}, f32[800,3200]{1,0:T(8,128)}) custom-call(s32[2]{0:T(128)} %get-tuple-element.211.own_ref, bf16[100,8,1664]{2,1,0:T(8,128)(2,1)} %pad_maximum_fusion.value_ref, bf16[100,8,1664]{2,1,0:T(8,128)(2,1)} %collective-permute-done.35.other_ref), custom_call_target="tpu_custom_call" | custom-call | flops 49999998976 | bytes 50000000 | tf_op jit(solution)/shard_map/unpack_grads/pallas_call | solution.py:202
  380.1 7.6 %unpack_grads.3 = (f32[800,3200]{1,0:T(8,128)}, f32[800,3200]{1,0:T(8,128)}) custom-call(s32[2]{0:T(128)} %get-tuple-element.212.own_ref, bf16[100,8,1536]{2,1,0:T(8,128)(2,1)} %copy-done.3, bf16[100,8,1536]{2,1,0:T(8,128)(2,1)} %collective-permute-done.38.other_ref, ...), custom_call_target="tpu_custom_call", output_to_operand_aliasing={{0}: (3, {}), {1}: (4, {})} | custom-call | flops 49999998976 | bytes 50000000 | tf_op jit(solution)/shard_map/unpack_grads/pallas_call | solution.py:202
  (257 shorter events, 129.9 us)
Async XLA Ops:
  4.0 16.0 %all-to-all-start = ((bf16[4,14,56,128]{3,2,1,0:T(8,128)(2,1)}), bf16[4,14,56,128]{3,2,1,0:T(8,128)(2,1)S(1)}, u32[]{:S(2)}, u32[]{:S(2)}) async-start(bf16[4,14,56,128]{3,2,1,0:T(8,128)(2,1)} %get-tuple-element.94), calls=%async_computation | async-start | bytes 1605632 | tf_op jit(solution)/shard_map/all_to_all | solution.py:811
  24.4 12.5 %collective-permute-start = (bf16[14,24,224]{2,1,0:T(8,128)(2,1)S(1)}, bf16[14,24,224]{2,1,0:T(8,128)(2,1)S(1)}, u32[]{:S(2)}, u32[]{:S(2)}) collective-permute-start(bf16[14,24,224]{2,1,0:T(8,128)(2,1)S(1)} %get-tuple-element.199), channel_id=1, source_target_pairs={{0,1},{1,2},{2,3},{3,4},{4,5},{5,6},{6,7},{8,9},{9,10},{10,11},{11... | collective-permute-start | bytes 451592 | tf_op jit(solution)/shard_map/ppermute | solution.py:816
  33.2 27.2 %all-to-all-start.1 = ((bf16[4,8,56,128]{3,2,1,0:T(8,128)(2,1)}), bf16[4,8,56,128]{3,2,1,0:T(8,128)(2,1)S(1)}, u32[]{:S(2)}, u32[]{:S(2)}) async-start(bf16[4,8,56,128]{3,2,1,0:T(8,128)(2,1)} %get-tuple-element.98), calls=%async_computation.1 | async-start | bytes 917504 | tf_op jit(solution)/shard_map/all_to_all | solution.py:812
  115.2 23.9 %collective-permute-start.8 = (bf16[100,8,1664]{2,1,0:T(8,128)(2,1)}, bf16[100,8,1664]{2,1,0:T(8,128)(2,1)}, u32[]{:S(2)}, u32[]{:S(2)}) collective-permute-start(bf16[100,8,1664]{2,1,0:T(8,128)(2,1)} %bitcast.68), channel_id=1, source_target_pairs={{0,8},{8,0},{16,24},{24,16},{1,9},{9,1},{17,25},{25,17},{2,10},{10... | collective-permute-start | bytes 7987208 | tf_op jit(solution)/shard_map/ppermute | solution.py:51
  138.0 19.6 %collective-permute-start.7 = (bf16[100,8,1536]{2,1,0:T(8,128)(2,1)}, bf16[100,8,1536]{2,1,0:T(8,128)(2,1)}, u32[]{:S(2)}, u32[]{:S(2)}) collective-permute-start(bf16[100,8,1536]{2,1,0:T(8,128)(2,1)} %bitcast.69), channel_id=1, source_target_pairs={{0,8},{8,0},{16,24},{24,16},{1,9},{9,1},{17,25},{25,17},{2,10},{10... | collective-permute-start | bytes 7372808 | tf_op jit(solution)/shard_map/ppermute | solution.py:51
  141.8 34.8 %collective-permute-start.9 = (bf16[50,8,1664]{2,1,0:T(8,128)(2,1)}, bf16[50,8,1664]{2,1,0:T(8,128)(2,1)}, u32[]{:S(2)}, u32[]{:S(2)}) collective-permute-start(bf16[50,8,1664]{2,1,0:T(8,128)(2,1)} %add_convert_fusion.1), channel_id=1, source_target_pairs={{0,16},{8,24},{16,0},{24,8},{1,17},{9,25},{17,1},{25,9},{2,18},{10... | collective-permute-start | bytes 3993608 | tf_op jit(solution)/shard_map/ppermute | solution.py:51
  157.5 21.6 %collective-permute-start.10 = (f32[8,800]{1,0:T(8,128)S(1)}, f32[8,800]{1,0:T(8,128)S(1)}, u32[]{:S(2)}, u32[]{:S(2)}) collective-permute-start(f32[8,800]{1,0:T(8,128)S(1)} %pad_maximum_fusion.19), channel_id=1, source_target_pairs={{0,8},{8,0},{16,24},{24,16},{1,9},{9,1},{17,25},{25,17},{2,10},{10... | collective-permute-start | bytes 76808 | tf_op jit(solution)/shard_map/ppermute | solution.py:51
  160.6 42.7 %collective-permute-start.15 = (bf16[50,8,1536]{2,1,0:T(8,128)(2,1)}, bf16[50,8,1536]{2,1,0:T(8,128)(2,1)}, u32[]{:S(2)}, u32[]{:S(2)}) collective-permute-start(bf16[50,8,1536]{2,1,0:T(8,128)(2,1)} %add_convert_fusion.2), channel_id=1, source_target_pairs={{0,1},{1,0},{2,3},{3,2},{4,5},{5,4},{6,7},{7,6},{8,9},{9,8},{10,11... | collective-permute-start | bytes 3686408 | tf_op jit(solution)/shard_map/ppermute | solution.py:51
  192.8 26.2 %collective-permute-start.18 = (bf16[25,8,1664]{2,1,0:T(8,128)(2,1)}, bf16[25,8,1664]{2,1,0:T(8,128)(2,1)S(1)}, u32[]{:S(2)}, u32[]{:S(2)}) collective-permute-start(bf16[25,8,1664]{2,1,0:T(8,128)(2,1)} %add_convert_fusion.3), channel_id=1, source_target_pairs={{0,1},{1,0},{2,3},{3,2},{4,5},{5,4},{6,7},{7,6},{8,9},{9,8},{10,11... | collective-permute-start | bytes 1996808 | tf_op jit(solution)/shard_map/ppermute | solution.py:51
  198.5 89.5 %all-to-all-start.2 = ((bf16[4,8,56,128]{3,2,1,0:T(8,128)(2,1)}), bf16[4,8,56,128]{3,2,1,0:T(8,128)(2,1)}, u32[]{:S(2)}, u32[]{:S(2)}) async-start(bf16[4,8,56,128]{3,2,1,0:T(8,128)(2,1)} %get-tuple-element.120), calls=%async_computation.2 | async-start | bytes 917504 | tf_op jit(solution)/shard_map/all_to_all | solution.py:885
  205.9 18.1 %collective-permute-start.16 = (bf16[25,8,1536]{2,1,0:T(8,128)(2,1)}, bf16[25,8,1536]{2,1,0:T(8,128)(2,1)}, u32[]{:S(2)}, u32[]{:S(2)}) collective-permute-start(bf16[25,8,1536]{2,1,0:T(8,128)(2,1)} %add_convert_fusion.4), channel_id=1, source_target_pairs={{0,16},{8,24},{16,0},{24,8},{1,17},{9,25},{17,1},{25,9},{2,18},{10... | collective-permute-start | bytes 1843208 | tf_op jit(solution)/shard_map/ppermute | solution.py:51
  219.2 21.2 %collective-permute-start.19 = (bf16[25,8,896]{2,1,0:T(8,128)(2,1)S(1)}, bf16[25,8,896]{2,1,0:T(8,128)(2,1)}, u32[]{:S(2)}, u32[]{:S(2)}) collective-permute-start(bf16[25,8,896]{2,1,0:T(8,128)(2,1)S(1)} %add_convert_fusion.7), channel_id=1, source_target_pairs={{0,2},{1,3},{2,0},{3,1},{4,6},{5,7},{6,4},{7,5},{8,10},{9,11},{10,... | collective-permute-start | bytes 1075208 | tf_op jit(solution)/shard_map/ppermute | solution.py:51
  240.0 34.8 %collective-permute-start.21 = (bf16[25,8,768]{2,1,0:T(8,128)(2,1)S(1)}, bf16[25,8,768]{2,1,0:T(8,128)(2,1)}, u32[]{:S(2)}, u32[]{:S(2)}) collective-permute-start(bf16[25,8,768]{2,1,0:T(8,128)(2,1)S(1)} %add_convert_fusion.9), channel_id=1, source_target_pairs={{0,4},{1,5},{2,6},{3,7},{4,0},{5,1},{6,2},{7,3},{8,12},{9,13},{10,... | collective-permute-start | bytes 921608 | tf_op jit(solution)/shard_map/ppermute | solution.py:51
  241.6 35.1 %collective-permute-start.22 = (bf16[25,8,896]{2,1,0:T(8,128)(2,1)S(1)}, bf16[25,8,896]{2,1,0:T(8,128)(2,1)}, u32[]{:S(2)}, u32[]{:S(2)}) collective-permute-start(bf16[25,8,896]{2,1,0:T(8,128)(2,1)S(1)} %add_convert_fusion.6), channel_id=1, source_target_pairs={{0,4},{1,5},{2,6},{3,7},{4,0},{5,1},{6,2},{7,3},{8,12},{9,13},{10,... | collective-permute-start | bytes 1075208 | tf_op jit(solution)/shard_map/ppermute | solution.py:51
  266.0 13.2 %collective-permute-start.23 = (bf16[14,24,224]{2,1,0:T(8,128)(2,1)}, bf16[14,24,224]{2,1,0:T(8,128)(2,1)S(1)}, u32[]{:S(2)}, u32[]{:S(2)}) collective-permute-start(bf16[14,24,224]{2,1,0:T(8,128)(2,1)} %bitcast.75), channel_id=1, source_target_pairs={{1,0},{2,1},{3,2},{4,3},{5,4},{6,5},{7,6},{9,8},{10,9},{11,10},{12... | collective-permute-start | bytes 451592 | tf_op jit(solution)/shard_map/ppermute | solution.py:910
  277.8 22.3 %collective-permute-start.28 = (bf16[25,8,896]{2,1,0:T(8,128)(2,1)S(1)}, bf16[25,8,896]{2,1,0:T(8,128)(2,1)S(1)}, u32[]{:S(2)}, u32[]{:S(2)}) collective-permute-start(bf16[25,8,896]{2,1,0:T(8,128)(2,1)S(1)} %add_convert_fusion.5), channel_id=1, source_target_pairs={{0,2},{1,3},{2,0},{3,1},{4,6},{5,7},{6,4},{7,5},{8,10},{9,11},{10,... | collective-permute-start | bytes 1075208 | tf_op jit(solution)/shard_map/ppermute | solution.py:51
  293.9 30.0 %all-to-all-start.3 = ((bf16[4,14,56,128]{3,2,1,0:T(8,128)(2,1)}), bf16[4,14,56,128]{3,2,1,0:T(8,128)(2,1)}, u32[]{:S(2)}, u32[]{:S(2)}) async-start(bf16[4,14,56,128]{3,2,1,0:T(8,128)(2,1)} %to_groups.1), calls=%async_computation.3 | async-start | bytes 1605632 | tf_op jit(solution)/shard_map/all_to_all | solution.py:934
  298.4 24.7 %collective-permute-start.26 = (bf16[25,8,1536]{2,1,0:T(8,128)(2,1)}, bf16[25,8,1536]{2,1,0:T(8,128)(2,1)S(1)}, u32[]{:S(2)}, u32[]{:S(2)}) collective-permute-start(bf16[25,8,1536]{2,1,0:T(8,128)(2,1)} %pad_maximum_fusion.6), channel_id=1, source_target_pairs={{0,16},{8,24},{16,0},{24,8},{1,17},{9,25},{17,1},{25,9},{2,18},{10... | collective-permute-start | bytes 1843208 | tf_op jit(solution)/shard_map/ppermute | solution.py:51
  301.2 25.3 %collective-permute-start.30 = (bf16[8,8,800]{2,1,0:T(8,128)(2,1)S(1)}, bf16[8,8,800]{2,1,0:T(8,128)(2,1)S(1)}, u32[]{:S(2)}, u32[]{:S(2)}) collective-permute-start(bf16[8,8,800]{2,1,0:T(8,128)(2,1)S(1)} %add_convert_fusion.14), channel_id=1, source_target_pairs={{0,4},{1,5},{2,6},{3,7},{4,0},{5,1},{6,2},{7,3},{8,12},{9,13},{10,... | collective-permute-start | bytes 307208 | tf_op jit(solution)/shard_map/ppermute | solution.py:51
  301.7 24.8 %collective-permute-start.33 = (bf16[25,8,1664]{2,1,0:T(8,128)(2,1)S(1)}, bf16[25,8,1664]{2,1,0:T(8,128)(2,1)S(1)}, u32[]{:S(2)}, u32[]{:S(2)}) collective-permute-start(bf16[25,8,1664]{2,1,0:T(8,128)(2,1)S(1)} %pad_maximum_fusion.5), channel_id=1, source_target_pairs={{0,1},{1,0},{2,3},{3,2},{4,5},{5,4},{6,7},{7,6},{8,9},{9,8},{10,11... | collective-permute-start | bytes 1996808 | tf_op jit(solution)/shard_map/ppermute | solution.py:51
  326.7 33.3 %collective-permute-start.34 = (bf16[50,8,1664]{2,1,0:T(8,128)(2,1)S(1)}, bf16[50,8,1664]{2,1,0:T(8,128)(2,1)S(1)}, u32[]{:S(2)}, u32[]{:S(2)}) collective-permute-start(bf16[50,8,1664]{2,1,0:T(8,128)(2,1)S(1)} %pad_maximum_fusion.2), channel_id=1, source_target_pairs={{0,16},{8,24},{16,0},{24,8},{1,17},{9,25},{17,1},{25,9},{2,18},{10... | collective-permute-start | bytes 3993608 | tf_op jit(solution)/shard_map/ppermute | solution.py:51
  327.1 32.8 %collective-permute-start.37 = (bf16[50,8,1536]{2,1,0:T(8,128)(2,1)S(1)}, bf16[50,8,1536]{2,1,0:T(8,128)(2,1)S(1)}, u32[]{:S(2)}, u32[]{:S(2)}) collective-permute-start(bf16[50,8,1536]{2,1,0:T(8,128)(2,1)S(1)} %pad_maximum_fusion.3), channel_id=1, source_target_pairs={{0,1},{1,0},{2,3},{3,2},{4,5},{5,4},{6,7},{7,6},{8,9},{9,8},{10,11... | collective-permute-start | bytes 3686408 | tf_op jit(solution)/shard_map/ppermute | solution.py:51
  328.7 31.2 %collective-permute-start.31 = (bf16[8,8,800]{2,1,0:T(8,128)(2,1)S(1)}, bf16[8,8,800]{2,1,0:T(8,128)(2,1)S(1)}, u32[]{:S(2)}, u32[]{:S(2)}) collective-permute-start(bf16[8,8,800]{2,1,0:T(8,128)(2,1)S(1)} %add_convert_fusion.13), channel_id=1, source_target_pairs={{0,16},{8,24},{16,0},{24,8},{1,17},{9,25},{17,1},{25,9},{2,18},{10... | collective-permute-start | bytes 307208 | tf_op jit(solution)/shard_map/ppermute | solution.py:51
  363.2 15.2 %collective-permute-start.32 = (bf16[8,8,800]{2,1,0:T(8,128)(2,1)S(1)}, bf16[8,8,800]{2,1,0:T(8,128)(2,1)S(1)}, u32[]{:S(2)}, u32[]{:S(2)}) collective-permute-start(bf16[8,8,800]{2,1,0:T(8,128)(2,1)S(1)} %add_convert_fusion.12), channel_id=1, source_target_pairs={{0,2},{1,3},{2,0},{3,1},{4,6},{5,7},{6,4},{7,5},{8,10},{9,11},{10,... | collective-permute-start | bytes 307208 | tf_op jit(solution)/shard_map/ppermute | solution.py:51
  (61 other events, 659.6 us)

commit v4 on v3

--- a/solution.py
+++ b/solution.py
@@ -92,9 +92,7 @@
     terms = [value]
     rest = stages
     if partner is not None:
-        came = hop(partner, stages[0])
-        token = yield partner
-        terms.append(after(came, token))
+        terms.append((yield partner, hop(partner, stages[0])))
         rest = stages[1:]
     row_halvings = 0
     for stage in rest:
@@ -118,14 +116,10 @@
             sent = total([pair[1] for pair in pairs]).astype(link)
             terms = [pair[0] for pair in pairs]
             kept.append((stage, axis))
-        came = hop(sent, stage)
-        token = yield sent
-        terms.append(after(came, token))
+        terms.append((yield sent, hop(sent, stage)))
     value = total(terms).astype(link)
     for stage, axis in reversed(kept):
-        came = hop(value, stage)
-        token = yield value
-        came = after(came, token)
+        came = yield value, hop(value, stage)
         if axis == 0:
             value = jnp.concatenate([value, came], axis=0)
         else:
@@ -135,9 +129,7 @@
             value = jnp.concatenate([low, high], axis=2)[:, :, :lanes]
     other = None
     if partner is not None:
-        came = hop(value, stages[0])
-        token = yield value
-        other = after(came, token)
+        other = yield value, hop(value, stages[0])
     yield value, other, own, 1 << row_halvings
 
 
@@ -152,22 +144,30 @@
 class Exchanges:
     def __init__(self):
         self.running = {}
+        self.came = {}
         self.done = {}
+
+    def hold(self, name, got):
+        if len(got) == 2:
+            self.came[name] = got[1]
+            return [got[0]]
+        self.done[name] = got
+        del self.running[name]
+        return []
 
     def begin(self, name, *args, **options):
         self.running[name] = exchange(*args, **options)
-        return next(self.running[name])
-
-    def step(self, token, *names):
+        return self.hold(name, next(self.running[name]))[0]
+
+    def step(self, token, *names, joint=False):
+        names = [name for name in names if name in self.running]
+        if joint:
+            came = lax.optimization_barrier(tuple(self.came[name] for name in names) + (token,))
+        else:
+            came = [after(self.came[name], token) for name in names]
         sent = []
-        for name in names:
-            if name in self.running:
-                got = self.running[name].send(token)
-                if isinstance(got, tuple):
-                    self.done[name] = got
-                    del self.running[name]
-                else:
-                    sent.append(got)
+        for name, value in zip(names, came):
+            sent += self.hold(name, self.running[name].send(value))
         return sent
 
     def finish(self, token, *names):
@@ -790,7 +790,7 @@
         core + lev_rest + sp_stages,
         core + sp_stages[:1] + lev_rest + sp_stages[1:],
         core + sp_stages[1:2] + lev_rest + sp_stages[:1] + sp_stages[2:],
-        core + sp_stages + lev_rest,
+        core + sp_stages[1:] + sp_stages[:1] + lev_rest,
     )
     forward = [(i, i + 1) for i in range(strips - 1)]
     backward = [(i + 1, i) for i in range(strips - 1)]
@@ -896,7 +896,7 @@
     shape4 = (rows, cols, dates, width)
     inputs = (d_normed.reshape(shape4), conv_out, d_sum.reshape(shape4), lowered, depth, tile)
     tiles = pl.cdiv(width, LANES)
-    steps = [0, 2, 4, tiles]
+    steps = [0, tiles - 4, tiles - 2, tiles]
     found = ()
     for number, (first, last) in enumerate(zip(steps[:-1], steps[1:])):
         found = conv_back(edges, after(coef, *sent), *inputs, first, last, found)
@@ -931,21 +931,28 @@
     d_state = to_groups(
         after(d_state, *sent).reshape(high_rows, row_pixels, slots), from_high, from_low, groups
     )
-    received = lax.all_to_all(d_state, "lev", split_axis=0, concat_axis=0, tiled=True)
-    sent = flight.step(d_state, "small", "b")
+    sent = flight.step(d_state, "small")
+    sent = flight.step(sent[0], "b", "a", joint=True)
     next_state = from_channel_rows(after(next_state, *sent), 0, dates, cols, group_ch)
     sent = flight.step(next_state, "small")
-    sent = flight.step(sent[0], "b", "a")
+    sent = flight.step(sent[0], "b", "a", joint=True)
     token = after(sent[0], sent[1])
-    sent += flight.step(token, "small")
+    received = lax.all_to_all(
+        after(d_state, token), "lev", split_axis=0, concat_axis=0, tiled=True
+    )
+    sent = flight.step(token, "small")
+    sent = flight.step(sent[0], "a", "b", joint=True)
+    token = after(sent[0], sent[1])
+    sent = flight.step(token, "small")
+    sent = flight.step(sent[0], "small")
+    flight.finish(sent[0], "a")
+    ready = flight.done["a"]
+    ready = (after(ready[0], *sent),) + ready[1:]
+    weights = unpack_grads(core_side, ready, width, ff, spans["a"][0])
+    sent = flight.step(weights[0], "small")
     grad_ocean_state = from_channel_rows(after(received, *sent), half, dates, cols, group_ch)
     sent = flight.step(grad_ocean_state, "small")
-    sent = flight.step(sent[0], "b", "a")
-    token = after(sent[0], sent[1])
-    sent = flight.step(token, "small")
-    flight.finish(sent[0], "b", "a")
-    weights = unpack_grads(core_side, flight.done["a"], width, ff, spans["a"][0])
-    sent = flight.step(weights[0], "small")
+    flight.finish(sent[0], "b")
     weights = (after(weights[0], *sent), weights[1])
     weights = unpack_grads(core_side, flight.done["b"], width, ff, spans["b"][0], weights)
     flight.finish(weights[0], "small")

time: 396 us -> 392 us (0.990)
  other arithmetic: 37.5 us -> 46.3 us
  waiting for transfers between devices: 87.9 us -> 80.8 us
  starting transfers between devices: 68.4 us -> 64 us
    concatenate x7, other arithmetic: 2.42 us -> 11.4 us  [exchange(): value = jnp.concatenate([value, came], axis=0)]
    ppermute x36, waiting for transfers between devices: 77.6 us -> 70.1 us  [hop(): lax.ppermute(value, axis, [(i, i ^ bit) for i in range(lax.axis_size(axis...]
    ppermute x36, starting transfers between devices: 40 us -> 35.6 us  [hop(): lax.ppermute(value, axis, [(i, i ^ bit) for i in range(lax.axis_size(axis...]
  transfers between devices with their start and end apart: 44 -> 44, of which waited for: 14 -> 16; matrix products, arithmetic and copies ran while one was open for 12% -> 14% of each run, Pallas kernels for 36% -> 36%
where the time goes in v4:
time: 392 us; the launch traced here: 390 us
  Pallas kernels  171 us (44%)
  waiting for transfers between devices  80.8 us (21%)
  starting transfers between devices  64 us (16%)
  other arithmetic  46.3 us (12%)
  local copies, waits for them, and re-layouts  15.9 us (4%)
  matrix products  10.9 us (3%)
    ppermute x36, waiting for transfers between devices, hop(): lax.ppermute(value, axis, [(i, i ^ bit) for i in range(lax.axis_size(axis...  70.1 us
    pallas_call x2, Pallas kernels, mlp(): pl.pallas_call(body, grid=(pl.cdiv(last - first, block),), in_specs=[pl.B...  46.2 us
    pallas_call x3, Pallas kernels, conv_back(): pl.pallas_call(body, grid=(last - first,), in_specs=[pl.BlockSpec(memory_...  35.8 us
    ppermute x36, starting transfers between devices, hop(): lax.ppermute(value, axis, [(i, i ^ bit) for i in range(lax.axis_size(axis...  35.6 us
    pallas_call x1, Pallas kernels, hidden_conv(): pl.pallas_call(functools.partial(hidden_conv_body, rows, cols, half), gri...  22.6 us
    convert_element_type x8, other arithmetic, exchange(): sent = total([pair[1] for pair in pairs]).astype(link)  15.9 us
    pallas_call x1, Pallas kernels, branch_out(): pl.pallas_call(branch_out_body, grid=(pixels // row_block,), in_specs=[pl...  15.5 us
    pallas_call x2, Pallas kernels, unpack_grads(): pl.pallas_call(body, grid_spec=pltpu.PrefetchScalarGridSpec(num_scalar_pr...  15.4 us
  transfers between devices with their start and end apart: 44, of which 16 were waited for; matrix products, arithmetic and copies ran while one was open for 14% of the time, Pallas kernels for 36%

profile of v4, /device:TPU:0, one launch (start us, length us, event | category | flops | bytes accessed | tf_op | source)
XLA Modules:
  0.0 390.3 jit_solution(8986994920557073546)
XLA Ops:
  4.0 4.2 %all-to-all-start = ((bf16[4,14,56,128]{3,2,1,0:T(8,128)(2,1)}), bf16[4,14,56,128]{3,2,1,0:T(8,128)(2,1)S(1)}, u32[]{:S(2)}, u32[]{:S(2)}) async-start(bf16[4,14,56,128]{3,2,1,0:T(8,128)(2,1)} %get-tuple-element.98), calls=%async_computation | async-start | bytes 1605632 | tf_op jit(solution)/shard_map/all_to_all | solution.py:811
  9.8 10.2 %all-to-all-done.in_ref = bf16[4,14,56,128]{3,2,1,0:T(8,128)(2,1)S(1)} async-done(((bf16[4,14,56,128]{3,2,1,0:T(8,128)(2,1)}), bf16[4,14,56,128]{3,2,1,0:T(8,128)(2,1)S(1)}, u32[]{:S(2)}, u32[]{:S(2)}) %all-to-all-start) | async-done | bytes 802848 | tf_op jit(solution)/shard_map/all_to_all | solution.py:811
  24.4 4.1 %collective-permute-start = (bf16[14,24,224]{2,1,0:T(8,128)(2,1)S(1)}, bf16[14,24,224]{2,1,0:T(8,128)(2,1)S(1)}, u32[]{:S(2)}, u32[]{:S(2)}) collective-permute-start(bf16[14,24,224]{2,1,0:T(8,128)(2,1)S(1)} %get-tuple-element.207), channel_id=1, source_target_pairs={{0,1},{1,2},{2,3},{3,4},{4,5},{5,6},{6,7},{8,9},{9,10},{10,11},{11... | collective-permute-start | bytes 451592 | tf_op jit(solution)/shard_map/ppermute | solution.py:816
  37.6 22.6 %hidden_conv.1 = (f32[8,16,8,800]{3,2,1,0:T(8,128)}, bf16[2464,800]{1,0:T(8,128)(2,1)}, f32[8,16,8,800]{3,2,1,0:T(8,128)}, f32[2,800]{1,0:T(2,128)}) custom-call(s32[4]{0:T(128)} %add_convert_fusion.16.edge_ref, bf16[1792,224]{1,0:T(8,128)(2,1)} %bitcast.61, bf16[336,224]{1,0:T(8,128)(2,1)} %bitcast.70, bf16[336,224]{1,0:T(8,128)(2,1)} %bitcast.72, ...), custom_call_target="tpu_custom_call" | custom-call | flops 49999998976 | bytes 50000000 | tf_op jit(solution)/shard_map/hidden_conv/pallas_call | solution.py:358
  63.2 4.5 %convert_reduce_fusion = (f32[800]{0:T(1024)S(1)}, bf16[1024,800]{1,0:T(8,128)(2,1)}, f32[1024,800]{1,0:T(8,128)}) fusion(f32[1024]{0:T(1024)S(1)} %broadcast_in_dim.20, bf16[1024,224]{1,0:T(8,128)(2,1)} %bitcast.58, bf16[224,800]{0,1:T(8,128)(2,1)S(1)} %copy-done.5), kind=kOutput, calls=%fused_computation | convolution fusion | flops 370277600 | bytes 5739648 | tf_op jit(solution)/shard_map/dot_general | solution.py:828
  90.8 24.4 %mlp.2 = (bf16[1024,3200]{1,0:T(8,128)(2,1)}, bf16[1024,3200]{1,0:T(8,128)(2,1)}, bf16[800,1664]{1,0:T(8,128)(2,1)}, bf16[800,1664]{1,0:T(8,128)(2,1)}, f32[1,3200]{1,0:T(1,128)}) custom-call(s32[1]{0:T(128)} %bitcast.core_ref, bf16[1024,800]{1,0:T(8,128)(2,1)} %add_convert_fusion.normed_ref, bf16[1024,800]{1,0:T(8,128)(2,1)} %get-tuple-element.203.branch_ref, ...), custom_call_target="tpu_custom_call" | custom-call | flops 49999998976 | bytes 50000000 | tf_op jit(solution)/shard_map/mlp/pallas_call | solution.py:443
  115.2 21.8 %mlp.3 = (bf16[1024,3200]{1,0:T(8,128)(2,1)}, bf16[1024,3200]{1,0:T(8,128)(2,1)}, bf16[800,1536]{1,0:T(8,128)(2,1)}, bf16[800,1536]{1,0:T(8,128)(2,1)}, f32[1,3200]{1,0:T(1,128)}) custom-call(s32[1]{0:T(128)} %bitcast.core_ref, bf16[1024,800]{1,0:T(8,128)(2,1)} %add_convert_fusion.normed_ref, ...), custom_call_target="tpu_custom_call", output_to_operand_aliasing={{0}: (6, {}), {1}: (7, {}), {4}: (8, {})} | custom-call | flops 49999998976 | bytes 50000000 | tf_op jit(solution)/shard_map/mlp/pallas_call | solution.py:443
  143.5 13.2 %norm_back.1 = (f32[1024,800]{1,0:T(8,128)}, f32[2,800]{1,0:T(2,128)}) custom-call(bf16[1024,3200]{1,0:T(8,128)(2,1)} %get-tuple-element.116.dup_ref, bf16[800,3200]{1,0:T(8,128)(2,1)} %w_ref.1, f32[1024,800]{1,0:T(8,128)} %bitcast.50, f32[2,800]{1,0:T(2,128)} %pad_maximum_fusion.21.norm_ref), custom_call_target="tpu_custom_call" | custom-call | flops 49999998976 | bytes 50000000 | tf_op jit(solution)/shard_map/norm_back/pallas_call | solution.py:492
  161.1 15.5 %branch_out.1 = (bf16[4,8,56,128]{3,2,1,0:T(8,128)(2,1)}, f32[224,800]{1,0:T(8,128)}) custom-call(bf16[1024,3200]{1,0:T(8,128)(2,1)} %get-tuple-element.119.act_ref, bf16[800,3200]{1,0:T(8,128)(2,1)} %bitcast.67, f32[1,800]{1,0:T(1,128)} %reshape.166.b_ref, f32[1024,800]{1,0:T(8,128)} %bitcast.81, f32[1024,1]{1,0:T(8,128)} %broadcast_in_dim.22.wet_ref, ...), custom_call_target="tpu_custom_call" | custom-call | flops 49999998976 | bytes 50000000 | tf_op jit(solution)/shard_map/branch_out/pallas_call | solution.py:540
  184.4 6.4 %collective-permute-done.13 = f32[8,800]{1,0:T(8,128)S(1)} collective-permute-done((f32[8,800]{1,0:T(8,128)S(1)}, f32[8,800]{1,0:T(8,128)S(1)}, u32[]{:S(2)}, u32[]{:S(2)}) %collective-permute-start.13) | collective-permute-done | bytes 25632 | tf_op jit(solution)/shard_map/ppermute | solution.py:51
  198.4 4.1 %all-to-all-start.2 = ((bf16[4,8,56,128]{3,2,1,0:T(8,128)(2,1)}), bf16[4,8,56,128]{3,2,1,0:T(8,128)(2,1)}, u32[]{:S(2)}, u32[]{:S(2)}) async-start(bf16[4,8,56,128]{3,2,1,0:T(8,128)(2,1)} %get-tuple-element.124), calls=%async_computation.2 | async-start | bytes 917504 | tf_op jit(solution)/shard_map/all_to_all | solution.py:885
  208.4 14.7 %conv_back.3 = (bf16[1792,800]{1,0:T(8,128)(2,1)}, bf16[336,800]{1,0:T(8,128)(2,1)}, bf16[336,800]{1,0:T(8,128)(2,1)}, f32[49,800]{1,0:T(8,128)}, f32[1,800]{1,0:T(1,128)}) custom-call(s32[4]{0:T(128)} %add_convert_fusion.16.edge_ref, f32[3,800]{1,0:T(4,128)} %pad_maximum_fusion.20.coef_ref, f32[8,16,8,800]{3,2,1,0:T(8,128)} %bitcast.78, ...), custom_call_target="tpu_custom_call" | custom-call | flops 49999998976 | bytes 50000000 | tf_op jit(solution)/shard_map/conv_back/pallas_call | solution.py:639
  227.9 10.5 %conv_back.4 = (bf16[1792,800]{1,0:T(8,128)(2,1)}, bf16[336,800]{1,0:T(8,128)(2,1)}, bf16[336,800]{1,0:T(8,128)(2,1)}, f32[49,800]{1,0:T(8,128)}, f32[1,800]{1,0:T(1,128)}) custom-call(s32[4]{0:T(128)} %add_convert_fusion.16.edge_ref, ...), custom_call_target="tpu_custom_call", output_to_operand_aliasing={{0}: (7, {}), {1}: (8, {}), {2}: (9, {}), {3}: (10, {}), {4... | custom-call | flops 49999998976 | bytes 50000000 | tf_op jit(solution)/shard_map/conv_back/pallas_call | solution.py:639
  246.9 10.6 %conv_back.5 = (bf16[1792,800]{1,0:T(8,128)(2,1)}, bf16[336,800]{1,0:T(8,128)(2,1)}, bf16[336,800]{1,0:T(8,128)(2,1)}, f32[49,800]{1,0:T(8,128)}, f32[1,800]{1,0:T(1,128)}) custom-call(s32[4]{0:T(128)} %add_convert_fusion.16.edge_ref, ...), custom_call_target="tpu_custom_call", output_to_operand_aliasing={{0}: (7, {}), {1}: (8, {}), {2}: (9, {}), {3}: (10, {}), {4... | custom-call | flops 49999998976 | bytes 50000000 | tf_op jit(solution)/shard_map/conv_back/pallas_call | solution.py:639
  257.5 6.9 %input_back.1 = (f32[1792,224]{1,0:T(8,128)}, bf16[336,224]{1,0:T(8,128)(2,1)}, bf16[336,224]{1,0:T(8,128)(2,1)}, f32[224,800]{1,0:T(8,128)}) custom-call(bf16[1792,800]{1,0:T(8,128)(2,1)} %get-tuple-element.146.dh_ref, bf16[336,800]{1,0:T(8,128)(2,1)} %get-tuple-element.147.dl_ref, bf16[336,800]{1,0:T(8,128)(2,1)} %get-tuple-element.148.dr_ref, ...), custom_call_target="tpu_custom_call" | custom-call | flops 49999998976 | bytes 50000000 | tf_op jit(solution)/shard_map/input_back/pallas_call | solution.py:701
  265.7 5.2 %collective-permute-start.26 = (bf16[14,24,224]{2,1,0:T(8,128)(2,1)}, bf16[14,24,224]{2,1,0:T(8,128)(2,1)}, u32[]{:S(2)}, u32[]{:S(2)}) collective-permute-start(bf16[14,24,224]{2,1,0:T(8,128)(2,1)} %bitcast.74), channel_id=1, source_target_pairs={{0,1},{1,2},{2,3},{3,4},{4,5},{5,6},{6,7},{8,9},{9,10},{10,11},{11... | collective-permute-start | bytes 451592 | tf_op jit(solution)/shard_map/ppermute | solution.py:911
  284.6 7.7 %collective-permute-done.23 = bf16[25,8,896]{2,1,0:T(8,128)(2,1)S(1)} collective-permute-done((bf16[25,8,896]{2,1,0:T(8,128)(2,1)S(1)}, bf16[25,8,896]{2,1,0:T(8,128)(2,1)S(1)}, u32[]{:S(2)}, u32[]{:S(2)}) %collective-permute-start.23) | collective-permute-done | bytes 358432 | tf_op jit(solution)/shard_map/ppermute | solution.py:51
  299.0 11.2 %collective-permute-done.27 = bf16[25,8,1536]{2,1,0:T(8,128)(2,1)} collective-permute-done((bf16[25,8,1536]{2,1,0:T(8,128)(2,1)}, bf16[25,8,1536]{2,1,0:T(8,128)(2,1)}, u32[]{:S(2)}, u32[]{:S(2)}) %collective-permute-start.27) | collective-permute-done | bytes 614432 | tf_op jit(solution)/shard_map/ppermute | solution.py:51
  316.6 6.7 %collective-permute-done.30 = bf16[8,8,800]{2,1,0:T(8,128)(2,1)} collective-permute-done((bf16[8,8,800]{2,1,0:T(8,128)(2,1)S(1)}, bf16[8,8,800]{2,1,0:T(8,128)(2,1)}, u32[]{:S(2)}, u32[]{:S(2)}) %collective-permute-start.30) | collective-permute-done | bytes 102432 | tf_op jit(solution)/shard_map/ppermute | solution.py:51
  324.3 18.2 %collective-permute-done.35 = bf16[50,8,1536]{2,1,0:T(8,128)(2,1)} collective-permute-done((bf16[50,8,1536]{2,1,0:T(8,128)(2,1)}, bf16[50,8,1536]{2,1,0:T(8,128)(2,1)}, u32[]{:S(2)}, u32[]{:S(2)}) %collective-permute-start.35) | collective-permute-done | bytes 1228832 | tf_op jit(solution)/shard_map/ppermute | solution.py:51
  354.2 4.5 %all-to-all-start.3 = ((bf16[4,14,56,128]{3,2,1,0:T(8,128)(2,1)}), bf16[4,14,56,128]{3,2,1,0:T(8,128)(2,1)}, u32[]{:S(2)}, u32[]{:S(2)}) async-start(bf16[4,14,56,128]{3,2,1,0:T(8,128)(2,1)} %to_groups.1), calls=%async_computation.3 | async-start | bytes 1605632 | tf_op jit(solution)/shard_map/all_to_all | solution.py:940
  360.8 7.9 %unpack_grads.2 = (f32[800,3200]{1,0:T(8,128)}, f32[800,3200]{1,0:T(8,128)}) custom-call(s32[2]{0:T(128)} %get-tuple-element.219.own_ref, bf16[100,8,1664]{2,1,0:T(8,128)(2,1)} %pad_maximum_fusion.value_ref, bf16[100,8,1664]{2,1,0:T(8,128)(2,1)} %collective-permute-done.36.other_ref), custom_call_target="tpu_custom_call" | custom-call | flops 49999998976 | bytes 50000000 | tf_op jit(solution)/shard_map/unpack_grads/pallas_call | solution.py:202
  372.8 4.0 %collective-permute-done.37 = bf16[16,8,800]{2,1,0:T(8,128)(2,1)S(1)} collective-permute-done((bf16[16,8,800]{2,1,0:T(8,128)(2,1)S(1)}, bf16[16,8,800]{2,1,0:T(8,128)(2,1)S(1)}, u32[]{:S(2)}, u32[]{:S(2)}) %collective-permute-start.37) | collective-permute-done | bytes 204832 | tf_op jit(solution)/shard_map/ppermute | solution.py:51
  377.6 7.4 %unpack_grads.3 = (f32[800,3200]{1,0:T(8,128)}, f32[800,3200]{1,0:T(8,128)}) custom-call(s32[2]{0:T(128)} %get-tuple-element.220.own_ref, bf16[100,8,1536]{2,1,0:T(8,128)(2,1)} %copy-done.3, bf16[100,8,1536]{2,1,0:T(8,128)(2,1)} %collective-permute-done.39.other_ref, ...), custom_call_target="tpu_custom_call", output_to_operand_aliasing={{0}: (3, {}), {1}: (4, {})} | custom-call | flops 49999998976 | bytes 50000000 | tf_op jit(solution)/shard_map/unpack_grads/pallas_call | solution.py:202
  (259 shorter events, 142.4 us)
Async XLA Ops:
  4.0 16.0 %all-to-all-start = ((bf16[4,14,56,128]{3,2,1,0:T(8,128)(2,1)}), bf16[4,14,56,128]{3,2,1,0:T(8,128)(2,1)S(1)}, u32[]{:S(2)}, u32[]{:S(2)}) async-start(bf16[4,14,56,128]{3,2,1,0:T(8,128)(2,1)} %get-tuple-element.98), calls=%async_computation | async-start | bytes 1605632 | tf_op jit(solution)/shard_map/all_to_all | solution.py:811
  33.2 27.2 %all-to-all-start.1 = ((bf16[4,8,56,128]{3,2,1,0:T(8,128)(2,1)}), bf16[4,8,56,128]{3,2,1,0:T(8,128)(2,1)S(1)}, u32[]{:S(2)}, u32[]{:S(2)}) async-start(bf16[4,8,56,128]{3,2,1,0:T(8,128)(2,1)} %get-tuple-element.102), calls=%async_computation.1 | async-start | bytes 917504 | tf_op jit(solution)/shard_map/all_to_all | solution.py:812
  115.2 23.8 %collective-permute-start.8 = (bf16[100,8,1664]{2,1,0:T(8,128)(2,1)}, bf16[100,8,1664]{2,1,0:T(8,128)(2,1)}, u32[]{:S(2)}, u32[]{:S(2)}) collective-permute-start(bf16[100,8,1664]{2,1,0:T(8,128)(2,1)} %bitcast.68), channel_id=1, source_target_pairs={{0,8},{8,0},{16,24},{24,16},{1,9},{9,1},{17,25},{25,17},{2,10},{10... | collective-permute-start | bytes 7987208 | tf_op jit(solution)/shard_map/ppermute | solution.py:51
  137.9 19.6 %collective-permute-start.7 = (bf16[100,8,1536]{2,1,0:T(8,128)(2,1)}, bf16[100,8,1536]{2,1,0:T(8,128)(2,1)}, u32[]{:S(2)}, u32[]{:S(2)}) collective-permute-start(bf16[100,8,1536]{2,1,0:T(8,128)(2,1)} %bitcast.69), channel_id=1, source_target_pairs={{0,8},{8,0},{16,24},{24,16},{1,9},{9,1},{17,25},{25,17},{2,10},{10... | collective-permute-start | bytes 7372808 | tf_op jit(solution)/shard_map/ppermute | solution.py:51
  141.7 34.9 %collective-permute-start.9 = (bf16[50,8,1664]{2,1,0:T(8,128)(2,1)}, bf16[50,8,1664]{2,1,0:T(8,128)(2,1)}, u32[]{:S(2)}, u32[]{:S(2)}) collective-permute-start(bf16[50,8,1664]{2,1,0:T(8,128)(2,1)} %add_convert_fusion.1), channel_id=1, source_target_pairs={{0,16},{8,24},{16,0},{24,8},{1,17},{9,25},{17,1},{25,9},{2,18},{10... | collective-permute-start | bytes 3993608 | tf_op jit(solution)/shard_map/ppermute | solution.py:51
  157.4 21.6 %collective-permute-start.11 = (f32[8,800]{1,0:T(8,128)S(1)}, f32[8,800]{1,0:T(8,128)S(1)}, u32[]{:S(2)}, u32[]{:S(2)}) collective-permute-start(f32[8,800]{1,0:T(8,128)S(1)} %pad_maximum_fusion.19), channel_id=1, source_target_pairs={{0,8},{8,0},{16,24},{24,16},{1,9},{9,1},{17,25},{25,17},{2,10},{10... | collective-permute-start | bytes 76808 | tf_op jit(solution)/shard_map/ppermute | solution.py:51
  160.5 42.8 %collective-permute-start.10 = (bf16[50,8,1536]{2,1,0:T(8,128)(2,1)}, bf16[50,8,1536]{2,1,0:T(8,128)(2,1)}, u32[]{:S(2)}, u32[]{:S(2)}) collective-permute-start(bf16[50,8,1536]{2,1,0:T(8,128)(2,1)} %add_convert_fusion.2), channel_id=1, source_target_pairs={{0,1},{1,0},{2,3},{3,2},{4,5},{5,4},{6,7},{7,6},{8,9},{9,8},{10,11... | collective-permute-start | bytes 3686408 | tf_op jit(solution)/shard_map/ppermute | solution.py:51
  192.7 30.4 %collective-permute-start.18 = (bf16[25,8,1664]{2,1,0:T(8,128)(2,1)}, bf16[25,8,1664]{2,1,0:T(8,128)(2,1)S(1)}, u32[]{:S(2)}, u32[]{:S(2)}) collective-permute-start(bf16[25,8,1664]{2,1,0:T(8,128)(2,1)} %add_convert_fusion.3), channel_id=1, source_target_pairs={{0,1},{1,0},{2,3},{3,2},{4,5},{5,4},{6,7},{7,6},{8,9},{9,8},{10,11... | collective-permute-start | bytes 1996808 | tf_op jit(solution)/shard_map/ppermute | solution.py:51
  198.4 97.2 %all-to-all-start.2 = ((bf16[4,8,56,128]{3,2,1,0:T(8,128)(2,1)}), bf16[4,8,56,128]{3,2,1,0:T(8,128)(2,1)}, u32[]{:S(2)}, u32[]{:S(2)}) async-start(bf16[4,8,56,128]{3,2,1,0:T(8,128)(2,1)} %get-tuple-element.124), calls=%async_computation.2 | async-start | bytes 917504 | tf_op jit(solution)/shard_map/all_to_all | solution.py:885
  205.8 18.1 %collective-permute-start.16 = (bf16[25,8,1536]{2,1,0:T(8,128)(2,1)}, bf16[25,8,1536]{2,1,0:T(8,128)(2,1)}, u32[]{:S(2)}, u32[]{:S(2)}) collective-permute-start(bf16[25,8,1536]{2,1,0:T(8,128)(2,1)} %add_convert_fusion.4), channel_id=1, source_target_pairs={{0,16},{8,24},{16,0},{24,8},{1,17},{9,25},{17,1},{25,9},{2,18},{10... | collective-permute-start | bytes 1843208 | tf_op jit(solution)/shard_map/ppermute | solution.py:51
  223.3 19.7 %collective-permute-start.20 = (bf16[25,8,896]{2,1,0:T(8,128)(2,1)S(1)}, bf16[25,8,896]{2,1,0:T(8,128)(2,1)}, u32[]{:S(2)}, u32[]{:S(2)}) collective-permute-start(bf16[25,8,896]{2,1,0:T(8,128)(2,1)S(1)} %add_convert_fusion.7), channel_id=1, source_target_pairs={{0,2},{1,3},{2,0},{3,1},{4,6},{5,7},{6,4},{7,5},{8,10},{9,11},{10,... | collective-permute-start | bytes 1075208 | tf_op jit(solution)/shard_map/ppermute | solution.py:51
  226.3 13.8 %collective-permute-start.17 = (bf16[25,8,768]{2,1,0:T(8,128)(2,1)}, bf16[25,8,768]{2,1,0:T(8,128)(2,1)S(1)}, u32[]{:S(2)}, u32[]{:S(2)}) collective-permute-start(bf16[25,8,768]{2,1,0:T(8,128)(2,1)} %add_convert_fusion.10), channel_id=1, source_target_pairs={{0,2},{1,3},{2,0},{3,1},{4,6},{5,7},{6,4},{7,5},{8,10},{9,11},{10,... | collective-permute-start | bytes 921608 | tf_op jit(solution)/shard_map/ppermute | solution.py:51
  242.6 30.7 %collective-permute-start.19 = (bf16[25,8,768]{2,1,0:T(8,128)(2,1)S(1)}, bf16[25,8,768]{2,1,0:T(8,128)(2,1)}, u32[]{:S(2)}, u32[]{:S(2)}) collective-permute-start(bf16[25,8,768]{2,1,0:T(8,128)(2,1)S(1)} %add_convert_fusion.9), channel_id=1, source_target_pairs={{0,4},{1,5},{2,6},{3,7},{4,0},{5,1},{6,2},{7,3},{8,12},{9,13},{10,... | collective-permute-start | bytes 921608 | tf_op jit(solution)/shard_map/ppermute | solution.py:51
  244.3 30.2 %collective-permute-start.22 = (bf16[25,8,896]{2,1,0:T(8,128)(2,1)S(1)}, bf16[25,8,896]{2,1,0:T(8,128)(2,1)}, u32[]{:S(2)}, u32[]{:S(2)}) collective-permute-start(bf16[25,8,896]{2,1,0:T(8,128)(2,1)S(1)} %add_convert_fusion.6), channel_id=1, source_target_pairs={{0,4},{1,5},{2,6},{3,7},{4,0},{5,1},{6,2},{7,3},{8,12},{9,13},{10,... | collective-permute-start | bytes 1075208 | tf_op jit(solution)/shard_map/ppermute | solution.py:51
  264.4 13.2 %collective-permute-start.25 = (bf16[14,24,224]{2,1,0:T(8,128)(2,1)}, bf16[14,24,224]{2,1,0:T(8,128)(2,1)S(1)}, u32[]{:S(2)}, u32[]{:S(2)}) collective-permute-start(bf16[14,24,224]{2,1,0:T(8,128)(2,1)} %bitcast.75), channel_id=1, source_target_pairs={{1,0},{2,1},{3,2},{4,3},{5,4},{6,5},{7,6},{9,8},{10,9},{11,10},{12... | collective-permute-start | bytes 451592 | tf_op jit(solution)/shard_map/ppermute | solution.py:910
  275.5 16.7 %collective-permute-start.23 = (bf16[25,8,896]{2,1,0:T(8,128)(2,1)S(1)}, bf16[25,8,896]{2,1,0:T(8,128)(2,1)S(1)}, u32[]{:S(2)}, u32[]{:S(2)}) collective-permute-start(bf16[25,8,896]{2,1,0:T(8,128)(2,1)S(1)} %add_convert_fusion.5), channel_id=1, source_target_pairs={{0,2},{1,3},{2,0},{3,1},{4,6},{5,7},{6,4},{7,5},{8,10},{9,11},{10,... | collective-permute-start | bytes 1075208 | tf_op jit(solution)/shard_map/ppermute | solution.py:51
  282.8 15.2 %collective-permute-start.29 = (bf16[16,8,800]{2,1,0:T(8,128)(2,1)}, bf16[16,8,800]{2,1,0:T(8,128)(2,1)S(1)}, u32[]{:S(2)}, u32[]{:S(2)}) collective-permute-start(bf16[16,8,800]{2,1,0:T(8,128)(2,1)} %add_convert_fusion.11), channel_id=1, source_target_pairs={{0,2},{1,3},{2,0},{3,1},{4,6},{5,7},{6,4},{7,5},{8,10},{9,11},{10,... | collective-permute-start | bytes 614408 | tf_op jit(solution)/shard_map/ppermute | solution.py:51
  293.4 16.8 %collective-permute-start.28 = (bf16[25,8,1664]{2,1,0:T(8,128)(2,1)S(1)}, bf16[25,8,1664]{2,1,0:T(8,128)(2,1)}, u32[]{:S(2)}, u32[]{:S(2)}) collective-permute-start(bf16[25,8,1664]{2,1,0:T(8,128)(2,1)S(1)} %pad_maximum_fusion.5), channel_id=1, source_target_pairs={{0,1},{1,0},{2,3},{3,2},{4,5},{5,4},{6,7},{7,6},{8,9},{9,8},{10,11... | collective-permute-start | bytes 1996808 | tf_op jit(solution)/shard_map/ppermute | solution.py:51
  295.2 15.0 %collective-permute-start.27 = (bf16[25,8,1536]{2,1,0:T(8,128)(2,1)}, bf16[25,8,1536]{2,1,0:T(8,128)(2,1)}, u32[]{:S(2)}, u32[]{:S(2)}) collective-permute-start(bf16[25,8,1536]{2,1,0:T(8,128)(2,1)} %pad_maximum_fusion.6), channel_id=1, source_target_pairs={{0,16},{8,24},{16,0},{24,8},{1,17},{9,25},{17,1},{25,9},{2,18},{10... | collective-permute-start | bytes 1843208 | tf_op jit(solution)/shard_map/ppermute | solution.py:51
  312.5 30.0 %collective-permute-start.34 = (bf16[50,8,1664]{2,1,0:T(8,128)(2,1)}, bf16[50,8,1664]{2,1,0:T(8,128)(2,1)}, u32[]{:S(2)}, u32[]{:S(2)}) collective-permute-start(bf16[50,8,1664]{2,1,0:T(8,128)(2,1)} %pad_maximum_fusion.2), channel_id=1, source_target_pairs={{0,16},{8,24},{16,0},{24,8},{1,17},{9,25},{17,1},{25,9},{2,18},{10... | collective-permute-start | bytes 3993608 | tf_op jit(solution)/shard_map/ppermute | solution.py:51
  315.1 27.4 %collective-permute-start.35 = (bf16[50,8,1536]{2,1,0:T(8,128)(2,1)}, bf16[50,8,1536]{2,1,0:T(8,128)(2,1)}, u32[]{:S(2)}, u32[]{:S(2)}) collective-permute-start(bf16[50,8,1536]{2,1,0:T(8,128)(2,1)} %pad_maximum_fusion.3), channel_id=1, source_target_pairs={{0,1},{1,0},{2,3},{3,2},{4,5},{5,4},{6,7},{7,6},{8,9},{9,8},{10,11... | collective-permute-start | bytes 3686408 | tf_op jit(solution)/shard_map/ppermute | solution.py:51
  345.8 15.0 %collective-permute-start.36 = (bf16[100,8,1664]{2,1,0:T(8,128)(2,1)}, bf16[100,8,1664]{2,1,0:T(8,128)(2,1)}, u32[]{:S(2)}, u32[]{:S(2)}) collective-permute-start(bf16[100,8,1664]{2,1,0:T(8,128)(2,1)} %pad_maximum_fusion.value_ref), channel_id=1, source_target_pairs={{0,8},{8,0},{16,24},{24,16},{1,9},{9,1},{17,25},{25,17},{2,10},{10... | collective-permute-start | bytes 7987208 | tf_op jit(solution)/shard_map/ppermute | solution.py:51
  354.2 16.1 %all-to-all-start.3 = ((bf16[4,14,56,128]{3,2,1,0:T(8,128)(2,1)}), bf16[4,14,56,128]{3,2,1,0:T(8,128)(2,1)}, u32[]{:S(2)}, u32[]{:S(2)}) async-start(bf16[4,14,56,128]{3,2,1,0:T(8,128)(2,1)} %to_groups.1), calls=%async_computation.3 | async-start | bytes 1605632 | tf_op jit(solution)/shard_map/all_to_all | solution.py:940
  360.7 16.9 %collective-permute-start.39 = (bf16[100,8,1536]{2,1,0:T(8,128)(2,1)S(1)}, bf16[100,8,1536]{2,1,0:T(8,128)(2,1)}, u32[]{:S(2)}, u32[]{:S(2)}) collective-permute-start(bf16[100,8,1536]{2,1,0:T(8,128)(2,1)S(1)} %pad_maximum_fusion.1.value_ref), channel_id=1, source_target_pairs={{0,8},{8,0},{16,24},{24,16},{1,9},{9,1},{17,25},{25,17},{2,10},{10... | collective-permute-start | bytes 7372808 | tf_op jit(solution)/shard_map/ppermute | solution.py:51
  (62 other events, 726.3 us)

commit v5 on v4

--- a/solution.py
+++ b/solution.py
@@ -398,9 +398,11 @@
     return values * below, below + values * (gauss * 0.3989422804014327)
 
 
-def mlp_body(row_block, core_ref, normed_ref, branch_ref, w_one_ref, b_one_ref, w_two_ref, act_ref, dup_ref, keep_ref, send_ref, gb_ref, normed_t, branch_t):
+def mlp_body(row_block, core_ref, conv_ref, norm_ref, branch_ref, w_one_ref, b_one_ref, w_two_ref, act_ref, dup_ref, keep_ref, send_ref, gb_ref, normed_ref, normed_t, branch_t):
     @pl.when(pl.program_id(0) == 0)
     def _():
+        centered = (conv_ref[...] - norm_ref[0:1]) * norm_ref[1:2]
+        normed_ref[...] = (centered * norm_ref[2:3] + norm_ref[3:4]).astype(BF16)
         normed_t[...] = normed_ref[...].T
         branch_t[...] = branch_ref[...].T
 
@@ -430,13 +432,13 @@
         send_ref[...] = grad_one
 
 
-def mlp(core_side, normed, d_branch, w_one, b_one, w_two, first, last, prior=(), block=256, row_block=128):
-    pixels, width = normed.shape
+def mlp(core_side, conv_flat, norm, d_branch, w_one, b_one, w_two, first, last, prior=(), block=256, row_block=128):
+    pixels, width = conv_flat.shape
     hidden = w_one.shape[1]
     start = first // block
 
-    def body(core_ref, normed_ref, branch_ref, w_one_ref, b_one_ref, w_two_ref, *refs):
-        mlp_body(row_block, core_ref, normed_ref, branch_ref, w_one_ref, b_one_ref, w_two_ref, *refs[len(prior) :])
+    def body(core_ref, conv_ref, norm_ref, branch_ref, w_one_ref, b_one_ref, w_two_ref, *refs):
+        mlp_body(row_block, core_ref, conv_ref, norm_ref, branch_ref, w_one_ref, b_one_ref, w_two_ref, *refs[len(prior) :])
 
     whole = jax.ShapeDtypeStruct((pixels, hidden), BF16)
     grad = jax.ShapeDtypeStruct((width, last - first), BF16)
@@ -446,6 +448,7 @@
         in_specs=[
             pl.BlockSpec(memory_space=pltpu.SMEM),
             pl.BlockSpec((pixels, width), lambda i: (0, 0)),
+            pl.BlockSpec((4, width), lambda i: (0, 0)),
             pl.BlockSpec((pixels, width), lambda i: (0, 0)),
             pl.BlockSpec((width, block), lambda i: (0, start + i)),
             pl.BlockSpec((1, block), lambda i: (0, start + i)),
@@ -460,12 +463,12 @@
             pl.BlockSpec((1, block), lambda i: (0, start + i)),
         ],
         out_shape=[whole, whole, grad, grad, jax.ShapeDtypeStruct((1, hidden), F32)],
-        scratch_shapes=[pltpu.VMEM((width, pixels), BF16), pltpu.VMEM((width, pixels), BF16)],
-        input_output_aliases={6 + n: k for n, k in enumerate((0, 1, 4)[: len(prior)])},
+        scratch_shapes=[pltpu.VMEM((pixels, width), BF16)] + [pltpu.VMEM((width, pixels), BF16)] * 2,
+        input_output_aliases={7 + n: k for n, k in enumerate((0, 1, 4)[: len(prior)])},
 
         cost_estimate=COST,
         name="mlp",
-    )(core_side.reshape(1).astype(jnp.int32), normed, d_branch, w_one, b_one.reshape(1, -1), w_two, *prior)
+    )(core_side.reshape(1).astype(jnp.int32), conv_flat, norm, d_branch, w_one, b_one.reshape(1, -1), w_two, *prior)
     activated, d_up, keep, send, bias = results
     blocks = (width // SUBLANES, SUBLANES, last - first)
     return (activated, d_up, bias), (keep.reshape(blocks), send.reshape(blocks))
@@ -496,7 +499,7 @@
             pl.BlockSpec((row_block, hidden), lambda i: (i, 0)),
             pl.BlockSpec((width, hidden), lambda i: (0, 0)),
             pl.BlockSpec((row_block, width), lambda i: (i, 0)),
-            pl.BlockSpec((2, width), lambda i: (0, 0)),
+            pl.BlockSpec((4, width), lambda i: (0, 0)),
         ],
         out_specs=[
             pl.BlockSpec((row_block, width), lambda i: (i, 0)),
@@ -835,8 +838,7 @@
     mean_value = sums[0] / pixel_total
     inv_scale = lax.rsqrt(sums[1] / pixel_total - mean_value * mean_value + 1e-05)
     conv_flat = conv_out.reshape(pixels, width)
-    centered = (conv_flat - mean_value) * inv_scale
-    normed = (centered * norm_gain + norm_bias).astype(BF16)
+    norm = jnp.stack([mean_value, inv_scale, norm_gain, norm_bias])
     ff = w_one.shape[1]
     block = 256
     cut = ff // 2 // block * block
@@ -853,7 +855,7 @@
 
     def part(name, order, prior=()):
         found, grads = mlp(
-            core_side, normed, d_branch, w_one, b_one, w_two_t, *spans[name], prior
+            core_side, conv_flat, norm, d_branch, w_one, b_one, w_two_t, *spans[name], prior
         )
         return found, flight.begin(name, grads[0], order, BF16, partner=grads[1])
 
@@ -862,7 +864,6 @@
     activated, d_up, g_b_one = found
     sent = [sent] + flight.step(g_b_one, "a")
 
-    norm = jnp.stack([mean_value, inv_scale])
     d_normed, parts = norm_back(after(d_up, *sent), w_one, conv_flat, norm)
     sent = flight.step(parts, "b")
     parts = jnp.concatenate(

time: 392 us -> 390 us (level)
  transfers between devices with their start and end apart: 44 -> 44, of which waited for: 16 -> 16; matrix products, arithmetic and copies ran while one was open for 14% -> 13% of each run, Pallas kernels for 36% -> 37%
where the time goes in v5:
time: 390 us; the launch traced here: 388 us
  Pallas kernels  173 us (44%)
  waiting for transfers between devices  80.9 us (21%)
  starting transfers between devices  63.9 us (16%)
  other arithmetic  42.4 us (11%)
  local copies, waits for them, and re-layouts  15.9 us (4%)
  matrix products  10.8 us (3%)
    ppermute x36, waiting for transfers between devices, hop(): lax.ppermute(value, axis, [(i, i ^ bit) for i in range(lax.axis_size(axis...  70.2 us
    pallas_call x2, Pallas kernels, mlp(): pl.pallas_call(body, grid=(pl.cdiv(last - first, block),), in_specs=[pl.B...  48.1 us
    pallas_call x3, Pallas kernels, conv_back(): pl.pallas_call(body, grid=(last - first,), in_specs=[pl.BlockSpec(memory_...  35.7 us
    ppermute x36, starting transfers between devices, hop(): lax.ppermute(value, axis, [(i, i ^ bit) for i in range(lax.axis_size(axis...  35.5 us
    pallas_call x1, Pallas kernels, hidden_conv(): pl.pallas_call(functools.partial(hidden_conv_body, rows, cols, half), gri...  22.7 us
    convert_element_type x8, other arithmetic, exchange(): sent = total([pair[1] for pair in pairs]).astype(link)  15.9 us
    pallas_call x1, Pallas kernels, branch_out(): pl.pallas_call(branch_out_body, grid=(pixels // row_block,), in_specs=[pl...  15.5 us
    pallas_call x2, Pallas kernels, unpack_grads(): pl.pallas_call(body, grid_spec=pltpu.PrefetchScalarGridSpec(num_scalar_pr...  15.4 us
  transfers between devices with their start and end apart: 44, of which 16 were waited for; matrix products, arithmetic and copies ran while one was open for 13% of the time, Pallas kernels for 37%

profile of v5, /device:TPU:0, one launch (start us, length us, event | category | flops | bytes accessed | tf_op | source)
XLA Modules:
  0.0 388.3 jit_solution(8766185861622773144)
XLA Ops:
  4.0 4.2 %all-to-all-start = ((bf16[4,14,56,128]{3,2,1,0:T(8,128)(2,1)}), bf16[4,14,56,128]{3,2,1,0:T(8,128)(2,1)S(1)}, u32[]{:S(2)}, u32[]{:S(2)}) async-start(bf16[4,14,56,128]{3,2,1,0:T(8,128)(2,1)} %get-tuple-element.98), calls=%async_computation | async-start | bytes 1605632 | tf_op jit(solution)/shard_map/all_to_all | solution.py:814
  9.8 10.2 %all-to-all-done.in_ref = bf16[4,14,56,128]{3,2,1,0:T(8,128)(2,1)S(1)} async-done(((bf16[4,14,56,128]{3,2,1,0:T(8,128)(2,1)}), bf16[4,14,56,128]{3,2,1,0:T(8,128)(2,1)S(1)}, u32[]{:S(2)}, u32[]{:S(2)}) %all-to-all-start) | async-done | bytes 802848 | tf_op jit(solution)/shard_map/all_to_all | solution.py:814
  24.4 4.1 %collective-permute-start = (bf16[14,24,224]{2,1,0:T(8,128)(2,1)S(1)}, bf16[14,24,224]{2,1,0:T(8,128)(2,1)S(1)}, u32[]{:S(2)}, u32[]{:S(2)}) collective-permute-start(bf16[14,24,224]{2,1,0:T(8,128)(2,1)S(1)} %get-tuple-element.205), channel_id=1, source_target_pairs={{0,1},{1,2},{2,3},{3,4},{4,5},{5,6},{6,7},{8,9},{9,10},{10,11},{11... | collective-permute-start | bytes 451592 | tf_op jit(solution)/shard_map/ppermute | solution.py:819
  37.5 22.7 %hidden_conv.1 = (f32[8,16,8,800]{3,2,1,0:T(8,128)}, bf16[2464,800]{1,0:T(8,128)(2,1)}, f32[8,16,8,800]{3,2,1,0:T(8,128)}, f32[2,800]{1,0:T(2,128)}) custom-call(s32[4]{0:T(128)} %add_convert_fusion.15.edge_ref, bf16[1792,224]{1,0:T(8,128)(2,1)} %bitcast.59, bf16[336,224]{1,0:T(8,128)(2,1)} %bitcast.68, bf16[336,224]{1,0:T(8,128)(2,1)} %bitcast.70, ...), custom_call_target="tpu_custom_call" | custom-call | flops 49999998976 | bytes 50000000 | tf_op jit(solution)/shard_map/hidden_conv/pallas_call | solution.py:358
  63.3 4.5 %convert_reduce_fusion = (f32[800]{0:T(1024)S(1)}, bf16[1024,800]{1,0:T(8,128)(2,1)}, f32[1024,800]{1,0:T(8,128)}) fusion(f32[1024]{0:T(1024)S(1)} %broadcast_in_dim.16, bf16[1024,224]{1,0:T(8,128)(2,1)} %bitcast.56, bf16[224,800]{0,1:T(8,128)(2,1)S(1)} %copy-done.5), kind=kOutput, calls=%fused_computation | convolution fusion | flops 370277600 | bytes 5739648 | tf_op jit(solution)/shard_map/dot_general | solution.py:831
  87.6 25.3 %mlp.2 = (bf16[1024,3200]{1,0:T(8,128)(2,1)}, bf16[1024,3200]{1,0:T(8,128)(2,1)}, bf16[800,1664]{1,0:T(8,128)(2,1)}, bf16[800,1664]{1,0:T(8,128)(2,1)}, f32[1,3200]{1,0:T(1,128)}) custom-call(s32[1]{0:T(128)} %bitcast.core_ref, f32[1024,800]{1,0:T(8,128)} %bitcast.76, f32[4,800]{1,0:T(4,128)} %pad_maximum_fusion.20.norm_ref, ...), custom_call_target="tpu_custom_call" | custom-call | flops 49999998976 | bytes 50000000 | tf_op jit(solution)/shard_map/mlp/pallas_call | solution.py:445
  112.9 22.8 %mlp.3 = (bf16[1024,3200]{1,0:T(8,128)(2,1)}, bf16[1024,3200]{1,0:T(8,128)(2,1)}, bf16[800,1536]{1,0:T(8,128)(2,1)}, bf16[800,1536]{1,0:T(8,128)(2,1)}, f32[1,3200]{1,0:T(1,128)}) custom-call(s32[1]{0:T(128)} %bitcast.core_ref, f32[1024,800]{1,0:T(8,128)} %bitcast.77, ...), custom_call_target="tpu_custom_call", output_to_operand_aliasing={{0}: (7, {}), {1}: (8, {}), {4}: (9, {})} | custom-call | flops 49999998976 | bytes 50000000 | tf_op jit(solution)/shard_map/mlp/pallas_call | solution.py:445
  141.5 13.2 %norm_back.1 = (f32[1024,800]{1,0:T(8,128)}, f32[2,800]{1,0:T(2,128)}) custom-call(bf16[1024,3200]{1,0:T(8,128)(2,1)} %get-tuple-element.116.dup_ref, bf16[800,3200]{1,0:T(8,128)(2,1)} %w_ref.1, f32[1024,800]{1,0:T(8,128)} %bitcast.78, f32[4,800]{1,0:T(4,128)} %pad_maximum_fusion.20.norm_ref), custom_call_target="tpu_custom_call" | custom-call | flops 49999998976 | bytes 50000000 | tf_op jit(solution)/shard_map/norm_back/pallas_call | solution.py:495
  159.1 15.5 %branch_out.1 = (bf16[4,8,56,128]{3,2,1,0:T(8,128)(2,1)}, f32[224,800]{1,0:T(8,128)}) custom-call(bf16[1024,3200]{1,0:T(8,128)(2,1)} %get-tuple-element.119.act_ref, bf16[800,3200]{1,0:T(8,128)(2,1)} %bitcast.65, f32[1,800]{1,0:T(1,128)} %reshape.164.b_ref, f32[1024,800]{1,0:T(8,128)} %bitcast.82, f32[1024,1]{1,0:T(8,128)} %broadcast_in_dim.18.wet_ref, ...), custom_call_target="tpu_custom_call" | custom-call | flops 49999998976 | bytes 50000000 | tf_op jit(solution)/shard_map/branch_out/pallas_call | solution.py:543
  182.4 6.4 %collective-permute-done.13 = f32[8,800]{1,0:T(8,128)S(1)} collective-permute-done((f32[8,800]{1,0:T(8,128)S(1)}, f32[8,800]{1,0:T(8,128)S(1)}, u32[]{:S(2)}, u32[]{:S(2)}) %collective-permute-start.13) | collective-permute-done | bytes 25632 | tf_op jit(solution)/shard_map/ppermute | solution.py:51
  196.5 4.1 %all-to-all-start.2 = ((bf16[4,8,56,128]{3,2,1,0:T(8,128)(2,1)}), bf16[4,8,56,128]{3,2,1,0:T(8,128)(2,1)}, u32[]{:S(2)}, u32[]{:S(2)}) async-start(bf16[4,8,56,128]{3,2,1,0:T(8,128)(2,1)} %get-tuple-element.124), calls=%async_computation.2 | async-start | bytes 917504 | tf_op jit(solution)/shard_map/all_to_all | solution.py:886
  206.4 14.7 %conv_back.3 = (bf16[1792,800]{1,0:T(8,128)(2,1)}, bf16[336,800]{1,0:T(8,128)(2,1)}, bf16[336,800]{1,0:T(8,128)(2,1)}, f32[49,800]{1,0:T(8,128)}, f32[1,800]{1,0:T(1,128)}) custom-call(s32[4]{0:T(128)} %add_convert_fusion.15.edge_ref, f32[3,800]{1,0:T(4,128)} %pad_maximum_fusion.21.coef_ref, f32[8,16,8,800]{3,2,1,0:T(8,128)} %bitcast.79, ...), custom_call_target="tpu_custom_call" | custom-call | flops 49999998976 | bytes 50000000 | tf_op jit(solution)/shard_map/conv_back/pallas_call | solution.py:642
  225.9 10.5 %conv_back.4 = (bf16[1792,800]{1,0:T(8,128)(2,1)}, bf16[336,800]{1,0:T(8,128)(2,1)}, bf16[336,800]{1,0:T(8,128)(2,1)}, f32[49,800]{1,0:T(8,128)}, f32[1,800]{1,0:T(1,128)}) custom-call(s32[4]{0:T(128)} %add_convert_fusion.15.edge_ref, ...), custom_call_target="tpu_custom_call", output_to_operand_aliasing={{0}: (7, {}), {1}: (8, {}), {2}: (9, {}), {3}: (10, {}), {4... | custom-call | flops 49999998976 | bytes 50000000 | tf_op jit(solution)/shard_map/conv_back/pallas_call | solution.py:642
  245.0 10.5 %conv_back.5 = (bf16[1792,800]{1,0:T(8,128)(2,1)}, bf16[336,800]{1,0:T(8,128)(2,1)}, bf16[336,800]{1,0:T(8,128)(2,1)}, f32[49,800]{1,0:T(8,128)}, f32[1,800]{1,0:T(1,128)}) custom-call(s32[4]{0:T(128)} %add_convert_fusion.15.edge_ref, ...), custom_call_target="tpu_custom_call", output_to_operand_aliasing={{0}: (7, {}), {1}: (8, {}), {2}: (9, {}), {3}: (10, {}), {4... | custom-call | flops 49999998976 | bytes 50000000 | tf_op jit(solution)/shard_map/conv_back/pallas_call | solution.py:642
  255.5 6.9 %input_back.1 = (f32[1792,224]{1,0:T(8,128)}, bf16[336,224]{1,0:T(8,128)(2,1)}, bf16[336,224]{1,0:T(8,128)(2,1)}, f32[224,800]{1,0:T(8,128)}) custom-call(bf16[1792,800]{1,0:T(8,128)(2,1)} %get-tuple-element.146.dh_ref, bf16[336,800]{1,0:T(8,128)(2,1)} %get-tuple-element.147.dl_ref, bf16[336,800]{1,0:T(8,128)(2,1)} %get-tuple-element.148.dr_ref, ...), custom_call_target="tpu_custom_call" | custom-call | flops 49999998976 | bytes 50000000 | tf_op jit(solution)/shard_map/input_back/pallas_call | solution.py:704
  263.7 5.2 %collective-permute-start.26 = (bf16[14,24,224]{2,1,0:T(8,128)(2,1)}, bf16[14,24,224]{2,1,0:T(8,128)(2,1)}, u32[]{:S(2)}, u32[]{:S(2)}) collective-permute-start(bf16[14,24,224]{2,1,0:T(8,128)(2,1)} %bitcast.72), channel_id=1, source_target_pairs={{0,1},{1,2},{2,3},{3,4},{4,5},{5,6},{6,7},{8,9},{9,10},{10,11},{11... | collective-permute-start | bytes 451592 | tf_op jit(solution)/shard_map/ppermute | solution.py:912
  282.5 7.7 %collective-permute-done.23 = bf16[25,8,896]{2,1,0:T(8,128)(2,1)S(1)} collective-permute-done((bf16[25,8,896]{2,1,0:T(8,128)(2,1)S(1)}, bf16[25,8,896]{2,1,0:T(8,128)(2,1)S(1)}, u32[]{:S(2)}, u32[]{:S(2)}) %collective-permute-start.23) | collective-permute-done | bytes 358432 | tf_op jit(solution)/shard_map/ppermute | solution.py:51
  296.9 11.2 %collective-permute-done.27 = bf16[25,8,1536]{2,1,0:T(8,128)(2,1)} collective-permute-done((bf16[25,8,1536]{2,1,0:T(8,128)(2,1)}, bf16[25,8,1536]{2,1,0:T(8,128)(2,1)}, u32[]{:S(2)}, u32[]{:S(2)}) %collective-permute-start.27) | collective-permute-done | bytes 614432 | tf_op jit(solution)/shard_map/ppermute | solution.py:51
  314.6 6.6 %collective-permute-done.30 = bf16[8,8,800]{2,1,0:T(8,128)(2,1)} collective-permute-done((bf16[8,8,800]{2,1,0:T(8,128)(2,1)S(1)}, bf16[8,8,800]{2,1,0:T(8,128)(2,1)}, u32[]{:S(2)}, u32[]{:S(2)}) %collective-permute-start.30) | collective-permute-done | bytes 102432 | tf_op jit(solution)/shard_map/ppermute | solution.py:51
  322.2 18.4 %collective-permute-done.35 = bf16[50,8,1536]{2,1,0:T(8,128)(2,1)} collective-permute-done((bf16[50,8,1536]{2,1,0:T(8,128)(2,1)}, bf16[50,8,1536]{2,1,0:T(8,128)(2,1)}, u32[]{:S(2)}, u32[]{:S(2)}) %collective-permute-start.35) | collective-permute-done | bytes 1228832 | tf_op jit(solution)/shard_map/ppermute | solution.py:51
  352.1 4.5 %all-to-all-start.3 = ((bf16[4,14,56,128]{3,2,1,0:T(8,128)(2,1)}), bf16[4,14,56,128]{3,2,1,0:T(8,128)(2,1)}, u32[]{:S(2)}, u32[]{:S(2)}) async-start(bf16[4,14,56,128]{3,2,1,0:T(8,128)(2,1)} %to_groups.1), calls=%async_computation.3 | async-start | bytes 1605632 | tf_op jit(solution)/shard_map/all_to_all | solution.py:941
  358.7 7.9 %unpack_grads.2 = (f32[800,3200]{1,0:T(8,128)}, f32[800,3200]{1,0:T(8,128)}) custom-call(s32[2]{0:T(128)} %get-tuple-element.216.own_ref, bf16[100,8,1664]{2,1,0:T(8,128)(2,1)} %pad_maximum_fusion.value_ref, bf16[100,8,1664]{2,1,0:T(8,128)(2,1)} %collective-permute-done.36.other_ref), custom_call_target="tpu_custom_call" | custom-call | flops 49999998976 | bytes 50000000 | tf_op jit(solution)/shard_map/unpack_grads/pallas_call | solution.py:202
  370.7 4.0 %collective-permute-done.37 = bf16[16,8,800]{2,1,0:T(8,128)(2,1)S(1)} collective-permute-done((bf16[16,8,800]{2,1,0:T(8,128)(2,1)S(1)}, bf16[16,8,800]{2,1,0:T(8,128)(2,1)S(1)}, u32[]{:S(2)}, u32[]{:S(2)}) %collective-permute-start.37) | collective-permute-done | bytes 204832 | tf_op jit(solution)/shard_map/ppermute | solution.py:51
  375.5 7.4 %unpack_grads.3 = (f32[800,3200]{1,0:T(8,128)}, f32[800,3200]{1,0:T(8,128)}) custom-call(s32[2]{0:T(128)} %get-tuple-element.217.own_ref, bf16[100,8,1536]{2,1,0:T(8,128)(2,1)} %copy-done.3, bf16[100,8,1536]{2,1,0:T(8,128)(2,1)} %collective-permute-done.39.other_ref, ...), custom_call_target="tpu_custom_call", output_to_operand_aliasing={{0}: (3, {}), {1}: (4, {})} | custom-call | flops 49999998976 | bytes 50000000 | tf_op jit(solution)/shard_map/unpack_grads/pallas_call | solution.py:202
  (258 shorter events, 138.4 us)
Async XLA Ops:
  4.0 16.0 %all-to-all-start = ((bf16[4,14,56,128]{3,2,1,0:T(8,128)(2,1)}), bf16[4,14,56,128]{3,2,1,0:T(8,128)(2,1)S(1)}, u32[]{:S(2)}, u32[]{:S(2)}) async-start(bf16[4,14,56,128]{3,2,1,0:T(8,128)(2,1)} %get-tuple-element.98), calls=%async_computation | async-start | bytes 1605632 | tf_op jit(solution)/shard_map/all_to_all | solution.py:814
  33.1 27.3 %all-to-all-start.1 = ((bf16[4,8,56,128]{3,2,1,0:T(8,128)(2,1)}), bf16[4,8,56,128]{3,2,1,0:T(8,128)(2,1)S(1)}, u32[]{:S(2)}, u32[]{:S(2)}) async-start(bf16[4,8,56,128]{3,2,1,0:T(8,128)(2,1)} %get-tuple-element.102), calls=%async_computation.1 | async-start | bytes 917504 | tf_op jit(solution)/shard_map/all_to_all | solution.py:815
  112.9 24.2 %collective-permute-start.8 = (bf16[100,8,1664]{2,1,0:T(8,128)(2,1)}, bf16[100,8,1664]{2,1,0:T(8,128)(2,1)}, u32[]{:S(2)}, u32[]{:S(2)}) collective-permute-start(bf16[100,8,1664]{2,1,0:T(8,128)(2,1)} %bitcast.66), channel_id=1, source_target_pairs={{0,8},{8,0},{16,24},{24,16},{1,9},{9,1},{17,25},{25,17},{2,10},{10... | collective-permute-start | bytes 7987208 | tf_op jit(solution)/shard_map/ppermute | solution.py:51
  136.6 19.0 %collective-permute-start.7 = (bf16[100,8,1536]{2,1,0:T(8,128)(2,1)}, bf16[100,8,1536]{2,1,0:T(8,128)(2,1)}, u32[]{:S(2)}, u32[]{:S(2)}) collective-permute-start(bf16[100,8,1536]{2,1,0:T(8,128)(2,1)} %bitcast.67), channel_id=1, source_target_pairs={{0,8},{8,0},{16,24},{24,16},{1,9},{9,1},{17,25},{25,17},{2,10},{10... | collective-permute-start | bytes 7372808 | tf_op jit(solution)/shard_map/ppermute | solution.py:51
  139.8 34.8 %collective-permute-start.9 = (bf16[50,8,1664]{2,1,0:T(8,128)(2,1)}, bf16[50,8,1664]{2,1,0:T(8,128)(2,1)}, u32[]{:S(2)}, u32[]{:S(2)}) collective-permute-start(bf16[50,8,1664]{2,1,0:T(8,128)(2,1)} %add_convert_fusion), channel_id=1, source_target_pairs={{0,16},{8,24},{16,0},{24,8},{1,17},{9,25},{17,1},{25,9},{2,18},{10... | collective-permute-start | bytes 3993608 | tf_op jit(solution)/shard_map/ppermute | solution.py:51
  155.4 21.6 %collective-permute-start.11 = (f32[8,800]{1,0:T(8,128)S(1)}, f32[8,800]{1,0:T(8,128)S(1)}, u32[]{:S(2)}, u32[]{:S(2)}) collective-permute-start(f32[8,800]{1,0:T(8,128)S(1)} %pad_maximum_fusion.19), channel_id=1, source_target_pairs={{0,8},{8,0},{16,24},{24,16},{1,9},{9,1},{17,25},{25,17},{2,10},{10... | collective-permute-start | bytes 76808 | tf_op jit(solution)/shard_map/ppermute | solution.py:51
  158.5 42.8 %collective-permute-start.10 = (bf16[50,8,1536]{2,1,0:T(8,128)(2,1)}, bf16[50,8,1536]{2,1,0:T(8,128)(2,1)}, u32[]{:S(2)}, u32[]{:S(2)}) collective-permute-start(bf16[50,8,1536]{2,1,0:T(8,128)(2,1)} %add_convert_fusion.1), channel_id=1, source_target_pairs={{0,1},{1,0},{2,3},{3,2},{4,5},{5,4},{6,7},{7,6},{8,9},{9,8},{10,11... | collective-permute-start | bytes 3686408 | tf_op jit(solution)/shard_map/ppermute | solution.py:51
  190.7 30.4 %collective-permute-start.18 = (bf16[25,8,1664]{2,1,0:T(8,128)(2,1)}, bf16[25,8,1664]{2,1,0:T(8,128)(2,1)S(1)}, u32[]{:S(2)}, u32[]{:S(2)}) collective-permute-start(bf16[25,8,1664]{2,1,0:T(8,128)(2,1)} %add_convert_fusion.2), channel_id=1, source_target_pairs={{0,1},{1,0},{2,3},{3,2},{4,5},{5,4},{6,7},{7,6},{8,9},{9,8},{10,11... | collective-permute-start | bytes 1996808 | tf_op jit(solution)/shard_map/ppermute | solution.py:51
  196.5 97.1 %all-to-all-start.2 = ((bf16[4,8,56,128]{3,2,1,0:T(8,128)(2,1)}), bf16[4,8,56,128]{3,2,1,0:T(8,128)(2,1)}, u32[]{:S(2)}, u32[]{:S(2)}) async-start(bf16[4,8,56,128]{3,2,1,0:T(8,128)(2,1)} %get-tuple-element.124), calls=%async_computation.2 | async-start | bytes 917504 | tf_op jit(solution)/shard_map/all_to_all | solution.py:886
  203.8 18.1 %collective-permute-start.16 = (bf16[25,8,1536]{2,1,0:T(8,128)(2,1)}, bf16[25,8,1536]{2,1,0:T(8,128)(2,1)}, u32[]{:S(2)}, u32[]{:S(2)}) collective-permute-start(bf16[25,8,1536]{2,1,0:T(8,128)(2,1)} %add_convert_fusion.3), channel_id=1, source_target_pairs={{0,16},{8,24},{16,0},{24,8},{1,17},{9,25},{17,1},{25,9},{2,18},{10... | collective-permute-start | bytes 1843208 | tf_op jit(solution)/shard_map/ppermute | solution.py:51
  221.4 19.6 %collective-permute-start.20 = (bf16[25,8,896]{2,1,0:T(8,128)(2,1)S(1)}, bf16[25,8,896]{2,1,0:T(8,128)(2,1)}, u32[]{:S(2)}, u32[]{:S(2)}) collective-permute-start(bf16[25,8,896]{2,1,0:T(8,128)(2,1)S(1)} %add_convert_fusion.6), channel_id=1, source_target_pairs={{0,2},{1,3},{2,0},{3,1},{4,6},{5,7},{6,4},{7,5},{8,10},{9,11},{10,... | collective-permute-start | bytes 1075208 | tf_op jit(solution)/shard_map/ppermute | solution.py:51
  224.3 13.8 %collective-permute-start.17 = (bf16[25,8,768]{2,1,0:T(8,128)(2,1)}, bf16[25,8,768]{2,1,0:T(8,128)(2,1)S(1)}, u32[]{:S(2)}, u32[]{:S(2)}) collective-permute-start(bf16[25,8,768]{2,1,0:T(8,128)(2,1)} %add_convert_fusion.9), channel_id=1, source_target_pairs={{0,2},{1,3},{2,0},{3,1},{4,6},{5,7},{6,4},{7,5},{8,10},{9,11},{10,... | collective-permute-start | bytes 921608 | tf_op jit(solution)/shard_map/ppermute | solution.py:51
  240.7 30.6 %collective-permute-start.19 = (bf16[25,8,768]{2,1,0:T(8,128)(2,1)S(1)}, bf16[25,8,768]{2,1,0:T(8,128)(2,1)}, u32[]{:S(2)}, u32[]{:S(2)}) collective-permute-start(bf16[25,8,768]{2,1,0:T(8,128)(2,1)S(1)} %add_convert_fusion.8), channel_id=1, source_target_pairs={{0,4},{1,5},{2,6},{3,7},{4,0},{5,1},{6,2},{7,3},{8,12},{9,13},{10,... | collective-permute-start | bytes 921608 | tf_op jit(solution)/shard_map/ppermute | solution.py:51
  242.3 30.1 %collective-permute-start.22 = (bf16[25,8,896]{2,1,0:T(8,128)(2,1)S(1)}, bf16[25,8,896]{2,1,0:T(8,128)(2,1)}, u32[]{:S(2)}, u32[]{:S(2)}) collective-permute-start(bf16[25,8,896]{2,1,0:T(8,128)(2,1)S(1)} %add_convert_fusion.5), channel_id=1, source_target_pairs={{0,4},{1,5},{2,6},{3,7},{4,0},{5,1},{6,2},{7,3},{8,12},{9,13},{10,... | collective-permute-start | bytes 1075208 | tf_op jit(solution)/shard_map/ppermute | solution.py:51
  262.4 13.2 %collective-permute-start.25 = (bf16[14,24,224]{2,1,0:T(8,128)(2,1)}, bf16[14,24,224]{2,1,0:T(8,128)(2,1)S(1)}, u32[]{:S(2)}, u32[]{:S(2)}) collective-permute-start(bf16[14,24,224]{2,1,0:T(8,128)(2,1)} %bitcast.73), channel_id=1, source_target_pairs={{1,0},{2,1},{3,2},{4,3},{5,4},{6,5},{7,6},{9,8},{10,9},{11,10},{12... | collective-permute-start | bytes 451592 | tf_op jit(solution)/shard_map/ppermute | solution.py:911
  273.5 16.7 %collective-permute-start.23 = (bf16[25,8,896]{2,1,0:T(8,128)(2,1)S(1)}, bf16[25,8,896]{2,1,0:T(8,128)(2,1)S(1)}, u32[]{:S(2)}, u32[]{:S(2)}) collective-permute-start(bf16[25,8,896]{2,1,0:T(8,128)(2,1)S(1)} %add_convert_fusion.4), channel_id=1, source_target_pairs={{0,2},{1,3},{2,0},{3,1},{4,6},{5,7},{6,4},{7,5},{8,10},{9,11},{10,... | collective-permute-start | bytes 1075208 | tf_op jit(solution)/shard_map/ppermute | solution.py:51
  280.8 15.2 %collective-permute-start.29 = (bf16[16,8,800]{2,1,0:T(8,128)(2,1)}, bf16[16,8,800]{2,1,0:T(8,128)(2,1)S(1)}, u32[]{:S(2)}, u32[]{:S(2)}) collective-permute-start(bf16[16,8,800]{2,1,0:T(8,128)(2,1)} %add_convert_fusion.10), channel_id=1, source_target_pairs={{0,2},{1,3},{2,0},{3,1},{4,6},{5,7},{6,4},{7,5},{8,10},{9,11},{10,... | collective-permute-start | bytes 614408 | tf_op jit(solution)/shard_map/ppermute | solution.py:51
  291.4 16.8 %collective-permute-start.28 = (bf16[25,8,1664]{2,1,0:T(8,128)(2,1)S(1)}, bf16[25,8,1664]{2,1,0:T(8,128)(2,1)}, u32[]{:S(2)}, u32[]{:S(2)}) collective-permute-start(bf16[25,8,1664]{2,1,0:T(8,128)(2,1)S(1)} %pad_maximum_fusion.5), channel_id=1, source_target_pairs={{0,1},{1,0},{2,3},{3,2},{4,5},{5,4},{6,7},{7,6},{8,9},{9,8},{10,11... | collective-permute-start | bytes 1996808 | tf_op jit(solution)/shard_map/ppermute | solution.py:51
  293.2 15.0 %collective-permute-start.27 = (bf16[25,8,1536]{2,1,0:T(8,128)(2,1)}, bf16[25,8,1536]{2,1,0:T(8,128)(2,1)}, u32[]{:S(2)}, u32[]{:S(2)}) collective-permute-start(bf16[25,8,1536]{2,1,0:T(8,128)(2,1)} %pad_maximum_fusion.6), channel_id=1, source_target_pairs={{0,16},{8,24},{16,0},{24,8},{1,17},{9,25},{17,1},{25,9},{2,18},{10... | collective-permute-start | bytes 1843208 | tf_op jit(solution)/shard_map/ppermute | solution.py:51
  310.4 30.2 %collective-permute-start.34 = (bf16[50,8,1664]{2,1,0:T(8,128)(2,1)}, bf16[50,8,1664]{2,1,0:T(8,128)(2,1)}, u32[]{:S(2)}, u32[]{:S(2)}) collective-permute-start(bf16[50,8,1664]{2,1,0:T(8,128)(2,1)} %pad_maximum_fusion.2), channel_id=1, source_target_pairs={{0,16},{8,24},{16,0},{24,8},{1,17},{9,25},{17,1},{25,9},{2,18},{10... | collective-permute-start | bytes 3993608 | tf_op jit(solution)/shard_map/ppermute | solution.py:51
  313.0 27.6 %collective-permute-start.35 = (bf16[50,8,1536]{2,1,0:T(8,128)(2,1)}, bf16[50,8,1536]{2,1,0:T(8,128)(2,1)}, u32[]{:S(2)}, u32[]{:S(2)}) collective-permute-start(bf16[50,8,1536]{2,1,0:T(8,128)(2,1)} %pad_maximum_fusion.3), channel_id=1, source_target_pairs={{0,1},{1,0},{2,3},{3,2},{4,5},{5,4},{6,7},{7,6},{8,9},{9,8},{10,11... | collective-permute-start | bytes 3686408 | tf_op jit(solution)/shard_map/ppermute | solution.py:51
  343.9 14.8 %collective-permute-start.36 = (bf16[100,8,1664]{2,1,0:T(8,128)(2,1)}, bf16[100,8,1664]{2,1,0:T(8,128)(2,1)}, u32[]{:S(2)}, u32[]{:S(2)}) collective-permute-start(bf16[100,8,1664]{2,1,0:T(8,128)(2,1)} %pad_maximum_fusion.value_ref), channel_id=1, source_target_pairs={{0,8},{8,0},{16,24},{24,16},{1,9},{9,1},{17,25},{25,17},{2,10},{10... | collective-permute-start | bytes 7987208 | tf_op jit(solution)/shard_map/ppermute | solution.py:51
  352.1 16.1 %all-to-all-start.3 = ((bf16[4,14,56,128]{3,2,1,0:T(8,128)(2,1)}), bf16[4,14,56,128]{3,2,1,0:T(8,128)(2,1)}, u32[]{:S(2)}, u32[]{:S(2)}) async-start(bf16[4,14,56,128]{3,2,1,0:T(8,128)(2,1)} %to_groups.1), calls=%async_computation.3 | async-start | bytes 1605632 | tf_op jit(solution)/shard_map/all_to_all | solution.py:941
  358.6 16.9 %collective-permute-start.39 = (bf16[100,8,1536]{2,1,0:T(8,128)(2,1)S(1)}, bf16[100,8,1536]{2,1,0:T(8,128)(2,1)}, u32[]{:S(2)}, u32[]{:S(2)}) collective-permute-start(bf16[100,8,1536]{2,1,0:T(8,128)(2,1)S(1)} %pad_maximum_fusion.1.value_ref), channel_id=1, source_target_pairs={{0,8},{8,0},{16,24},{24,16},{1,9},{9,1},{17,25},{25,17},{2,10},{10... | collective-permute-start | bytes 7372808 | tf_op jit(solution)/shard_map/ppermute | solution.py:51
  (61 other events, 709.5 us)
